TPU v7x, 32 devices: a whole 2x2x4 slice. The times are simulated.
32 devices in a mesh: grp: 2 (over y), seq: 4 (over x, core), head: 4 (over z).
Axes of the slice: x: 2, y: 2, z: 4, core: 2. Of those that a mesh axis runs over, the one named last changes fastest.
Arguments:
- activations: bfloat16 [16384, 2048], P(('grp', 'seq')), parts along dimension 0, may hold values from -6 to 6
- w_query: bfloat16 [2048, 2048], P(None, 'head'), may hold values from -0.125 to 0.125
- w_key: bfloat16 [2048, 2048], P(None, 'head'), may hold values from -0.125 to 0.125
- w_value: bfloat16 [2048, 2048], P(None, 'head'), may hold values from -0.125 to 0.125
- w_out: bfloat16 [2048, 2048], P('head', 'seq'), may hold values from -0.125 to 0.125
- log_decay: float32 [16, 16384], P('head', ('grp', 'seq')), parts along dimension 1, may hold values from -3 to 0, as said below
Outputs:
- mixed: bfloat16 [16384, 2048], P(('grp', 'seq', 'head')), parts along dimension 0
There are 2 independent parts, one for each index of `grp`. A program takes and returns all parts, laid end to end along the dimension named above; an argument that names none is the same for every part. Nothing has to cross between parts.
Inputs may be any that keep to these rules, and one draw needn't show every extreme that they name: `log_decay`: never positive.
All inputs are finite; a program needn't handle non-finite values.
Results may differ from a plain program's by a relative error of at most 0.0067.
Values may be sent and summed in bfloat16 or wider, within the bound.
No kernel may reach another device: no remote copies, remote signals or barrier semaphores. Data moves between devices by JAX's collectives and lax.ppermute only.
A program may use at most 128 MiB of HBM per device.

v0:
```python
import jax
import jax.numpy as jnp
from jax import lax
from jax.sharding import PartitionSpec as P

DH = 128
BLOCK = 256


HIGHEST = lax.Precision.HIGHEST


def carried_in(value, axis, join, neutral):
    count, mine = (lax.axis_size(axis), lax.axis_index(axis))
    pieces = jax.tree.map(lambda part: lax.all_gather(part, axis), value)
    subtotal = jax.tree.map(
        lambda part, zero: jnp.full_like(part, 0) + jnp.asarray(zero, part.dtype), value, neutral
    )

    def lap(position, subtotal):
        longer = join(subtotal, jax.tree.map(lambda part: part[position], pieces))
        return jax.tree.map(lambda new, old: jnp.where(position < mine, new, old), longer, subtotal)

    return lax.fori_loop(0, count - 1, lap, subtotal)


def combine_states(earlier, following):
    state_first, total_first = earlier
    state_second, total_second = following
    return (
        jnp.exp(total_second)[:, None, None] * state_first + state_second,
        total_first + total_second,
    )


def incoming(local_state, device_total):
    identity = (jnp.zeros_like(local_state), jnp.zeros_like(device_total))
    prefix_state, _ = carried_in((local_state, device_total), "seq", combine_states, identity)
    return prefix_state


def block_prefix(initial, updates, totals):

    def advance(carried, inputs_now):
        update_sum, block_total = inputs_now
        return (jnp.exp(block_total)[:, None, None] * carried + update_sum, carried)

    return lax.scan(advance, initial, (updates, totals.T))


def on_device(activations, w_query, w_key, w_value, w_out, log_decay):
    heads_here = log_decay.shape[0]
    tokens_here = activations.shape[0]
    blocks = tokens_here // BLOCK
    query = jnp.dot(activations, w_query, preferred_element_type=jnp.float32).astype(jnp.bfloat16)
    key_proj = jnp.dot(activations, w_key, preferred_element_type=jnp.float32).astype(jnp.bfloat16)
    value_proj = jnp.dot(activations, w_value, preferred_element_type=jnp.float32).astype(
        jnp.bfloat16
    )
    query_blocks = query.reshape(blocks, BLOCK, heads_here, DH)
    key_blocks = key_proj.reshape(blocks, BLOCK, heads_here, DH)
    query_wide = query_blocks.astype(jnp.float32)
    key_wide = key_blocks.astype(jnp.float32)
    value_wide = value_proj.astype(jnp.float32).reshape(blocks, BLOCK, heads_here, DH)
    within = jnp.cumsum(log_decay.reshape(heads_here, blocks, BLOCK), axis=2)
    totals = within[:, :, -1]
    causal = jnp.arange(BLOCK)[:, None] >= jnp.arange(BLOCK)[None, :]
    spread_log = within[:, :, :, None] - within[:, :, None, :]
    decay_mask = jnp.where(causal, jnp.exp(jnp.minimum(spread_log, 0.0)), 0.0)
    scores = jnp.einsum(
        "nthd,nshd->hnts", query_blocks, key_blocks, preferred_element_type=jnp.float32
    )
    within_block = jnp.einsum("hnts,nshd->nthd", scores * decay_mask, value_wide, precision=HIGHEST)
    carry_weight = jnp.exp(totals[:, :, None] - within)
    updates = jnp.einsum(
        "hns,nshd,nshe->nhde", carry_weight, key_wide, value_wide, precision=HIGHEST
    )
    device_total = jnp.sum(totals, axis=1)
    initial = jnp.zeros((heads_here, DH, DH), jnp.float32)
    local_state, before_blocks = block_prefix(initial, updates, totals)
    across_block = jnp.einsum(
        "hnt,nthd,nhde->nthe", jnp.exp(within), query_wide, before_blocks, precision=HIGHEST
    )
    prefix_state = incoming(local_state, device_total)
    earlier_sum = jnp.cumsum(totals, axis=1) - totals
    reach_weight = jnp.exp(within + earlier_sum[:, :, None])
    late_term = jnp.einsum(
        "hnt,nthd,hde->nthe", reach_weight, query_wide, prefix_state, precision=HIGHEST
    )
    attended = within_block + across_block + late_term
    attended = attended.reshape(tokens_here, heads_here, DH)
    normed = attended * lax.rsqrt(jnp.mean(attended * attended, axis=-1, keepdims=True) + 1e-05)
    normed = normed.astype(jnp.bfloat16).reshape(tokens_here, heads_here * DH)
    token_features = lax.all_to_all(normed, "head", split_axis=0, concat_axis=1, tiled=True)
    weight_rows = lax.all_gather(w_out, "head", axis=0, tiled=True)
    mixed = jnp.dot(
        token_features,
        lax.all_gather(weight_rows, "seq", axis=1, tiled=True),
        preferred_element_type=jnp.float32,
    )
    return mixed.astype(jnp.bfloat16)


def solution(mesh):
    return jax.shard_map(
        on_device,
        mesh=mesh,
        in_specs=(
            P(("grp", "seq"), None),
            P(None, "head"),
            P(None, "head"),
            P(None, "head"),
            P("head", "seq"),
            P("head", ("grp", "seq")),
        ),
        out_specs=P(("grp", "seq", "head"), None),
        check_vma=False,
    )
```

profile of v0, /device:TPU:0, one launch (start us, length us, event | category | flops | bytes accessed | tf_op | source)
XLA Modules:
  0.0 212.9 jit_solution(9722926669350448896)
XLA Ops:
  8.1 2.3 %reduce-window.6 = f32[4,8,2,128]{3,1,2,0:T(8,128)S(1)} reduce-window(f32[4,8,2,128]{3,1,2,0:T(8,128)S(1)} %copy.81, f32[]{:T(128)} %constant.50.clone.1), window={size=1x1x1x128 pad=0_0x0_0x0_0x127_0}, to_apply=%region_0.0 | reduce-window | flops 1040384 | bytes 65540 | tf_op jit(solution)/shard_map/reduce-window
  11.1 9.1 %convolution_convert_fusion.1 = bf16[2048,512]{1,0:T(8,128)(2,1)} fusion(bf16[2048,2048]{1,0:T(8,128)(2,1)} %param.10, bf16[2048,512]{1,0:T(8,128)(2,1)S(1)} %copy-done), kind=kOutput, calls=%fused_computation.30 | convolution fusion | flops 4296015872 | bytes 12582912 | tf_op jit(solution)/shard_map/dot_general | solution.py:56
  20.2 4.0 %reshape.92 = bf16[8,256,4,128]{3,2,1,0:T(4,128)(2,1)} reshape(bf16[2048,512]{1,0:T(8,128)(2,1)} %convolution_convert_fusion.1) | data formatting | bytes 4194304 | tf_op jit(solution)/shard_map/reshape | solution.py:61
  24.2 2.8 %copy.90 = bf16[8,256,4,128]{1,3,2,0:T(8,128)(2,1)S(1)} copy(bf16[8,256,4,128]{3,2,1,0:T(4,128)(2,1)} %reshape.92) | data formatting | bytes 4194304 | tf_op jit(solution)/shard_map/reshape | solution.py:61
  27.1 10.7 %convolution_convert_fusion.3 = bf16[2048,512]{1,0:T(8,128)(2,1)} fusion(bf16[2048,2048]{1,0:T(8,128)(2,1)} %param.10, bf16[2048,512]{1,0:T(8,128)(2,1)} %param.13), kind=kOutput, calls=%fused_computation.32 | convolution fusion | flops 4296015872 | bytes 12582912 | tf_op jit(solution)/shard_map/dot_general | solution.py:57
  37.7 4.0 %reshape.90 = bf16[8,256,4,128]{3,2,1,0:T(4,128)(2,1)} reshape(bf16[2048,512]{1,0:T(8,128)(2,1)} %convolution_convert_fusion.3) | data formatting | bytes 4194304 | tf_op jit(solution)/shard_map/reshape | solution.py:64
  41.8 5.4 %fusion.11 = f32[8,4,128,128]{3,2,1,0:T(8,128)} fusion(bf16[8,256,4,128]{1,3,2,0:T(8,128)(2,1)S(1)} %copy.90, f32[8,256,4]{1,2,0:T(4,128)S(1)} %copy.89, bf16[8,256,4,128]{3,2,1,0:T(4,128)(2,1)} %reshape.90), kind=kOutput, calls=%fused_computation.22 | convolution fusion | flops 1612709888 | bytes 6324224 | tf_op jit(solution)/shard_map/hns,nshd,nshe->nhde/dot_general | solution.py:75
  47.2 14.4 %while.27 = (s32[]{:T(128)}, f32[4,128,128]{2,1,0:T(8,128)S(1)}, f32[8,4,128,128]{3,2,1,0:T(8,128)}, f32[8,4]{1,0:T(8,128)S(1)}, f32[8,4,128,128]{3,2,1,0:T(8,128)}, /*index=5*/s32[]{:T(128)}, s32[]{:T(128)}) while((s32[]{:T(128)}, f32[4,128,128]{2,1,0:T(8,128)S(1)}, f32[8,4,128,128]{3,2,1,0:T(8,128)}, f32[8,4]{1,0:T(8,128)S(1)}, ...), condition=%wide.region_3.4_spmd.clone, body=%wide.region_2.3_spmd.clone.sunk | while | flops 262147 | bytes 1311376 | solution.py:48
  64.6 8.5 %all-reduce = f32[16]{0:T(128)S(1)} all-reduce(f32[16]{0:T(128)S(1)} %dynamic-update-slice), channel_id=2, replica_groups=mesh['grp'=2,'seq'=4,'head'=4] {'seq'}, use_global_device_ids=true, to_apply=%add | all-reduce | flops 16 | bytes 128
  73.2 9.2 %convolution_convert_fusion.2 = bf16[2048,512]{1,0:T(8,128)(2,1)} fusion(bf16[2048,2048]{1,0:T(8,128)(2,1)} %param.10, bf16[2048,512]{1,0:T(8,128)(2,1)S(1)} %copy-done.6), kind=kOutput, calls=%fused_computation.31 | convolution fusion | flops 4296015872 | bytes 12582912 | tf_op jit(solution)/shard_map/dot_general | solution.py:55
  82.4 2.5 %reshape.91 = bf16[8,256,4,128]{3,2,1,0:T(4,128)(2,1)S(1)} reshape(bf16[2048,512]{1,0:T(8,128)(2,1)} %convolution_convert_fusion.2) | data formatting | bytes 4194304 | tf_op jit(solution)/shard_map/reshape | solution.py:60
  85.0 7.9 %fusion.9 = f32[8,4,256,128]{2,3,1,0:T(8,128)} fusion(f32[8,4,128,128]{3,2,1,0:T(8,128)} %get-tuple-element.127, f32[8,256,4]{1,2,0:T(4,128)S(1)} %copy.87, bf16[8,256,4,128]{3,2,1,0:T(4,128)(2,1)S(1)} %reshape.91), kind=kOutput, calls=%fused_computation.16 | convolution fusion | flops 1612709888 | bytes 8421376 | tf_op jit(solution)/shard_map/hnt,nthd,nhde->nthe/dot_general | solution.py:81
  92.9 1.2 fusion.25
  94.7 8.8 %fusion.3 = f32[8,4,128,256]{3,2,1,0:T(8,128)} fusion(f32[4,8,256,256]{3,2,0,1:T(8,128)S(1)} %fusion.25, f32[4,8,256]{2,0,1:T(4,128)S(1)} %copy.84, pred[256,256]{1,0:T(8,128)(4,1)S(1)} %iota_compare_fusion, bf16[8,256,4,128]{3,2,1,0:T(4,128)(2,1)S(1)} %copy-done.5), kind=kOutput, calls=%fused_computation.8 | convolution fusion | flops 3229614080 | bytes 14778368 | tf_op jit(solution)/shard_map/hnts,nshd->nthd/dot_general | solution.py:73
  103.5 3.3 %while.28 = (s32[]{:T(128)}, f32[4,128,128]{2,1,0:T(8,128)S(1)}, s32[]{:T(128)}, f32[4,4]{1,0:T(4,128)S(1)}, f32[4,4,128,128]{3,2,1,0:T(8,128)}, /*index=5*/s32[]{:T(128)}, s32[]{:T(128)}) while((s32[]{:T(128)}, f32[4,128,128]{2,1,0:T(8,128)S(1)}, s32[]{:T(128)}, f32[4,4]{1,0:T(4,128)S(1)}, f32[4,4,128,128]{3,2,1,0:T(8,128)}, ...), condition=%wide.region_7.8_spmd.clone, body=%wide.region_6.7_spmd.clone.sunk | while | flops 262148 | bytes 786585 | solution.py:24
  106.7 8.7 %multiply_reduce_fusion = (f32[8,256,4]{1,2,0:T(4,128)S(1)}, f32[8,256,4,128]{1,3,2,0:T(8,128)}) fusion(f32[4,128,128]{2,1,0:T(8,128)S(1)} %get-tuple-element.129, f32[8,256,4]{1,2,0:T(4,128)S(1)} %copy.94, bf16[8,256,4,128]{3,2,1,0:T(4,128)(2,1)S(1)} %reshape.91, f32[8,4,256,128]{2,3,1,0:T(8,128)} %fusion.9, f32[8,4,128,256]{3,2,1,0:T(8,128)} %fusion.3), kind=kOutput, calls=%fused_computation.21 | convolution fusion | flops 1616896000 | bytes 15007744 | tf_op jit(solution)/shard_map/hnt,nthd,hde->nthe/dot_general | solution.py:87
  115.9 3.9 %mul.51 = f32[2048,4,128]{2,1,0:T(4,128)} broadcast(f32[2048,4]{1,0:T(8,128)S(1)} %copy.97), dimensions={0,1} | broadcast | bytes 4227072 | tf_op jit(solution)/shard_map/mul | solution.py:92
  119.7 5.5 %mul.52 = f32[4,512,512]{2,1,0:T(8,128)} reshape(f32[2048,4,128]{2,1,0:T(4,128)} %mul.51) | data formatting | bytes 8388608 | tf_op jit(solution)/shard_map/mul | solution.py:92
  125.2 5.2 %copy.96 = f32[8,256,4,128]{3,2,1,0:T(4,128)} copy(f32[8,256,4,128]{1,3,2,0:T(8,128)} %get-tuple-element.219) | data formatting | bytes 8388608 | tf_op jit(solution)/shard_map/add | solution.py:90
  130.4 5.5 %reshape.95 = f32[4,512,512]{2,1,0:T(8,128)} reshape(f32[8,256,4,128]{3,2,1,0:T(4,128)} %copy.96) | data formatting | bytes 8388608 | tf_op jit(solution)/shard_map/reshape | solution.py:91
  135.9 4.2 %multiply_convert_fusion = bf16[4,512,512]{2,1,0:T(8,128)(2,1)S(1)} fusion(f32[4,512,512]{2,1,0:T(8,128)} %reshape.95, f32[4,512,512]{2,1,0:T(8,128)} %mul.52), kind=kLoop, calls=%fused_computation.20 | loop fusion | flops 2097152 | bytes 10485760 | tf_op jit(solution)/shard_map/convert_element_type | solution.py:93
  140.1 52.1 %all_to_all.16 = bf16[4,512,512]{2,1,0:T(8,128)(2,1)} all-to-all(bf16[4,512,512]{2,1,0:T(8,128)(2,1)S(1)} %multiply_convert_fusion), channel_id=1, replica_groups=mesh['grp'=2,'seq'=4,'head'=4] {'head'}, dimensions={0} | all-to-all | bytes 4194304 | tf_op jit(solution)/shard_map/all_to_all | solution.py:94
  192.2 4.2 %copy.98 = bf16[512,4,512]{0,2,1:T(8,128)(2,1)} copy(bf16[512,4,512]{2,0,1:T(8,128)(2,1)} %bitcast.63) | data formatting | bytes 4194304 | tf_op jit(solution)/shard_map/all_to_all | solution.py:94
  196.3 10.0 %convolution_convert_fusion = bf16[512,2048]{1,0:T(8,128)(2,1)} fusion(bf16[512,2048]{0,1:T(8,128)(2,1)} %bitcast.64, bf16[2048,2048]{1,0:T(8,128)(2,1)} %all-gather.8.cloned.1.call-done), kind=kOutput, calls=%fused_computation.29 | convolution fusion | flops 4296015872 | bytes 12582912 | tf_op jit(solution)/shard_map/dot_general | solution.py:96
  (82 shorter events, 23.1 us)
Async XLA Ops:
  6.5 4.6 %copy-start = (bf16[2048,512]{1,0:T(8,128)(2,1)S(1)}, bf16[2048,512]{1,0:T(8,128)(2,1)}, u32[]{:S(2)}) copy-start(bf16[2048,512]{1,0:T(8,128)(2,1)} %param.12) | copy-start | bytes 6291460
  6.5 55.9 %all-gather.6.cloned.1.call-start = ((), (), s32[]{:S(2)}) async-start(), calls=%async_computation.1 | async-start | bytes 2621440 | tf_op jit(solution)/shard_map/all_gather | solution.py:95
  7.3 96.2 %all-gather.10.cloned.1.call-start = ((), (), s32[]{:S(2)}) async-start(), calls=%async_computation.3 | async-start | bytes 1310720 | tf_op jit(solution)/shard_map/all_gather | solution.py:15
  27.1 14.7 %copy-start.3 = (bf16[8,256,4,128]{1,3,2,0:T(8,128)(2,1)}, bf16[8,256,4,128]{1,3,2,0:T(8,128)(2,1)S(1)}, u32[]{:S(2)}) copy-start(bf16[8,256,4,128]{1,3,2,0:T(8,128)(2,1)S(1)} %copy.90) | copy-start | bytes 6291460
  61.6 0.7 copy-start.2
  61.6 1.5 copy-start.7
  61.6 11.6 %copy-start.6 = (bf16[2048,512]{1,0:T(8,128)(2,1)S(1)}, bf16[2048,512]{1,0:T(8,128)(2,1)}, u32[]{:S(2)}) copy-start(bf16[2048,512]{1,0:T(8,128)(2,1)} %param.11) | copy-start | bytes 6291460
  62.3 134.0 %all-gather.8.cloned.1.call-start = ((), (), s32[]{:S(2)}) async-start(), calls=%async_computation.2 | async-start | bytes 10485760 | tf_op jit(solution)/shard_map/all_gather | solution.py:98
  85.0 7.9 %copy-start.4 = (bf16[8,256,4,128]{1,3,2,0:T(8,128)(2,1)S(1)}, bf16[8,256,4,128]{1,3,2,0:T(8,128)(2,1)}, u32[]{:S(2)}) copy-start(bf16[8,256,4,128]{1,3,2,0:T(8,128)(2,1)} %copy-done.3) | copy-start | bytes 6291460
  92.9 1.8 copy-start.5
  196.3 10.0 %copy-start.1 = (bf16[2048,512]{1,0:T(8,128)(2,1)S(1)}, bf16[2048,512]{1,0:T(8,128)(2,1)}, u32[]{:S(2)}) copy-start(bf16[2048,512]{1,0:T(8,128)(2,1)} %param.12) | copy-start | bytes 6291460
Sparse Core Ops, SparseCore 0:
  8.9 48.6 all-gather.5
  62.5 19.4 all-gather.9
  83.5 58.2 all-gather.7
where the time goes:
time: 214 us; the launch traced here: 213 us
  matrix products  71.1 us (33%)
  blocking collectives  60.5 us (28%)
  local copies, waits for them, and re-layouts  41.4 us (19%)
  other arithmetic  24.2 us (11%)
  between operations  14 us (7%)
    all_to_all x1, blocking collectives, on_device(): lax.all_to_all(normed, 'head', split_axis=0, concat_axis=1, tiled=True)  52.1 us
    dot_general x1, matrix products, on_device(): jnp.dot(activations, w_value, preferred_element_type=jnp.float32)  10.7 us
    dot_general x1, matrix products, on_device(): jnp.dot(token_features, lax.all_gather(weight_rows, 'seq', axis=1, tiled=...  10 us
    mul x2, local copies, waits for them, and re-layouts, on_device(): attended * lax.rsqrt(jnp.mean(attended * attended, axis=-1, keepdims=True...  9.33 us
    dot_general x1, matrix products, on_device(): jnp.dot(activations, w_query, preferred_element_type=jnp.float32)  9.19 us
    dot_general x1, matrix products, on_device(): jnp.dot(activations, w_key, preferred_element_type=jnp.float32)  9.11 us
    dot_general x1, matrix products, on_device(): jnp.einsum('hnts,nshd->nthd', scores * decay_mask, value_wide, precision=...  8.77 us
    dot_general x1, matrix products, on_device(): jnp.einsum('hnt,nthd,hde->nthe', reach_weight, query_wide, prefix_state,...  8.74 us
  transfers between devices with their start and end apart: 3, of which 0 were waited for; matrix products, arithmetic and copies ran while one was open for 59% of the time, Pallas kernels for 0%

commit v1 on v0

v1 whole, which is shorter than its diff:
```python
import functools

import jax
import jax.numpy as jnp
from jax import lax
from jax.experimental import pallas as pl
from jax.experimental.pallas import tpu as pltpu
from jax.sharding import PartitionSpec as P

DH = 128
BLOCK = 256
STEP = 512
EXTRA = 16
CHUNKS = ((0, 2), (2, 4))
F32 = jnp.float32
BF16 = jnp.bfloat16
HIGHEST = lax.Precision.HIGHEST
MIB = 1 << 20


def dot(a, b, dims=((1,), (0,)), precision=None):
    return lax.dot_general(a, b, (dims, ((), ())), precision=precision, preferred_element_type=F32)


def relative_half(part, width):
    start = lax.rem(part + lax.axis_index("grp"), 2) * width
    return pl.ds(pl.multiple_of(start, width), width)


def kv_kernel(act, wk, wv, decay, k_out, v_out, before, payload, wcol, wrow, state, factor):
    step = pl.program_id(0)
    heads, tokens = decay.shape
    blocks = tokens // BLOCK
    half = heads // 2

    @pl.when(step == 0)
    def _():
        logs = decay[...]
        swapped = jnp.concatenate([logs[half:], logs[:half]], axis=0)
        logs = jnp.where(lax.axis_index("grp") == 0, logs, swapped)
        logs = jnp.concatenate([logs, jnp.zeros((8 - heads, tokens), F32)], axis=0)
        stacked = jnp.concatenate(
            [logs[:, n * BLOCK : (n + 1) * BLOCK] for n in range(blocks)], axis=0
        )
        upper = (
            lax.broadcasted_iota(jnp.int32, (BLOCK, BLOCK), 0)
            <= lax.broadcasted_iota(jnp.int32, (BLOCK, BLOCK), 1)
        ).astype(F32)
        within = dot(stacked, upper, precision=HIGHEST)
        total = jnp.zeros((8, 1), F32)
        for n in range(blocks):
            rows = within[n * 8 : (n + 1) * 8]
            wrow[n] = rows
            wcol[n] = rows.T
            total = total + rows[:, BLOCK - 1 :]
        factor[...] = jnp.broadcast_to(jnp.exp(total), (8, DH))
        state[...] = jnp.zeros_like(state)

    rows = act[...]
    k_halves, v_halves = [], []
    for part in range(2):
        columns = relative_half(part, half * DH)
        k_halves.append(dot(rows, wk[:, columns]).astype(BF16))
        v_halves.append(dot(rows, wv[:, columns]).astype(BF16))
        k_out[:, part * half * DH : (part + 1) * half * DH] = k_halves[part]
        v_out[:, part * half * DH : (part + 1) * half * DH] = v_halves[part]
    for b in range(STEP // BLOCK):
        cols = wcol[step * (STEP // BLOCK) + b]
        last = cols[BLOCK - 1 :]
        carry = jnp.exp(last - cols)
        shrink = jnp.exp(last)
        for h in range(heads):
            part, lane = h // half, (h % half) * DH
            k_b = k_halves[part][b * BLOCK : (b + 1) * BLOCK, lane : lane + DH]
            v_b = v_halves[part][b * BLOCK : (b + 1) * BLOCK, lane : lane + DH]
            k_b = (k_b.astype(F32) * carry[:, h : h + 1]).astype(BF16)
            update = dot(k_b, v_b, ((0,), (0,)))
            old = state[h]
            before[b, h] = old
            state[h] = shrink[:, h : h + 1] * old + update

    @pl.when(step == pl.num_programs(0) - 1)
    def _():
        for h in range(heads):
            payload[h, :DH] = state[h].astype(BF16)
            whole = jnp.broadcast_to(factor[h : h + 1], (EXTRA, DH))
            high = whole.astype(BF16).astype(F32)
            first = lax.broadcasted_iota(jnp.int32, (EXTRA, DH), 0) < EXTRA // 2
            payload[h, DH:] = jnp.where(first, high, whole - high).astype(BF16)


def project_kernel(act, w, out):
    half = out.shape[1] // 2
    rows = act[...]
    for part in range(2):
        columns = relative_half(part, half)
        out[:, part * half : (part + 1) * half] = dot(rows, w[:, columns]).astype(BF16)


def attend_kernel(first, count, received, q, k, v, before, wcol, wrow, *rest):
    arrivals, (out, prefix) = rest[:received], rest[received:]
    heads = range(first, first + count)

    @pl.when(pl.program_id(0) == 0)
    def _():
        for at, h in enumerate(heads):
            total = jnp.zeros((DH, DH), F32)
            reach = jnp.ones((1, DH), F32)
            for piece in arrivals:
                total = total + reach * piece[h, :DH].astype(F32)
                extra = piece[h, DH:].astype(F32)
                reach = reach * (extra[:1] + extra[EXTRA // 2 : EXTRA // 2 + 1])
            prefix[at] = total

    causal = lax.broadcasted_iota(jnp.int32, (BLOCK, BLOCK), 0) >= lax.broadcasted_iota(
        jnp.int32, (BLOCK, BLOCK), 1
    )
    for b in range(STEP // BLOCK):
        tokens = slice(b * BLOCK, (b + 1) * BLOCK)
        cols = wcol[b]
        grown = jnp.exp(cols)
        for at, h in enumerate(heads):
            lanes = slice(h * DH, (h + 1) * DH)
            q_b, k_b, v_b = q[tokens, lanes], k[tokens, lanes], v[tokens, lanes]
            spread = cols[:, h : h + 1] - wrow[b, h : h + 1]
            mask = jnp.exp(jnp.where(causal, jnp.minimum(spread, 0.0), -1e30))
            scores = (dot(q_b, k_b, ((1,), (1,))) * mask).astype(BF16)
            reached = (q_b.astype(F32) * grown[:, h : h + 1]).astype(BF16)
            carried = prefix[at]
            incoming = (before[b, h] + carried).astype(BF16)
            attended = dot(scores, v_b) + dot(reached, incoming)
            prefix[at] = carried * grown[BLOCK - 1 :, h : h + 1]
            mean = jnp.mean(attended * attended, axis=1, keepdims=True)
            out[tokens, at * DH : (at + 1) * DH] = (attended * lax.rsqrt(mean + 1e-5)).astype(BF16)


def out_kernel(plan, order, lead, features, *rest):
    if lead:
        earlier, rest = rest[0], rest[1:]
    weights, out = rest[:-1], rest[-1]
    mine, place = lax.axis_index("head"), lax.axis_index("seq")
    sources = features.shape[0]
    for offset, pieces in plan:
        total = None
        for at, first, count, lane, row, size, stride in pieces:
            for r in range(first, first + count):
                left = features[lax.bitwise_xor(mine, order[r]), :, lane : lane + size]
                start = (r - first) * stride + row
                term = dot(left, weights[at][start : start + size])
                total = term if total is None else total + term
        width = total.shape[1]
        columns = pl.ds(pl.multiple_of(lax.bitwise_xor(place, offset) * width, width), width)
        if lead:
            total = total + earlier[:, columns]
        out[:, columns] = total.astype(out.dtype)


def params(limit):
    return pltpu.CompilerParams(vmem_limit_bytes=limit, dimension_semantics=("arbitrary",))


def whole_block(shape):
    return pl.BlockSpec(shape, lambda i: (0,) * len(shape))


def keys_values(activations, w_key, w_value, log_decay):
    tokens, width = activations.shape
    heads = log_decay.shape[0]
    columns, blocks, inner = heads * DH, tokens // BLOCK, STEP // BLOCK
    row_block = pl.BlockSpec((STEP, columns), lambda i: (i, 0))
    return pl.pallas_call(
        kv_kernel,
        grid=(tokens // STEP,),
        in_specs=[
            pl.BlockSpec((STEP, width), lambda i: (i, 0)),
            whole_block((width, columns)),
            whole_block((width, columns)),
            whole_block((heads, tokens)),
        ],
        out_specs=[
            row_block,
            row_block,
            pl.BlockSpec((inner, heads, DH, DH), lambda i: (i, 0, 0, 0)),
            whole_block((heads, DH + EXTRA, DH)),
            whole_block((blocks, BLOCK, 8)),
            whole_block((blocks, 8, BLOCK)),
        ],
        out_shape=[
            jax.ShapeDtypeStruct((tokens, columns), BF16),
            jax.ShapeDtypeStruct((tokens, columns), BF16),
            jax.ShapeDtypeStruct((blocks, heads, DH, DH), F32),
            jax.ShapeDtypeStruct((heads, DH + EXTRA, DH), BF16),
            jax.ShapeDtypeStruct((blocks, BLOCK, 8), F32),
            jax.ShapeDtypeStruct((blocks, 8, BLOCK), F32),
        ],
        scratch_shapes=[pltpu.VMEM((heads, DH, DH), F32), pltpu.VMEM((8, DH), F32)],
        compiler_params=params(32 * MIB),
        name="keys_values",
    )(activations, w_key, w_value, log_decay)


def queries(activations, w_query):
    tokens, width = activations.shape
    columns = w_query.shape[1]
    return pl.pallas_call(
        project_kernel,
        grid=(tokens // STEP,),
        in_specs=[pl.BlockSpec((STEP, width), lambda i: (i, 0)), whole_block((width, columns))],
        out_specs=pl.BlockSpec((STEP, columns), lambda i: (i, 0)),
        out_shape=jax.ShapeDtypeStruct((tokens, columns), BF16),
        compiler_params=params(24 * MIB),
        name="queries",
    )(activations, w_query)


def attend(first, count, query, key, value, before, wcol, wrow, arrivals):
    tokens, columns = query.shape
    heads, inner = columns // DH, STEP // BLOCK
    row_block = pl.BlockSpec((STEP, columns), lambda i: (i, 0))
    return pl.pallas_call(
        functools.partial(attend_kernel, first, count, len(arrivals)),
        grid=(tokens // STEP,),
        in_specs=[
            row_block,
            row_block,
            row_block,
            pl.BlockSpec((inner, heads, DH, DH), lambda i: (i, 0, 0, 0)),
            pl.BlockSpec((inner, BLOCK, 8), lambda i: (i, 0, 0)),
            pl.BlockSpec((inner, 8, BLOCK), lambda i: (i, 0, 0)),
        ]
        + [whole_block(piece.shape) for piece in arrivals],
        out_specs=pl.BlockSpec((STEP, count * DH), lambda i: (i, 0)),
        out_shape=jax.ShapeDtypeStruct((tokens, count * DH), BF16),
        scratch_shapes=[pltpu.VMEM((count, DH, DH), F32)],
        compiler_params=params(24 * MIB),
        name="attend",
    )(query, key, value, before, wcol, wrow, *arrivals)


def swap(value, axis, bit):
    count = lax.axis_size(axis)
    return lax.ppermute(value, axis, [(i, i ^ bit) for i in range(count)])


def bits_of(count):
    return [1 << b for b in reversed(range(count.bit_length() - 1))]


def gather_rows(w_out):
    half = w_out.shape[0] // 2
    piece = lax.dynamic_slice_in_dim(w_out, lax.axis_index("grp") * half, half, axis=0)
    order = [0]
    for bit in bits_of(lax.axis_size("head")):
        piece = jnp.concatenate([piece, swap(piece, "head", bit)], axis=0)
        order = order + [r ^ bit for r in order]
    return piece, order


def gather_columns(piece):
    middle = piece.shape[0] // 2
    across, beside = swap(piece, "seq", 2), swap(piece, "grp", 1)
    corner = [swap(beside[:middle], "seq", 2), swap(across[middle:], "grp", 1)]
    found = {(0, 0): [piece], (0, 2): [across], (1, 0): [beside], (1, 2): corner}
    for bit in bits_of(lax.axis_size("seq"))[:-2]:
        found.update(
            {
                (g, s ^ bit): [swap(part, "seq", bit) for part in parts]
                for (g, s), parts in list(found.items())
            }
        )
    found.update(
        {(g, s ^ 1): [swap(part, "seq", 1) for part in parts] for (g, s), parts in found.items()}
    )
    return found


def project_out(features, found, order, first, count, heads, earlier, dtype):
    sources, rows, _ = features.shape
    half = heads // 2
    operands, plan = [], []
    for offset in sorted({s for _, s in found}):
        pieces = []
        for g in range(2):
            low, high = max(first, g * half), min(first + count, (g + 1) * half)
            if low >= high:
                continue
            done = 0
            for part in found[(g, offset)]:
                held = part.shape[0] // (half * DH)
                pieces.append((len(operands), done, held, (low - first) * DH, (low - g * half) * DH,
                               (high - low) * DH, half * DH))
                operands.append(part)
                done += held
        plan.append((offset, tuple(pieces)))
    width = sum(1 for _ in plan) * operands[0].shape[1]
    lead = [] if earlier is None else [earlier]
    return pl.pallas_call(
        functools.partial(out_kernel, tuple(plan), order, bool(lead)),
        out_shape=jax.ShapeDtypeStruct((rows, width), dtype),
        compiler_params=pltpu.CompilerParams(vmem_limit_bytes=40 * MIB),
        name="project_out",
    )(features, *lead, *operands)


def on_device(activations, w_query, w_key, w_value, w_out, log_decay):
    heads, tokens = log_decay.shape
    places, sources = lax.axis_size("seq"), lax.axis_size("head")
    rows, order = gather_rows(w_out)
    key, value, before, payload, wcol, wrow = keys_values(activations, w_key, w_value, log_decay)
    arrivals = [
        lax.ppermute(payload, "seq", [(i, i + r) for i in range(places - r)])
        for r in range(1, places)
    ]
    query = queries(activations, w_query)
    found = gather_columns(rows)
    chunks = CHUNKS if heads == 4 else ((0, heads),)
    mixed = None
    for first, last in chunks:
        normed = attend(first, last - first, query, key, value, before, wcol, wrow, arrivals)
        features = lax.all_to_all(
            normed.reshape(sources, tokens // sources, (last - first) * DH), "head", 0, 0
        )
        dtype = BF16 if last == heads else F32
        mixed = project_out(features, found, order, first, last - first, heads, mixed, dtype)
    return mixed


def solution(mesh):
    return jax.shard_map(
        on_device,
        mesh=mesh,
        in_specs=(
            P(("grp", "seq"), None),
            P(None, "head"),
            P(None, "head"),
            P(None, "head"),
            P("head", "seq"),
            P("head", ("grp", "seq")),
        ),
        out_specs=P(("grp", "seq", "head"), None),
        check_vma=False,
    )
```

time: 214 us -> 142 us (0.66)
  matrix products: 71.1 us -> 0 us
  blocking collectives: 60.5 us -> 0 us
  waiting for transfers between devices: 1.4 us -> 49.1 us
  Pallas kernels: 0 us -> 34.2 us
  starting transfers between devices: 0.08 us -> 25.5 us
  other arithmetic: 24.2 us -> 3.12 us
  between operations: 14 us -> 0.26 us
  local copies, waits for them, and re-layouts: 41.4 us -> 28.8 us
    dot_general x9 -> x0, matrix products: 71.1 us -> none  [the longest x1 10.7 us: on_device(): jnp.dot(activations, w_value, preferred_element_type=jnp.float32)]
    all_to_all x1 -> x0, blocking collectives: 52.1 us -> none  [on_device(): lax.all_to_all(normed, 'head', split_axis=0, concat_axis=1, tiled=True)]
    ppermute x0 -> x14, waiting for transfers between devices: none -> 49.1 us  [the longest x11 49.1 us: swap(): return lax.ppermute(value, axis, [(i, i ^ bit) for i in range(count)])]
    pallas_call x0 -> x6, Pallas kernels: none -> 34.2 us  [the longest x1 11.1 us: keys_values(): pl.pallas_call(kv_kernel, grid=(tokens // STEP,), in_specs=[pl.BlockSpec(...]
    unnamed x20 -> x46, local copies, waits for them, and re-layouts: 2.19 us -> 26.6 us
    reshape x7 -> x0, local copies, waits for them, and re-layouts: 19.6 us -> none  [the longest x2 6.8 us: on_device(): key_blocks = key_proj.reshape(blocks, BLOCK, heads_here, DH)]
    ppermute x0 -> x14, starting transfers between devices: none -> 17.5 us  [the longest x11 9.48 us: swap(): return lax.ppermute(value, axis, [(i, i ^ bit) for i in range(count)])]
    mul x2 -> x0, local copies, waits for them, and re-layouts: 9.33 us -> none  [on_device(): attended * lax.rsqrt(jnp.mean(attended * attended, axis=-1, keepdims=True...]
  transfers between devices with their start and end apart: 3 -> 16, of which waited for: 0 -> 4; matrix products, arithmetic and copies ran while one was open for 59% -> 4% of each run, Pallas kernels for 0% -> 13%
where the time goes in v1:
time: 142 us; the launch traced here: 141 us
  waiting for transfers between devices  49.1 us (35%)
  Pallas kernels  34.2 us (24%)
  local copies, waits for them, and re-layouts  28.8 us (20%)
  starting transfers between devices  25.5 us (18%)
  other arithmetic  3.12 us (2%)
    ppermute x11, waiting for transfers between devices, swap(): return lax.ppermute(value, axis, [(i, i ^ bit) for i in range(count)])  49.1 us
    unnamed x46, local copies, waits for them, and re-layouts  26.6 us
    pallas_call x1, Pallas kernels, keys_values(): pl.pallas_call(kv_kernel, grid=(tokens // STEP,), in_specs=[pl.BlockSpec(...  11.1 us
    pallas_call x2, Pallas kernels, project_out(): pl.pallas_call(functools.partial(out_kernel, tuple(plan), order, bool(lea...  9.52 us
    ppermute x11, starting transfers between devices, swap(): return lax.ppermute(value, axis, [(i, i ^ bit) for i in range(count)])  9.48 us
    pallas_call x2, Pallas kernels, attend(): pl.pallas_call(functools.partial(attend_kernel, first, count, len(arrival...  8.44 us
    ppermute x3, starting transfers between devices, on_device(): lax.ppermute(payload, 'seq', [(i, i + r) for i in range(places - r)])  8.06 us
    all_to_all x2, starting transfers between devices, on_device(): lax.all_to_all(normed.reshape(sources, tokens // sources, (last - first)...  7.93 us
  transfers between devices with their start and end apart: 16, of which 4 were waited for; matrix products, arithmetic and copies ran while one was open for 4% of the time, Pallas kernels for 13%

profile of v1, /device:TPU:0, one launch (start us, length us, event | category | flops | bytes accessed | tf_op | source)
XLA Modules:
  0.0 141.0 jit_solution(5201829477480741523)
XLA Ops:
  0.0 3.4 %copy-done.1 = bf16[2048,2048]{1,0:T(8,128)(2,1)S(1)} copy-done((bf16[2048,2048]{1,0:T(8,128)(2,1)S(1)}, bf16[2048,2048]{1,0:T(8,128)(2,1)}, u32[]{:S(2)}) %copy-start.1) | copy-done | bytes 8388632
  7.4 11.1 %keys_values.1 = (bf16[2048,512]{1,0:T(8,128)(2,1)S(1)}, bf16[2048,512]{1,0:T(8,128)(2,1)S(1)}, f32[8,4,128,128]{3,2,1,0:T(8,128)S(1)}, bf16[4,144,128]{2,1,0:T(...) custom-call(bf16[2048,2048]{1,0:T(8,128)(2,1)S(1)} %copy-done.1, bf16[2048,512]{1,0:T(8,128)(2,1)S(1)} %copy-done.19, ...), custom_call_target="tpu_custom_call" | custom-call | tf_op jit(solution)/shard_map/keys_values/pallas_call | solution.py:171
  23.5 2.4 %collective-permute-start = (bf16[4,144,128]{2,1,0:T(8,128)(2,1)S(1)}, bf16[4,144,128]{2,1,0:T(8,128)(2,1)S(1)}, u32[]{:S(2)}, u32[]{:S(2)}) collective-permute-start(bf16[4,144,128]{2,1,0:T(8,128)(2,1)S(1)} %get-tuple-element.16), channel_id=1, source_target_pairs={{0,4},{4,8},{8,12},{1,5},{5,9},{9,13},{2,6},{6,10},{10,14},{3,7},{... | collective-permute-start | bytes 442376 | tf_op jit(solution)/shard_map/ppermute | solution.py:311
  25.8 4.4 %collective-permute-start.1 = (bf16[4,144,128]{2,1,0:T(8,128)(2,1)S(1)}, bf16[4,144,128]{2,1,0:T(8,128)(2,1)S(1)}, u32[]{:S(2)}, u32[]{:S(2)}) collective-permute-start(bf16[4,144,128]{2,1,0:T(8,128)(2,1)S(1)} %get-tuple-element.16), channel_id=1, source_target_pairs={{0,8},{4,12},{1,9},{5,13},{2,10},{6,14},{3,11},{7,15},{16,24},{20,... | collective-permute-start | bytes 442376 | tf_op jit(solution)/shard_map/ppermute | solution.py:311
  31.6 2.7 %collective-permute-start.3 = (bf16[256,512]{1,0:T(8,128)(2,1)S(1)}, bf16[256,512]{1,0:T(8,128)(2,1)}, u32[]{:S(2)}, u32[]{:S(2)}) collective-permute-start(bf16[256,512]{1,0:T(8,128)(2,1)S(1)} %constant_dynamic-slice_fusion), channel_id=1, source_target_pairs={{0,2},{1,3},{2,0},{3,1},{4,6},{5,7},{6,4},{7,5},{8,10},{9,11},{10,... | collective-permute-start | bytes 786440 | tf_op jit(solution)/shard_map/ppermute | solution.py:242
  34.3 3.4 %copy-done.2 = bf16[2048,2048]{1,0:T(8,128)(2,1)S(1)} copy-done((bf16[2048,2048]{1,0:T(8,128)(2,1)S(1)}, bf16[2048,2048]{1,0:T(8,128)(2,1)}, u32[]{:S(2)}) %copy-start.2) | copy-done | bytes 8388632
  37.6 1.6 %copy-done.21 = bf16[2048,512]{1,0:T(8,128)(2,1)S(1)} copy-done((bf16[2048,512]{1,0:T(8,128)(2,1)S(1)}, bf16[2048,512]{1,0:T(8,128)(2,1)}, u32[]{:S(2)}) %copy-start.21) | copy-done | bytes 2097176
  39.2 5.1 %queries.1.q = bf16[2048,512]{1,0:T(8,128)(2,1)S(1)} custom-call(bf16[2048,2048]{1,0:T(8,128)(2,1)S(1)} %copy-done.2, bf16[2048,512]{1,0:T(8,128)(2,1)S(1)} %copy-done.21), custom_call_target="tpu_custom_call" | custom-call | tf_op jit(solution)/shard_map/queries/pallas_call | solution.py:205
  44.5 4.2 %attend.3 = bf16[2048,256]{1,0:T(8,128)(2,1)S(1)} custom-call(bf16[2048,512]{1,0:T(8,128)(2,1)S(1)} %queries.1.q, bf16[2048,512]{1,0:T(8,128)(2,1)S(1)} %copy-done.6, bf16[2048,512]{1,0:T(8,128)(2,1)S(1)} %copy-done.9, f32[8,4,128,128]{3,2,1,0:T(8,128)S(1)} %copy-done.12, f32[8,256,8]{2,1,0:T(8,128)S(1)} %copy-done.17, ...), custom_call_target="tpu_custom_call" | custom-call | tf_op jit(solution)/shard_map/attend/pallas_call | solution.py:220
  49.6 4.2 %all-to-all-start.1 = ((bf16[4,512,256]{2,1,0:T(8,128)(2,1)}), bf16[4,512,256]{2,1,0:T(8,128)(2,1)}, u32[]{:S(2)}, u32[]{:S(2)}) async-start(bf16[4,512,256]{2,1,0:T(8,128)(2,1)} %bitcast.3), calls=%async_computation.1 | async-start | bytes 2097152 | tf_op jit(solution)/shard_map/all_to_all | solution.py:320
  55.1 2.0 %collective-permute-start.4 = (bf16[512,512]{1,0:T(8,128)(2,1)S(1)}, bf16[512,512]{1,0:T(8,128)(2,1)S(1)}, u32[]{:S(2)}, u32[]{:S(2)}) collective-permute-start(bf16[512,512]{1,0:T(8,128)(2,1)S(1)} %pad_maximum_fusion.1), channel_id=1, source_target_pairs={{0,1},{1,0},{2,3},{3,2},{4,5},{5,4},{6,7},{7,6},{8,9},{9,8},{10,11... | collective-permute-start | bytes 1572872 | tf_op jit(solution)/shard_map/ppermute | solution.py:242
  57.1 26.2 %collective-permute-done.4 = bf16[512,512]{1,0:T(8,128)(2,1)S(1)} collective-permute-done((bf16[512,512]{1,0:T(8,128)(2,1)S(1)}, bf16[512,512]{1,0:T(8,128)(2,1)S(1)}, u32[]{:S(2)}, u32[]{:S(2)}) %collective-permute-start.4) | collective-permute-done | bytes 524320 | tf_op jit(solution)/shard_map/ppermute | solution.py:242
  83.3 2.0 %pad_maximum_fusion.rest_0_ = bf16[1024,512]{1,0:T(8,128)(2,1)} fusion(bf16[512,512]{1,0:T(8,128)(2,1)S(1)} %collective-permute-done.4, bf16[256,512]{1,0:T(8,128)(2,1)} %collective-permute-done.3, bf16[256,512]{1,0:T(8,128)(2,1)S(1)} %constant_dynamic-slice_fusion), kind=kLoop, calls=%fused_computation | loop fusion | flops 3145728 | bytes 2097152 | tf_op jit(solution)/shard_map/concatenate | solution.py:254
  86.8 1.6 %copy-done.10 = bf16[2048,512]{1,0:T(8,128)(2,1)S(1)} copy-done((bf16[2048,512]{1,0:T(8,128)(2,1)S(1)}, bf16[2048,512]{1,0:T(8,128)(2,1)}, u32[]{:S(2)}) %copy-start.10) | copy-done | bytes 2097176
  90.0 4.2 %attend.2 = bf16[2048,256]{1,0:T(8,128)(2,1)S(1)} custom-call(bf16[2048,512]{1,0:T(8,128)(2,1)S(1)} %queries.1.q, bf16[2048,512]{1,0:T(8,128)(2,1)S(1)} %copy-done.7, bf16[2048,512]{1,0:T(8,128)(2,1)S(1)} %copy-done.10, f32[8,4,128,128]{3,2,1,0:T(8,128)S(1)} %copy-done.13, f32[8,256,8]{2,1,0:T(8,128)S(1)} %copy-done.18, ...), custom_call_target="tpu_custom_call" | custom-call | tf_op jit(solution)/shard_map/attend/pallas_call | solution.py:220
  95.2 3.7 %all-to-all-start = ((bf16[4,512,256]{2,1,0:T(8,128)(2,1)}), bf16[4,512,256]{2,1,0:T(8,128)(2,1)S(1)}, u32[]{:S(2)}, u32[]{:S(2)}) async-start(bf16[4,512,256]{2,1,0:T(8,128)(2,1)} %bitcast.2), calls=%async_computation | async-start | bytes 2097152 | tf_op jit(solution)/shard_map/all_to_all | solution.py:320
  98.9 9.9 %collective-permute-done.6.rest_2_ = bf16[1024,512]{1,0:T(8,128)(2,1)} collective-permute-done((bf16[1024,512]{1,0:T(8,128)(2,1)}, bf16[1024,512]{1,0:T(8,128)(2,1)}, u32[]{:S(2)}, u32[]{:S(2)}) %collective-permute-start.6) | collective-permute-done | bytes 1048608 | tf_op jit(solution)/shard_map/ppermute | solution.py:242
  109.9 1.8 %collective-permute-start.10 = (bf16[512,512]{1,0:T(8,128)(2,1)S(1)}, bf16[512,512]{1,0:T(8,128)(2,1)S(1)}, u32[]{:S(2)}, u32[]{:S(2)}) collective-permute-start(bf16[512,512]{1,0:T(8,128)(2,1)S(1)} %slice.8), channel_id=1, source_target_pairs={{0,8},{4,12},{8,0},{12,4},{1,9},{5,13},{9,1},{13,5},{2,10},{6,14},... | collective-permute-start | bytes 1572872 | tf_op jit(solution)/shard_map/ppermute | solution.py:242
  114.3 10.0 %collective-permute-done.10.rest_3_ = bf16[512,512]{1,0:T(8,128)(2,1)S(1)} collective-permute-done((bf16[512,512]{1,0:T(8,128)(2,1)S(1)}, bf16[512,512]{1,0:T(8,128)(2,1)S(1)}, u32[]{:S(2)}, u32[]{:S(2)}) %collective-permute-start.10) | collective-permute-done | bytes 524320 | tf_op jit(solution)/shard_map/ppermute | solution.py:242
  124.3 3.0 %collective-permute-done.11.rest_4_ = bf16[512,512]{1,0:T(8,128)(2,1)} collective-permute-done((bf16[512,512]{1,0:T(8,128)(2,1)S(1)}, bf16[512,512]{1,0:T(8,128)(2,1)}, u32[]{:S(2)}, u32[]{:S(2)}) %collective-permute-start.11) | collective-permute-done | bytes 524320 | tf_op jit(solution)/shard_map/ppermute | solution.py:242
  127.3 4.2 %project_out.2.rest_0_ = f32[512,2048]{1,0:T(8,128)S(1)} custom-call(bf16[4,512,256]{2,1,0:T(8,128)(2,1)} %all-to-all-done.1.features, bf16[1024,512]{1,0:T(8,128)(2,1)} %pad_maximum_fusion.rest_0_, bf16[1024,512]{1,0:T(8,128)(2,1)S(1)} %collective-permute-done.5.rest_1_, bf16[1024,512]{1,0:T(8,128)(2,1)} %collective-permute-done.6.rest_2_, ...), custom_call_target="tpu_custom_call" | custom-call | tf_op jit(solution)/shard_map/project_out/pallas_call | solution.py:297
  131.5 2.0 %copy-done.3 = f32[512,2048]{1,0:T(8,128)} copy-done((f32[512,2048]{1,0:T(8,128)}, f32[512,2048]{1,0:T(8,128)S(1)}, u32[]{:S(2)}) %copy-start.3) | copy-done | bytes 4194328
  133.5 2.2 %copy-done.4 = f32[512,2048]{1,0:T(8,128)S(1)} copy-done((f32[512,2048]{1,0:T(8,128)S(1)}, f32[512,2048]{1,0:T(8,128)}, u32[]{:S(2)}) %copy-start.4) | copy-done | bytes 4194328
  135.7 5.3 %project_out.3 = bf16[512,2048]{1,0:T(8,128)(2,1)} custom-call(bf16[4,512,256]{2,1,0:T(8,128)(2,1)S(1)} %all-to-all-done.features, f32[512,2048]{1,0:T(8,128)S(1)} %copy-done.4, bf16[1024,512]{1,0:T(8,128)(2,1)} %collective-permute-done.8.rest_1_, bf16[1024,512]{1,0:T(8,128)(2,1)S(1)} %collective-permute-done.9.rest_2_, ...), custom_call_target="tpu_custom_call" | custom-call | tf_op jit(solution)/shard_map/project_out/pallas_call | solution.py:297
  (65 shorter events, 20.1 us)
Async XLA Ops:
  0.0 31.6 %copy-start = (bf16[512,512]{1,0:T(8,128)(2,1)S(1)}, bf16[512,512]{1,0:T(8,128)(2,1)}, u32[]{:S(2)}) copy-start(bf16[512,512]{1,0:T(8,128)(2,1)} %param.10) | copy-start | bytes 1572868
  0.0 3.4 %copy-start.1 = (bf16[2048,2048]{1,0:T(8,128)(2,1)S(1)}, bf16[2048,2048]{1,0:T(8,128)(2,1)}, u32[]{:S(2)}) copy-start(bf16[2048,2048]{1,0:T(8,128)(2,1)} %act.3) | copy-start | bytes 25165828
  23.5 20.9 %collective-permute-start = (bf16[4,144,128]{2,1,0:T(8,128)(2,1)S(1)}, bf16[4,144,128]{2,1,0:T(8,128)(2,1)S(1)}, u32[]{:S(2)}, u32[]{:S(2)}) collective-permute-start(bf16[4,144,128]{2,1,0:T(8,128)(2,1)S(1)} %get-tuple-element.16), channel_id=1, source_target_pairs={{0,4},{4,8},{8,12},{1,5},{5,9},{9,13},{2,6},{6,10},{10,14},{3,7},{... | collective-permute-start | bytes 442376 | tf_op jit(solution)/shard_map/ppermute | solution.py:311
  25.8 18.6 %collective-permute-start.1 = (bf16[4,144,128]{2,1,0:T(8,128)(2,1)S(1)}, bf16[4,144,128]{2,1,0:T(8,128)(2,1)S(1)}, u32[]{:S(2)}, u32[]{:S(2)}) collective-permute-start(bf16[4,144,128]{2,1,0:T(8,128)(2,1)S(1)} %get-tuple-element.16), channel_id=1, source_target_pairs={{0,8},{4,12},{1,9},{5,13},{2,10},{6,14},{3,11},{7,15},{16,24},{20,... | collective-permute-start | bytes 442376 | tf_op jit(solution)/shard_map/ppermute | solution.py:311
  30.2 14.2 %collective-permute-start.2 = (bf16[4,144,128]{2,1,0:T(8,128)(2,1)S(1)}, bf16[4,144,128]{2,1,0:T(8,128)(2,1)S(1)}, u32[]{:S(2)}, u32[]{:S(2)}) collective-permute-start(bf16[4,144,128]{2,1,0:T(8,128)(2,1)S(1)} %get-tuple-element.16), channel_id=1, source_target_pairs={{0,12},{1,13},{2,14},{3,15},{16,28},{17,29},{18,30},{19,31}} | collective-permute-start | bytes 442376 | tf_op jit(solution)/shard_map/ppermute | solution.py:311
  31.6 22.3 %collective-permute-start.3 = (bf16[256,512]{1,0:T(8,128)(2,1)S(1)}, bf16[256,512]{1,0:T(8,128)(2,1)}, u32[]{:S(2)}, u32[]{:S(2)}) collective-permute-start(bf16[256,512]{1,0:T(8,128)(2,1)S(1)} %constant_dynamic-slice_fusion), channel_id=1, source_target_pairs={{0,2},{1,3},{2,0},{3,1},{4,6},{5,7},{6,4},{7,5},{8,10},{9,11},{10,... | collective-permute-start | bytes 786440 | tf_op jit(solution)/shard_map/ppermute | solution.py:242
  39.2 5.2 %copy-start.6 = (bf16[2048,512]{1,0:T(8,128)(2,1)S(1)}, bf16[2048,512]{1,0:T(8,128)(2,1)}, u32[]{:S(2)}) copy-start(bf16[2048,512]{1,0:T(8,128)(2,1)} %copy-done.5) | copy-start | bytes 6291460
  39.2 5.2 %copy-start.9 = (bf16[2048,512]{1,0:T(8,128)(2,1)S(1)}, bf16[2048,512]{1,0:T(8,128)(2,1)}, u32[]{:S(2)}) copy-start(bf16[2048,512]{1,0:T(8,128)(2,1)} %copy-done.8) | copy-start | bytes 6291460
  39.2 5.2 %copy-start.12 = (f32[8,4,128,128]{3,2,1,0:T(8,128)S(1)}, f32[8,4,128,128]{3,2,1,0:T(8,128)}, u32[]{:S(2)}) copy-start(f32[8,4,128,128]{3,2,1,0:T(8,128)} %copy-done.11) | copy-start | bytes 6291460
  39.2 5.2 %copy-start.17 = (f32[8,256,8]{2,1,0:T(8,128)S(1)}, f32[8,256,8]{2,1,0:T(8,128)}, u32[]{:S(2)}) copy-start(f32[8,256,8]{2,1,0:T(8,128)} %copy-done.16) | copy-start | bytes 196612
  49.6 45.5 %all-to-all-start.1 = ((bf16[4,512,256]{2,1,0:T(8,128)(2,1)}), bf16[4,512,256]{2,1,0:T(8,128)(2,1)}, u32[]{:S(2)}, u32[]{:S(2)}) async-start(bf16[4,512,256]{2,1,0:T(8,128)(2,1)} %bitcast.3), calls=%async_computation.1 | async-start | bytes 2097152 | tf_op jit(solution)/shard_map/all_to_all | solution.py:320
  53.9 32.9 %copy-start.7 = (bf16[2048,512]{1,0:T(8,128)(2,1)S(1)}, bf16[2048,512]{1,0:T(8,128)(2,1)}, u32[]{:S(2)}) copy-start(bf16[2048,512]{1,0:T(8,128)(2,1)} %copy-done.5) | copy-start | bytes 6291460
  53.9 32.9 %copy-start.18 = (f32[8,256,8]{2,1,0:T(8,128)S(1)}, f32[8,256,8]{2,1,0:T(8,128)}, u32[]{:S(2)}) copy-start(f32[8,256,8]{2,1,0:T(8,128)} %copy-done.16) | copy-start | bytes 196612
  55.1 28.2 %collective-permute-start.4 = (bf16[512,512]{1,0:T(8,128)(2,1)S(1)}, bf16[512,512]{1,0:T(8,128)(2,1)S(1)}, u32[]{:S(2)}, u32[]{:S(2)}) collective-permute-start(bf16[512,512]{1,0:T(8,128)(2,1)S(1)} %pad_maximum_fusion.1), channel_id=1, source_target_pairs={{0,1},{1,0},{2,3},{3,2},{4,5},{5,4},{6,7},{7,6},{8,9},{9,8},{10,11... | collective-permute-start | bytes 1572872 | tf_op jit(solution)/shard_map/ppermute | solution.py:242
  85.3 23.5 %collective-permute-start.6 = (bf16[1024,512]{1,0:T(8,128)(2,1)}, bf16[1024,512]{1,0:T(8,128)(2,1)}, u32[]{:S(2)}, u32[]{:S(2)}) collective-permute-start(bf16[1024,512]{1,0:T(8,128)(2,1)} %pad_maximum_fusion.rest_0_), channel_id=1, source_target_pairs={{0,8},{4,12},{8,0},{12,4},{1,9},{5,13},{9,1},{13,5},{2,10},{6,14},... | collective-permute-start | bytes 3145736 | tf_op jit(solution)/shard_map/ppermute | solution.py:242
  85.3 23.5 %collective-permute-start.8 = (bf16[1024,512]{1,0:T(8,128)(2,1)}, bf16[1024,512]{1,0:T(8,128)(2,1)}, u32[]{:S(2)}, u32[]{:S(2)}) collective-permute-start(bf16[1024,512]{1,0:T(8,128)(2,1)} %pad_maximum_fusion.rest_0_), channel_id=1, source_target_pairs={{0,16},{16,0},{1,17},{17,1},{2,18},{18,2},{3,19},{19,3},{4,20},{20... | collective-permute-start | bytes 3145736 | tf_op jit(solution)/shard_map/ppermute | solution.py:242
  95.2 38.3 %all-to-all-start = ((bf16[4,512,256]{2,1,0:T(8,128)(2,1)}), bf16[4,512,256]{2,1,0:T(8,128)(2,1)S(1)}, u32[]{:S(2)}, u32[]{:S(2)}) async-start(bf16[4,512,256]{2,1,0:T(8,128)(2,1)} %bitcast.2), calls=%async_computation | async-start | bytes 2097152 | tf_op jit(solution)/shard_map/all_to_all | solution.py:320
  98.9 28.4 %collective-permute-start.5 = (bf16[1024,512]{1,0:T(8,128)(2,1)}, bf16[1024,512]{1,0:T(8,128)(2,1)S(1)}, u32[]{:S(2)}, u32[]{:S(2)}) collective-permute-start(bf16[1024,512]{1,0:T(8,128)(2,1)} %pad_maximum_fusion.rest_0_), channel_id=1, source_target_pairs={{0,4},{4,0},{8,12},{12,8},{1,5},{5,1},{9,13},{13,9},{2,6},{6,2},{1... | collective-permute-start | bytes 3145736 | tf_op jit(solution)/shard_map/ppermute | solution.py:242
  108.8 18.5 %collective-permute-start.7 = (bf16[1024,512]{1,0:T(8,128)(2,1)}, bf16[1024,512]{1,0:T(8,128)(2,1)S(1)}, u32[]{:S(2)}, u32[]{:S(2)}) collective-permute-start(bf16[1024,512]{1,0:T(8,128)(2,1)} %collective-permute-done.6.rest_2_), channel_id=1, source_target_pairs={{0,4},{4,0},{8,12},{12,8},{1,5},{5,1},{9,13},{13,9},{2,6},{6,2},{1... | collective-permute-start | bytes 3145736 | tf_op jit(solution)/shard_map/ppermute | solution.py:242
  109.9 14.4 %collective-permute-start.10 = (bf16[512,512]{1,0:T(8,128)(2,1)S(1)}, bf16[512,512]{1,0:T(8,128)(2,1)S(1)}, u32[]{:S(2)}, u32[]{:S(2)}) collective-permute-start(bf16[512,512]{1,0:T(8,128)(2,1)S(1)} %slice.8), channel_id=1, source_target_pairs={{0,8},{4,12},{8,0},{12,4},{1,9},{5,13},{9,1},{13,5},{2,10},{6,14},... | collective-permute-start | bytes 1572872 | tf_op jit(solution)/shard_map/ppermute | solution.py:242
  111.7 21.8 %collective-permute-start.9 = (bf16[1024,512]{1,0:T(8,128)(2,1)}, bf16[1024,512]{1,0:T(8,128)(2,1)S(1)}, u32[]{:S(2)}, u32[]{:S(2)}) collective-permute-start(bf16[1024,512]{1,0:T(8,128)(2,1)} %collective-permute-done.8.rest_1_), channel_id=1, source_target_pairs={{0,4},{4,0},{8,12},{12,8},{1,5},{5,1},{9,13},{13,9},{2,6},{6,2},{1... | collective-permute-start | bytes 3145736 | tf_op jit(solution)/shard_map/ppermute | solution.py:242
  112.8 14.5 %collective-permute-start.11 = (bf16[512,512]{1,0:T(8,128)(2,1)S(1)}, bf16[512,512]{1,0:T(8,128)(2,1)}, u32[]{:S(2)}, u32[]{:S(2)}) collective-permute-start(bf16[512,512]{1,0:T(8,128)(2,1)S(1)} %slice.9), channel_id=1, source_target_pairs={{0,16},{16,0},{1,17},{17,1},{2,18},{18,2},{3,19},{19,3},{4,20},{20... | collective-permute-start | bytes 1572872 | tf_op jit(solution)/shard_map/ppermute | solution.py:242
  124.3 9.2 %collective-permute-start.12 = (bf16[512,512]{1,0:T(8,128)(2,1)S(1)}, bf16[512,512]{1,0:T(8,128)(2,1)}, u32[]{:S(2)}, u32[]{:S(2)}) collective-permute-start(bf16[512,512]{1,0:T(8,128)(2,1)S(1)} %collective-permute-done.10.rest_3_), channel_id=1, source_target_pairs={{0,4},{4,0},{8,12},{12,8},{1,5},{5,1},{9,13},{13,9},{2,6},{6,2},{1... | collective-permute-start | bytes 1572872 | tf_op jit(solution)/shard_map/ppermute | solution.py:242
  127.3 6.2 %collective-permute-start.13 = (bf16[512,512]{1,0:T(8,128)(2,1)}, bf16[512,512]{1,0:T(8,128)(2,1)}, u32[]{:S(2)}, u32[]{:S(2)}) collective-permute-start(bf16[512,512]{1,0:T(8,128)(2,1)} %collective-permute-done.11.rest_4_), channel_id=1, source_target_pairs={{0,4},{4,0},{8,12},{12,8},{1,5},{5,1},{9,13},{13,9},{2,6},{6,2},{1... | collective-permute-start | bytes 1572872 | tf_op jit(solution)/shard_map/ppermute | solution.py:242
  (15 other events, 23.2 us)

commit v2 on v1

--- a/solution.py
+++ b/solution.py
@@ -97,7 +97,7 @@
         out[:, part * half : (part + 1) * half] = dot(rows, w[:, columns]).astype(BF16)
 
 
-def attend_kernel(first, count, received, q, k, v, before, wcol, wrow, *rest):
+def attend_kernel(first, count, lane, received, q, k, v, before, wcol, wrow, *rest):
     arrivals, (out, prefix) = rest[:received], rest[received:]
     heads = range(first, first + count)
 
@@ -120,14 +120,14 @@
         cols = wcol[b]
         grown = jnp.exp(cols)
         for at, h in enumerate(heads):
-            lanes = slice(h * DH, (h + 1) * DH)
+            lanes = slice((h - lane) * DH, (h - lane + 1) * DH)
             q_b, k_b, v_b = q[tokens, lanes], k[tokens, lanes], v[tokens, lanes]
             spread = cols[:, h : h + 1] - wrow[b, h : h + 1]
             mask = jnp.exp(jnp.where(causal, jnp.minimum(spread, 0.0), -1e30))
             scores = (dot(q_b, k_b, ((1,), (1,))) * mask).astype(BF16)
             reached = (q_b.astype(F32) * grown[:, h : h + 1]).astype(BF16)
             carried = prefix[at]
-            incoming = (before[b, h] + carried).astype(BF16)
+            incoming = (before[b, h - lane] + carried).astype(BF16)
             attended = dot(scores, v_b) + dot(reached, incoming)
             prefix[at] = carried * grown[BLOCK - 1 :, h : h + 1]
             mean = jnp.mean(attended * attended, axis=1, keepdims=True)
@@ -159,6 +159,10 @@
     return pltpu.CompilerParams(vmem_limit_bytes=limit, dimension_semantics=("arbitrary",))
 
 
+def cost(flops, moved):
+    return pl.CostEstimate(flops=flops, bytes_accessed=moved, transcendentals=0)
+
+
 def whole_block(shape):
     return pl.BlockSpec(shape, lambda i: (0,) * len(shape))
 
@@ -194,7 +198,8 @@
             jax.ShapeDtypeStruct((blocks, 8, BLOCK), F32),
         ],
         scratch_shapes=[pltpu.VMEM((heads, DH, DH), F32), pltpu.VMEM((8, DH), F32)],
-        compiler_params=params(32 * MIB),
+        compiler_params=params(60 * MIB),
+        cost_estimate=cost(4 * tokens * width * columns, 4 * tokens * width),
         name="keys_values",
     )(activations, w_key, w_value, log_decay)
 
@@ -208,7 +213,8 @@
         in_specs=[pl.BlockSpec((STEP, width), lambda i: (i, 0)), whole_block((width, columns))],
         out_specs=pl.BlockSpec((STEP, columns), lambda i: (i, 0)),
         out_shape=jax.ShapeDtypeStruct((tokens, columns), BF16),
-        compiler_params=params(24 * MIB),
+        compiler_params=params(60 * MIB),
+        cost_estimate=cost(2 * tokens * width * columns, 2 * tokens * width),
         name="queries",
     )(activations, w_query)
 
@@ -216,15 +222,17 @@
 def attend(first, count, query, key, value, before, wcol, wrow, arrivals):
     tokens, columns = query.shape
     heads, inner = columns // DH, STEP // BLOCK
-    row_block = pl.BlockSpec((STEP, columns), lambda i: (i, 0))
+    held = count if first % count == 0 else heads
+    group = first // held
+    row_block = pl.BlockSpec((STEP, held * DH), lambda i: (i, group))
     return pl.pallas_call(
-        functools.partial(attend_kernel, first, count, len(arrivals)),
+        functools.partial(attend_kernel, first, count, group * held, len(arrivals)),
         grid=(tokens // STEP,),
         in_specs=[
             row_block,
             row_block,
             row_block,
-            pl.BlockSpec((inner, heads, DH, DH), lambda i: (i, 0, 0, 0)),
+            pl.BlockSpec((inner, held, DH, DH), lambda i: (i, group, 0, 0)),
             pl.BlockSpec((inner, BLOCK, 8), lambda i: (i, 0, 0)),
             pl.BlockSpec((inner, 8, BLOCK), lambda i: (i, 0, 0)),
         ]
@@ -232,7 +240,8 @@
         out_specs=pl.BlockSpec((STEP, count * DH), lambda i: (i, 0)),
         out_shape=jax.ShapeDtypeStruct((tokens, count * DH), BF16),
         scratch_shapes=[pltpu.VMEM((count, DH, DH), F32)],
-        compiler_params=params(24 * MIB),
+        compiler_params=params(60 * MIB),
+        cost_estimate=cost(8 * tokens * BLOCK * count * DH, 8 * tokens * count * DH),
         name="attend",
     )(query, key, value, before, wcol, wrow, *arrivals)
 
@@ -249,11 +258,17 @@
 def gather_rows(w_out):
     half = w_out.shape[0] // 2
     piece = lax.dynamic_slice_in_dim(w_out, lax.axis_index("grp") * half, half, axis=0)
-    order = [0]
-    for bit in bits_of(lax.axis_size("head")):
+    return piece, swap(piece, "head", bits_of(lax.axis_size("head"))[0])
+
+
+def gather_rest(piece, received):
+    top, *others = bits_of(lax.axis_size("head"))
+    order = [0, top]
+    piece = jnp.concatenate([piece, received], axis=0)
+    for bit in others[:-1]:
         piece = jnp.concatenate([piece, swap(piece, "head", bit)], axis=0)
         order = order + [r ^ bit for r in order]
-    return piece, order
+    return piece, swap(piece, "head", others[-1]), order + [r ^ others[-1] for r in order]
 
 
 def gather_columns(piece):
@@ -297,29 +312,43 @@
     return pl.pallas_call(
         functools.partial(out_kernel, tuple(plan), order, bool(lead)),
         out_shape=jax.ShapeDtypeStruct((rows, width), dtype),
-        compiler_params=pltpu.CompilerParams(vmem_limit_bytes=40 * MIB),
+        compiler_params=pltpu.CompilerParams(vmem_limit_bytes=60 * MIB),
+        cost_estimate=cost(2 * rows * width * sources * count * DH, 4 * width * sources * count * DH),
         name="project_out",
     )(features, *lead, *operands)
+
+
+def after(value, *earlier):
+    return lax.optimization_barrier((value, *earlier))[0]
 
 
 def on_device(activations, w_query, w_key, w_value, w_out, log_decay):
     heads, tokens = log_decay.shape
     places, sources = lax.axis_size("seq"), lax.axis_size("head")
-    rows, order = gather_rows(w_out)
+    own, farthest = gather_rows(w_out)
     key, value, before, payload, wcol, wrow = keys_values(activations, w_key, w_value, log_decay)
+    payload, farthest = lax.optimization_barrier((payload, farthest))
     arrivals = [
         lax.ppermute(payload, "seq", [(i, i + r) for i in range(places - r)])
         for r in range(1, places)
     ]
-    query = queries(activations, w_query)
-    found = gather_columns(rows)
+    low, high, order = gather_rest(own, farthest)
+    query = queries(after(activations, low), w_query)
     chunks = CHUNKS if heads == 4 else ((0, heads),)
-    mixed = None
+    query, high = lax.optimization_barrier((query, high))
+    sends = []
     for first, last in chunks:
         normed = attend(first, last - first, query, key, value, before, wcol, wrow, arrivals)
-        features = lax.all_to_all(
-            normed.reshape(sources, tokens // sources, (last - first) * DH), "head", 0, 0
+        if not sends:
+            high = after(high, normed)
+        sends.append(
+            lax.all_to_all(
+                normed.reshape(sources, tokens // sources, (last - first) * DH), "head", 0, 0
+            )
         )
+    found = gather_columns(jnp.concatenate([low, high], axis=0))
+    mixed = None
+    for (first, last), features in zip(chunks, sends):
         dtype = BF16 if last == heads else F32
         mixed = project_out(features, found, order, first, last - first, heads, mixed, dtype)
     return mixed

time: 142 us -> 113 us (0.80)
  local copies, waits for them, and re-layouts: 28.8 us -> 6.65 us
  waiting for transfers between devices: 49.1 us -> 28.4 us
  Pallas kernels: 34.2 us -> 52 us
  other arithmetic: 3.12 us -> 1.15 us
  starting transfers between devices: 25.5 us -> 24 us
    ppermute x11, waiting for transfers between devices: 49.1 us -> 12.9 us  [swap(): return lax.ppermute(value, axis, [(i, i ^ bit) for i in range(count)])]
    unnamed x46 -> x22, local copies, waits for them, and re-layouts: 26.6 us -> 4.48 us
    all_to_all x2, waiting for transfers between devices: 0.01 us -> 15.5 us  [on_device(): lax.all_to_all(normed.reshape(sources, tokens // sources, (last - first)...]
    pallas_call x2, Pallas kernels: 8.44 us -> 13.5 us  [attend(): pl.pallas_call(functools.partial(attend_kernel, first, count, group * hel...]
    pallas_call x2, Pallas kernels: 9.52 us -> 14.1 us  [project_out(): pl.pallas_call(functools.partial(out_kernel, tuple(plan), order, bool(lea...]
    pallas_call x1, Pallas kernels: 11.1 us -> 15.6 us  [keys_values(): pl.pallas_call(kv_kernel, grid=(tokens // STEP,), in_specs=[pl.BlockSpec(...]
    pallas_call x1, Pallas kernels: 5.14 us -> 8.77 us  [queries(): pl.pallas_call(project_kernel, grid=(tokens // STEP,), in_specs=[pl.Block...]
    concatenate x2, other arithmetic: 3.12 us -> 1.15 us  [the longest x1 1.11 us: on_device(): found = gather_columns(jnp.concatenate([low, high], axis=0))]
  transfers between devices with their start and end apart: 16 -> 16, of which waited for: 4 -> 3; matrix products, arithmetic and copies ran while one was open for 4% -> 3% of each run, Pallas kernels for 13% -> 34%
where the time goes in v2:
time: 113 us; the launch traced here: 112 us
  Pallas kernels  52 us (46%)
  waiting for transfers between devices  28.4 us (25%)
  starting transfers between devices  24 us (21%)
  local copies, waits for them, and re-layouts  6.65 us (6%)
  other arithmetic  1.15 us (1%)
    pallas_call x1, Pallas kernels, keys_values(): pl.pallas_call(kv_kernel, grid=(tokens // STEP,), in_specs=[pl.BlockSpec(...  15.6 us
    all_to_all x2, waiting for transfers between devices, on_device(): lax.all_to_all(normed.reshape(sources, tokens // sources, (last - first)...  15.5 us
    pallas_call x2, Pallas kernels, project_out(): pl.pallas_call(functools.partial(out_kernel, tuple(plan), order, bool(lea...  14.1 us
    pallas_call x2, Pallas kernels, attend(): pl.pallas_call(functools.partial(attend_kernel, first, count, group * hel...  13.5 us
    ppermute x11, waiting for transfers between devices, swap(): return lax.ppermute(value, axis, [(i, i ^ bit) for i in range(count)])  12.9 us
    ppermute x11, starting transfers between devices, swap(): return lax.ppermute(value, axis, [(i, i ^ bit) for i in range(count)])  9.67 us
    pallas_call x1, Pallas kernels, queries(): pl.pallas_call(project_kernel, grid=(tokens // STEP,), in_specs=[pl.Block...  8.77 us
    all_to_all x2, starting transfers between devices, on_device(): lax.all_to_all(normed.reshape(sources, tokens // sources, (last - first)...  7.77 us
  transfers between devices with their start and end apart: 16, of which 3 were waited for; matrix products, arithmetic and copies ran while one was open for 3% of the time, Pallas kernels for 34%

profile of v2, /device:TPU:0, one launch (start us, length us, event | category | flops | bytes accessed | tf_op | source)
XLA Modules:
  0.0 112.5 jit_solution(18214698476033058239)
XLA Ops:
  0.0 1.0 copy-done
  1.1 4.1 %collective-permute-start = (bf16[256,512]{1,0:T(8,128)(2,1)S(1)}, bf16[256,512]{1,0:T(8,128)(2,1)S(1)}, u32[]{:S(2)}, u32[]{:S(2)}) collective-permute-start(bf16[256,512]{1,0:T(8,128)(2,1)S(1)} %constant_dynamic-slice_fusion), channel_id=1, source_target_pairs={{0,2},{1,3},{2,0},{3,1},{4,6},{5,7},{6,4},{7,5},{8,10},{9,11},{10,... | collective-permute-start | bytes 786440 | tf_op jit(solution)/shard_map/ppermute | solution.py:251
  5.2 15.6 %keys_values.1 = (bf16[2048,512]{1,0:T(8,128)(2,1)}, bf16[2048,512]{1,0:T(8,128)(2,1)}, f32[8,4,128,128]{3,2,1,0:T(8,128)}, bf16[4,144,128]{2,1,0:T(8,128)(2,1)}...) custom-call(bf16[2048,2048]{1,0:T(8,128)(2,1)} %act.2, bf16[2048,512]{1,0:T(8,128)(2,1)} %wk.1, bf16[2048,512]{1,0:T(8,128)(2,1)} %wv.1, ...), custom_call_target="tpu_custom_call" | custom-call | flops 8589934592 | bytes 16777216 | tf_op jit(solution)/shard_map/keys_values/pallas_call | solution.py:175
  20.8 1.6 %collective-permute-start.1 = (bf16[512,512]{1,0:T(8,128)(2,1)S(1)}, bf16[512,512]{1,0:T(8,128)(2,1)S(1)}, u32[]{:S(2)}, u32[]{:S(2)}) collective-permute-start(bf16[512,512]{1,0:T(8,128)(2,1)S(1)} %pad_maximum_fusion.1), channel_id=1, source_target_pairs={{0,1},{1,0},{2,3},{3,2},{4,5},{5,4},{6,7},{7,6},{8,9},{9,8},{10,11... | collective-permute-start | bytes 1572872 | tf_op jit(solution)/shard_map/ppermute | solution.py:251
  22.5 1.3 %collective-permute-start.2 = (bf16[4,144,128]{2,1,0:T(8,128)(2,1)}, bf16[4,144,128]{2,1,0:T(8,128)(2,1)S(1)}, u32[]{:S(2)}, u32[]{:S(2)}) collective-permute-start(bf16[4,144,128]{2,1,0:T(8,128)(2,1)} %get-tuple-element.26), channel_id=1, source_target_pairs={{0,4},{4,8},{8,12},{1,5},{5,9},{9,13},{2,6},{6,10},{10,14},{3,7},{... | collective-permute-start | bytes 442376 | tf_op jit(solution)/shard_map/ppermute | solution.py:332
  23.8 4.0 %collective-permute-start.3 = (bf16[4,144,128]{2,1,0:T(8,128)(2,1)}, bf16[4,144,128]{2,1,0:T(8,128)(2,1)S(1)}, u32[]{:S(2)}, u32[]{:S(2)}) collective-permute-start(bf16[4,144,128]{2,1,0:T(8,128)(2,1)} %get-tuple-element.26), channel_id=1, source_target_pairs={{0,8},{4,12},{1,9},{5,13},{2,10},{6,14},{3,11},{7,15},{16,24},{20,... | collective-permute-start | bytes 442376 | tf_op jit(solution)/shard_map/ppermute | solution.py:332
  27.8 1.3 %collective-permute-start.4 = (bf16[4,144,128]{2,1,0:T(8,128)(2,1)}, bf16[4,144,128]{2,1,0:T(8,128)(2,1)S(1)}, u32[]{:S(2)}, u32[]{:S(2)}) collective-permute-start(bf16[4,144,128]{2,1,0:T(8,128)(2,1)} %get-tuple-element.26), channel_id=1, source_target_pairs={{0,12},{1,13},{2,14},{3,15},{16,28},{17,29},{18,30},{19,31}} | collective-permute-start | bytes 442376 | tf_op jit(solution)/shard_map/ppermute | solution.py:332
  29.1 8.8 %queries.1.q = bf16[2048,512]{1,0:T(8,128)(2,1)} custom-call(bf16[2048,2048]{1,0:T(8,128)(2,1)} %act.2, bf16[2048,512]{1,0:T(8,128)(2,1)} %w.1), custom_call_target="tpu_custom_call" | custom-call | flops 4294967296 | bytes 8388608 | tf_op jit(solution)/shard_map/queries/pallas_call | solution.py:210
  38.7 6.7 %attend.3 = bf16[2048,256]{1,0:T(8,128)(2,1)} custom-call(bf16[2048,512]{1,0:T(8,128)(2,1)} %queries.1.q, bf16[2048,512]{1,0:T(8,128)(2,1)} %get-tuple-element.21.k, bf16[2048,512]{1,0:T(8,128)(2,1)} %get-tuple-element.22.v, f32[8,4,128,128]{3,2,1,0:T(8,128)} %get-tuple-element.23.before, f32[8,256,8]{2,1,0:T(8,128)} %get-tuple-element.24.wcol, ...), custom_call_target="tpu_custom_call" | custom-call | flops 1073741824 | bytes 4194304 | tf_op jit(solution)/shard_map/attend/pallas_call | solution.py:228
  45.5 3.5 %all-to-all-start.1 = ((bf16[4,512,256]{2,1,0:T(8,128)(2,1)}), bf16[4,512,256]{2,1,0:T(8,128)(2,1)S(1)}, u32[]{:S(2)}, u32[]{:S(2)}) async-start(bf16[4,512,256]{2,1,0:T(8,128)(2,1)} %bitcast.3), calls=%async_computation.1 | async-start | bytes 2097152 | tf_op jit(solution)/shard_map/all_to_all | solution.py:345
  49.0 1.1 pad_maximum_fusion.rest_0_
  50.2 1.5 %collective-permute-start.8 = (bf16[1024,512]{1,0:T(8,128)(2,1)S(1)}, bf16[1024,512]{1,0:T(8,128)(2,1)}, u32[]{:S(2)}, u32[]{:S(2)}) collective-permute-start(bf16[1024,512]{1,0:T(8,128)(2,1)S(1)} %pad_maximum_fusion.rest_0_), channel_id=1, source_target_pairs={{0,16},{16,0},{1,17},{17,1},{2,18},{18,2},{3,19},{19,3},{4,20},{20... | collective-permute-start | bytes 3145736 | tf_op jit(solution)/shard_map/ppermute | solution.py:251
  51.7 6.8 %attend.2 = bf16[2048,256]{1,0:T(8,128)(2,1)} custom-call(bf16[2048,512]{1,0:T(8,128)(2,1)} %queries.1.q, bf16[2048,512]{1,0:T(8,128)(2,1)} %get-tuple-element.21.k, bf16[2048,512]{1,0:T(8,128)(2,1)} %get-tuple-element.22.v, f32[8,4,128,128]{3,2,1,0:T(8,128)} %get-tuple-element.23.before, f32[8,256,8]{2,1,0:T(8,128)} %get-tuple-element.24.wcol, ...), custom_call_target="tpu_custom_call" | custom-call | flops 1073741824 | bytes 4194304 | tf_op jit(solution)/shard_map/attend/pallas_call | solution.py:228
  58.5 15.5 %all-to-all-done.1.features = bf16[4,512,256]{2,1,0:T(8,128)(2,1)S(1)} async-done(((bf16[4,512,256]{2,1,0:T(8,128)(2,1)}), bf16[4,512,256]{2,1,0:T(8,128)(2,1)S(1)}, u32[]{:S(2)}, u32[]{:S(2)}) %all-to-all-start.1) | async-done | bytes 1048608 | tf_op jit(solution)/shard_map/all_to_all | solution.py:345
  74.0 4.2 %all-to-all-start = ((bf16[4,512,256]{2,1,0:T(8,128)(2,1)}), bf16[4,512,256]{2,1,0:T(8,128)(2,1)}, u32[]{:S(2)}, u32[]{:S(2)}) async-start(bf16[4,512,256]{2,1,0:T(8,128)(2,1)} %bitcast.2), calls=%async_computation | async-start | bytes 2097152 | tf_op jit(solution)/shard_map/all_to_all | solution.py:345
  78.8 1.1 slice.8
  80.1 1.1 slice.9
  81.2 1.5 %collective-permute-start.11 = (bf16[512,512]{1,0:T(8,128)(2,1)S(1)}, bf16[512,512]{1,0:T(8,128)(2,1)}, u32[]{:S(2)}, u32[]{:S(2)}) collective-permute-start(bf16[512,512]{1,0:T(8,128)(2,1)S(1)} %slice.9), channel_id=1, source_target_pairs={{0,16},{16,0},{1,17},{17,1},{2,18},{18,2},{3,19},{19,3},{4,20},{20... | collective-permute-start | bytes 1572872 | tf_op jit(solution)/shard_map/ppermute | solution.py:251
  82.8 11.1 %collective-permute-done.10.rest_3_ = bf16[512,512]{1,0:T(8,128)(2,1)S(1)} collective-permute-done((bf16[512,512]{1,0:T(8,128)(2,1)S(1)}, bf16[512,512]{1,0:T(8,128)(2,1)S(1)}, u32[]{:S(2)}, u32[]{:S(2)}) %collective-permute-start.10) | collective-permute-done | bytes 524320 | tf_op jit(solution)/shard_map/ppermute | solution.py:251
  93.9 1.8 %collective-permute-done.11.rest_4_ = bf16[512,512]{1,0:T(8,128)(2,1)} collective-permute-done((bf16[512,512]{1,0:T(8,128)(2,1)S(1)}, bf16[512,512]{1,0:T(8,128)(2,1)}, u32[]{:S(2)}, u32[]{:S(2)}) %collective-permute-start.11) | collective-permute-done | bytes 524320 | tf_op jit(solution)/shard_map/ppermute | solution.py:251
  95.7 1.0 copy-done.3
  96.7 6.8 %project_out.2.rest_0_ = f32[512,2048]{1,0:T(8,128)} custom-call(bf16[4,512,256]{2,1,0:T(8,128)(2,1)} %copy-done.1, bf16[1024,512]{1,0:T(8,128)(2,1)} %copy-done.2, bf16[1024,512]{1,0:T(8,128)(2,1)} %copy-done.3, bf16[1024,512]{1,0:T(8,128)(2,1)} %collective-permute-done.6.rest_2_, bf16[1024,512]{1,0:T(8,128)(2,1)} %collective-permute-done.7.rest_3_), custom_call_target="tpu_custom_call" | custom-call | flops 2147483648 | bytes 8388608 | tf_op jit(solution)/shard_map/project_out/pallas_call | solution.py:312
  104.3 0.9 copy-done.9
  105.2 7.3 %project_out.3 = bf16[512,2048]{1,0:T(8,128)(2,1)} custom-call(bf16[4,512,256]{2,1,0:T(8,128)(2,1)} %all-to-all-done.features, f32[512,2048]{1,0:T(8,128)} %project_out.2.rest_0_, bf16[1024,512]{1,0:T(8,128)(2,1)} %collective-permute-done.8.rest_1_, bf16[1024,512]{1,0:T(8,128)(2,1)} %collective-permute-done.9.rest_2_, bf16[512,512]{1,0:T(8,128)(2,1)} %copy-done.7, ...), custom_call_target="tpu_custom_call" | custom-call | flops 2147483648 | bytes 8388608 | tf_op jit(solution)/shard_map/project_out/pallas_call | solution.py:312
  (41 shorter events, 2.6 us)
Async XLA Ops:
  0.0 1.0 copy-start
  1.1 19.7 %collective-permute-start = (bf16[256,512]{1,0:T(8,128)(2,1)S(1)}, bf16[256,512]{1,0:T(8,128)(2,1)S(1)}, u32[]{:S(2)}, u32[]{:S(2)}) collective-permute-start(bf16[256,512]{1,0:T(8,128)(2,1)S(1)} %constant_dynamic-slice_fusion), channel_id=1, source_target_pairs={{0,2},{1,3},{2,0},{3,1},{4,6},{5,7},{6,4},{7,5},{8,10},{9,11},{10,... | collective-permute-start | bytes 786440 | tf_op jit(solution)/shard_map/ppermute | solution.py:251
  20.8 17.0 %collective-permute-start.1 = (bf16[512,512]{1,0:T(8,128)(2,1)S(1)}, bf16[512,512]{1,0:T(8,128)(2,1)S(1)}, u32[]{:S(2)}, u32[]{:S(2)}) collective-permute-start(bf16[512,512]{1,0:T(8,128)(2,1)S(1)} %pad_maximum_fusion.1), channel_id=1, source_target_pairs={{0,1},{1,0},{2,3},{3,2},{4,5},{5,4},{6,7},{7,6},{8,9},{9,8},{10,11... | collective-permute-start | bytes 1572872 | tf_op jit(solution)/shard_map/ppermute | solution.py:251
  22.5 15.4 %collective-permute-start.2 = (bf16[4,144,128]{2,1,0:T(8,128)(2,1)}, bf16[4,144,128]{2,1,0:T(8,128)(2,1)S(1)}, u32[]{:S(2)}, u32[]{:S(2)}) collective-permute-start(bf16[4,144,128]{2,1,0:T(8,128)(2,1)} %get-tuple-element.26), channel_id=1, source_target_pairs={{0,4},{4,8},{8,12},{1,5},{5,9},{9,13},{2,6},{6,10},{10,14},{3,7},{... | collective-permute-start | bytes 442376 | tf_op jit(solution)/shard_map/ppermute | solution.py:332
  23.8 14.1 %collective-permute-start.3 = (bf16[4,144,128]{2,1,0:T(8,128)(2,1)}, bf16[4,144,128]{2,1,0:T(8,128)(2,1)S(1)}, u32[]{:S(2)}, u32[]{:S(2)}) collective-permute-start(bf16[4,144,128]{2,1,0:T(8,128)(2,1)} %get-tuple-element.26), channel_id=1, source_target_pairs={{0,8},{4,12},{1,9},{5,13},{2,10},{6,14},{3,11},{7,15},{16,24},{20,... | collective-permute-start | bytes 442376 | tf_op jit(solution)/shard_map/ppermute | solution.py:332
  27.8 10.1 %collective-permute-start.4 = (bf16[4,144,128]{2,1,0:T(8,128)(2,1)}, bf16[4,144,128]{2,1,0:T(8,128)(2,1)S(1)}, u32[]{:S(2)}, u32[]{:S(2)}) collective-permute-start(bf16[4,144,128]{2,1,0:T(8,128)(2,1)} %get-tuple-element.26), channel_id=1, source_target_pairs={{0,12},{1,13},{2,14},{3,15},{16,28},{17,29},{18,30},{19,31}} | collective-permute-start | bytes 442376 | tf_op jit(solution)/shard_map/ppermute | solution.py:332
  37.9 7.6 %copy-start.10 = (bf16[512,512]{1,0:T(8,128)(2,1)}, bf16[512,512]{1,0:T(8,128)(2,1)S(1)}, u32[]{:S(2)}) copy-start(bf16[512,512]{1,0:T(8,128)(2,1)S(1)} %collective-permute-done.1) | copy-start | bytes 1572868
  45.5 28.5 %all-to-all-start.1 = ((bf16[4,512,256]{2,1,0:T(8,128)(2,1)}), bf16[4,512,256]{2,1,0:T(8,128)(2,1)S(1)}, u32[]{:S(2)}, u32[]{:S(2)}) async-start(bf16[4,512,256]{2,1,0:T(8,128)(2,1)} %bitcast.3), calls=%async_computation.1 | async-start | bytes 2097152 | tf_op jit(solution)/shard_map/all_to_all | solution.py:345
  50.1 28.1 %copy-start.2 = (bf16[1024,512]{1,0:T(8,128)(2,1)}, bf16[1024,512]{1,0:T(8,128)(2,1)S(1)}, u32[]{:S(2)}) copy-start(bf16[1024,512]{1,0:T(8,128)(2,1)S(1)} %pad_maximum_fusion.rest_0_) | copy-start | bytes 3145732
  50.1 28.2 %collective-permute-start.6 = (bf16[1024,512]{1,0:T(8,128)(2,1)S(1)}, bf16[1024,512]{1,0:T(8,128)(2,1)}, u32[]{:S(2)}, u32[]{:S(2)}) collective-permute-start(bf16[1024,512]{1,0:T(8,128)(2,1)S(1)} %pad_maximum_fusion.rest_0_), channel_id=1, source_target_pairs={{0,8},{4,12},{8,0},{12,4},{1,9},{5,13},{9,1},{13,5},{2,10},{6,14},... | collective-permute-start | bytes 3145736 | tf_op jit(solution)/shard_map/ppermute | solution.py:251
  50.2 28.6 %collective-permute-start.8 = (bf16[1024,512]{1,0:T(8,128)(2,1)S(1)}, bf16[1024,512]{1,0:T(8,128)(2,1)}, u32[]{:S(2)}, u32[]{:S(2)}) collective-permute-start(bf16[1024,512]{1,0:T(8,128)(2,1)S(1)} %pad_maximum_fusion.rest_0_), channel_id=1, source_target_pairs={{0,16},{16,0},{1,17},{17,1},{2,18},{18,2},{3,19},{19,3},{4,20},{20... | collective-permute-start | bytes 3145736 | tf_op jit(solution)/shard_map/ppermute | solution.py:251
  74.0 7.2 %copy-start.1 = (bf16[4,512,256]{2,1,0:T(8,128)(2,1)}, bf16[4,512,256]{2,1,0:T(8,128)(2,1)S(1)}, u32[]{:S(2)}) copy-start(bf16[4,512,256]{2,1,0:T(8,128)(2,1)S(1)} %all-to-all-done.1.features) | copy-start | bytes 3145732
  74.0 29.5 %all-to-all-start = ((bf16[4,512,256]{2,1,0:T(8,128)(2,1)}), bf16[4,512,256]{2,1,0:T(8,128)(2,1)}, u32[]{:S(2)}, u32[]{:S(2)}) async-start(bf16[4,512,256]{2,1,0:T(8,128)(2,1)} %bitcast.2), calls=%async_computation | async-start | bytes 2097152 | tf_op jit(solution)/shard_map/all_to_all | solution.py:345
  78.2 17.4 %collective-permute-start.5 = (bf16[1024,512]{1,0:T(8,128)(2,1)S(1)}, bf16[1024,512]{1,0:T(8,128)(2,1)S(1)}, u32[]{:S(2)}, u32[]{:S(2)}) collective-permute-start(bf16[1024,512]{1,0:T(8,128)(2,1)S(1)} %pad_maximum_fusion.rest_0_), channel_id=1, source_target_pairs={{0,4},{4,0},{8,12},{12,8},{1,5},{5,1},{9,13},{13,9},{2,6},{6,2},{1... | collective-permute-start | bytes 3145736 | tf_op jit(solution)/shard_map/ppermute | solution.py:251
  78.3 18.3 %collective-permute-start.7 = (bf16[1024,512]{1,0:T(8,128)(2,1)}, bf16[1024,512]{1,0:T(8,128)(2,1)}, u32[]{:S(2)}, u32[]{:S(2)}) collective-permute-start(bf16[1024,512]{1,0:T(8,128)(2,1)} %collective-permute-done.6.rest_2_), channel_id=1, source_target_pairs={{0,4},{4,0},{8,12},{12,8},{1,5},{5,1},{9,13},{13,9},{2,6},{6,2},{1... | collective-permute-start | bytes 3145736 | tf_op jit(solution)/shard_map/ppermute | solution.py:251
  79.9 14.0 %collective-permute-start.10 = (bf16[512,512]{1,0:T(8,128)(2,1)S(1)}, bf16[512,512]{1,0:T(8,128)(2,1)S(1)}, u32[]{:S(2)}, u32[]{:S(2)}) collective-permute-start(bf16[512,512]{1,0:T(8,128)(2,1)S(1)} %slice.8), channel_id=1, source_target_pairs={{0,8},{4,12},{8,0},{12,4},{1,9},{5,13},{9,1},{13,5},{2,10},{6,14},... | collective-permute-start | bytes 1572872 | tf_op jit(solution)/shard_map/ppermute | solution.py:251
  80.0 23.5 %collective-permute-start.9 = (bf16[1024,512]{1,0:T(8,128)(2,1)}, bf16[1024,512]{1,0:T(8,128)(2,1)}, u32[]{:S(2)}, u32[]{:S(2)}) collective-permute-start(bf16[1024,512]{1,0:T(8,128)(2,1)} %collective-permute-done.8.rest_1_), channel_id=1, source_target_pairs={{0,4},{4,0},{8,12},{12,8},{1,5},{5,1},{9,13},{13,9},{2,6},{6,2},{1... | collective-permute-start | bytes 3145736 | tf_op jit(solution)/shard_map/ppermute | solution.py:251
  81.2 14.4 %collective-permute-start.11 = (bf16[512,512]{1,0:T(8,128)(2,1)S(1)}, bf16[512,512]{1,0:T(8,128)(2,1)}, u32[]{:S(2)}, u32[]{:S(2)}) collective-permute-start(bf16[512,512]{1,0:T(8,128)(2,1)S(1)} %slice.9), channel_id=1, source_target_pairs={{0,16},{16,0},{1,17},{17,1},{2,18},{18,2},{3,19},{19,3},{4,20},{20... | collective-permute-start | bytes 1572872 | tf_op jit(solution)/shard_map/ppermute | solution.py:251
  93.9 9.6 %copy-start.7 = (bf16[512,512]{1,0:T(8,128)(2,1)}, bf16[512,512]{1,0:T(8,128)(2,1)S(1)}, u32[]{:S(2)}) copy-start(bf16[512,512]{1,0:T(8,128)(2,1)S(1)} %collective-permute-done.10.rest_3_) | copy-start | bytes 1572868
  93.9 9.6 %collective-permute-start.12 = (bf16[512,512]{1,0:T(8,128)(2,1)S(1)}, bf16[512,512]{1,0:T(8,128)(2,1)S(1)}, u32[]{:S(2)}, u32[]{:S(2)}) collective-permute-start(bf16[512,512]{1,0:T(8,128)(2,1)S(1)} %collective-permute-done.10.rest_3_), channel_id=1, source_target_pairs={{0,4},{4,0},{8,12},{12,8},{1,5},{5,1},{9,13},{13,9},{2,6},{6,2},{1... | collective-permute-start | bytes 1572872 | tf_op jit(solution)/shard_map/ppermute | solution.py:251
  95.7 7.9 %collective-permute-start.13 = (bf16[512,512]{1,0:T(8,128)(2,1)}, bf16[512,512]{1,0:T(8,128)(2,1)S(1)}, u32[]{:S(2)}, u32[]{:S(2)}) collective-permute-start(bf16[512,512]{1,0:T(8,128)(2,1)} %collective-permute-done.11.rest_4_), channel_id=1, source_target_pairs={{0,4},{4,0},{8,12},{12,8},{1,5},{5,1},{9,13},{13,9},{2,6},{6,2},{1... | collective-permute-start | bytes 1572872 | tf_op jit(solution)/shard_map/ppermute | solution.py:251
  95.7 1.0 copy-start.3
  103.5 0.8 copy-start.8
  104.3 0.9 copy-start.9
  (3 other events, 2.3 us)

commit v3 on v0

v3 whole, which is shorter than its diff:
```python
import functools

import jax
import jax.numpy as jnp
from jax import lax
from jax.experimental import pallas as pl
from jax.experimental.pallas import tpu as pltpu
from jax.sharding import PartitionSpec as P

DH = 128
BLOCK = 256
STEP = 512
EXTRA = 16
F32 = jnp.float32
BF16 = jnp.bfloat16
HIGHEST = lax.Precision.HIGHEST
MIB = 1 << 20


def dot(a, b, dims=((1,), (0,)), precision=None):
    return lax.dot_general(a, b, (dims, ((), ())), precision=precision, preferred_element_type=F32)


def relative_half(part, width):
    start = lax.rem(part + lax.axis_index("grp"), 2) * width
    return pl.ds(pl.multiple_of(start, width), width)


def kv_kernel(act, wk, wv, wq, decay, act_out, wq_out, kv_out, before, payload, wcol, wrow, reach,
              held, logs, state, sems):
    heads, tokens = decay.shape
    blocks, steps = tokens // BLOCK, tokens // STEP
    half = heads // 2
    wide = half * DH
    columns = heads * DH

    def load_rows(step):
        rows = pl.ds(pl.multiple_of(step * STEP, STEP), STEP)
        return pltpu.make_async_copy(act.at[rows], act_out.at[rows], sems.at[step])

    def load_half(source, target, part, lane, at):
        return pltpu.make_async_copy(
            source.at[:, relative_half(part, wide)],
            target.at[:, pl.ds(lane, wide)],
            sems.at[steps + at],
        )

    load_logs = pltpu.make_async_copy(decay, logs, sems.at[steps + 6])
    weights = [
        load_half(source, held, part, at * wide, at)
        for at, (source, part) in enumerate([(wk, 0), (wk, 1), (wv, 0), (wv, 1)])
    ]
    q_loads = [load_half(wq, wq_out, part, part * wide, 4 + part) for part in range(2)]
    queue = [load_rows(0)] + weights + [load_rows(1)]
    for copy in [load_logs] + queue[:3]:
        copy.start()

    load_logs.wait()
    rates = logs[...]
    swapped = jnp.concatenate([rates[half:], rates[:half]], axis=0)
    rates = jnp.where(lax.axis_index("grp") == 0, rates, swapped)
    rates = jnp.concatenate([rates, jnp.zeros((8 - heads, tokens), F32)], axis=0)
    stacked = jnp.concatenate([rates[:, n * BLOCK : (n + 1) * BLOCK] for n in range(blocks)], axis=0)
    upper = (
        lax.broadcasted_iota(jnp.int32, (BLOCK, BLOCK), 0)
        <= lax.broadcasted_iota(jnp.int32, (BLOCK, BLOCK), 1)
    ).astype(F32)
    within = dot(stacked, upper, precision=HIGHEST)
    total = jnp.zeros((8, 1), F32)
    for n in range(blocks):
        rows = within[n * 8 : (n + 1) * 8]
        wrow[n] = rows
        wcol[n] = rows.T
        reach[n] = jnp.broadcast_to(jnp.exp(total), (8, DH))
        total = total + rows[:, BLOCK - 1 :]
    factor = jnp.broadcast_to(jnp.exp(total), (8, DH))
    state[...] = jnp.zeros_like(state)

    def advance(step, first):
        start = pl.multiple_of(step * STEP, STEP)
        rows = pl.ds(start, STEP)
        if first:
            for at in range(5):
                queue[at].wait()
                if at + 3 < len(queue):
                    queue[at + 3].start()
                if at > 0:
                    lanes = slice((at - 1) * wide, at * wide)
                    kv_out[rows, lanes] = dot(act_out[rows], held[:, lanes]).astype(BF16)
        else:
            load_rows(step).wait()

            @pl.when(step + 1 < steps)
            def _():
                load_rows(step + 1).start()

            kv_out[rows] = dot(act_out[rows], held[...]).astype(BF16)
        for b in range(STEP // BLOCK):
            n = step * (STEP // BLOCK) + b
            cols = wcol[n]
            last = cols[BLOCK - 1 :]
            carry = jnp.exp(last - cols)
            shrink = jnp.exp(last)
            block = pl.ds(pl.multiple_of(start + b * BLOCK, BLOCK), BLOCK)
            for h in range(heads):
                k_b = kv_out[block, h * DH : (h + 1) * DH].astype(F32) * carry[:, h : h + 1]
                v_b = kv_out[block, columns + h * DH : columns + (h + 1) * DH]
                update = dot(k_b.astype(BF16), v_b, ((0,), (0,)))
                old = state[h]
                before[n, h] = old
                state[h] = shrink[:, h : h + 1] * old + update

    advance(0, True)
    for copy in q_loads:
        copy.start()

    @pl.loop(1, steps)
    def _(step):
        advance(step, False)

    for h in range(heads):
        payload[h, :DH] = state[h].astype(BF16)
        whole = jnp.broadcast_to(factor[h : h + 1], (EXTRA, DH))
        high = whole.astype(BF16).astype(F32)
        first = lax.broadcasted_iota(jnp.int32, (EXTRA, DH), 0) < EXTRA // 2
        payload[h, DH:] = jnp.where(first, high, whole - high).astype(BF16)
    for copy in q_loads:
        copy.wait()


def project_kernel(act, w, out):
    for step in range(act.shape[0] // STEP):
        rows = pl.ds(step * STEP, STEP)
        out[rows] = dot(act[rows], w[...]).astype(BF16)


def incoming_state(arrivals, h):
    place = lax.axis_index("seq")
    sources = [lax.bitwise_xor(place, r + 1) for r in range(len(arrivals))]
    reaches = []
    for piece in arrivals:
        extra = piece[h, DH:].astype(F32)
        reaches.append(extra[:1] + extra[EXTRA // 2 : EXTRA // 2 + 1])
    total = jnp.zeros((DH, DH), F32)
    for source, piece in zip(sources, arrivals):
        weight = jnp.where(source < place, jnp.ones((1, DH), F32), 0.0)
        for other, reach in zip(sources, reaches):
            between = jnp.logical_and(other > source, other < place)
            weight = weight * jnp.where(between, reach, 1.0)
        total = total + weight * piece[h, :DH].astype(F32)
    return total


def attend_kernel(received, q, kv, before, wcol, wrow, reach, *rest):
    arrivals, (out, held, sems) = rest[:received], rest[received:]
    sources, share, columns = out.shape
    heads = columns // DH

    def send(target):
        return pltpu.make_async_copy(held.at[target], out.at[target], sems.at[target])

    causal = lax.broadcasted_iota(jnp.int32, (BLOCK, BLOCK), 0) >= lax.broadcasted_iota(
        jnp.int32, (BLOCK, BLOCK), 1
    )
    prefix = [incoming_state(arrivals, h) for h in range(heads)]

    @pl.loop(0, sources)
    def _(target):
        for b in range(share // BLOCK):
            n = target * (share // BLOCK) + b
            rows = pl.ds(pl.multiple_of(n * BLOCK, BLOCK), BLOCK)
            cols = wcol[n]
            grown = jnp.exp(cols)
            reached_here = reach[n]
            for h in range(heads):
                lanes = slice(h * DH, (h + 1) * DH)
                q_b, k_b = q[rows, lanes], kv[rows, lanes]
                v_b = kv[rows, columns + h * DH : columns + (h + 1) * DH]
                spread = cols[:, h : h + 1] - wrow[n, h : h + 1]
                mask = jnp.exp(jnp.where(causal, jnp.minimum(spread, 0.0), -1e30))
                scores = (dot(q_b, k_b, ((1,), (1,))) * mask).astype(BF16)
                reached = (q_b.astype(F32) * grown[:, h : h + 1]).astype(BF16)
                incoming = (before[n, h] + reached_here[h : h + 1] * prefix[h]).astype(BF16)
                attended = dot(scores, v_b) + dot(reached, incoming)
                mean = jnp.mean(attended * attended, axis=1, keepdims=True)
                normed = (attended * lax.rsqrt(mean + 1e-5)).astype(BF16)
                held[target, b * BLOCK : (b + 1) * BLOCK, lanes] = normed
        send(target).start()

    for target in range(sources):
        send(target).wait()


def out_kernel(plan, features, *rest):
    weights, (out, held, sems) = rest[:-3], rest[-3:]
    mine, place = lax.axis_index("head"), lax.axis_index("seq")
    half = features.shape[2] // 2

    def load(slot, at, begin):
        rows = weights[at].shape[0]
        return pltpu.make_async_copy(weights[at], held.at[slot, pl.ds(begin, rows)], sems.at[at])

    def loads(at):
        offset, pieces, products = plan[at]
        return [load(at, piece, begin) for piece, begin in pieces]

    for at in range(len(plan)):
        if at < 2:
            for copy in loads(at):
                copy.start()
    for at, (offset, pieces, products) in enumerate(plan):
        for copy in loads(at):
            copy.wait()
        if at + 2 < len(plan):
            for copy in loads(at + 2):
                copy.start()
        total = None
        for source, lane, row in products:
            left = features[lax.bitwise_xor(mine, source), :, lane : lane + half]
            term = dot(left, held[at, row : row + half])
            total = term if total is None else total + term
        width = total.shape[1]
        columns = pl.ds(pl.multiple_of(lax.bitwise_xor(place, offset) * width, width), width)
        out[:, columns] = total.astype(out.dtype)


def cost(flops, moved):
    return pl.CostEstimate(flops=flops, bytes_accessed=moved, transcendentals=0)


def in_hbm():
    return pl.BlockSpec(memory_space=pltpu.HBM)


def stay_in_hbm(*values):
    return [pltpu.with_memory_space_constraint(value, pltpu.HBM) for value in values]


def in_vmem():
    return pl.BlockSpec(memory_space=pltpu.VMEM)


def keys_values(activations, w_key, w_value, w_query, log_decay):
    tokens, width = activations.shape
    heads = log_decay.shape[0]
    columns, blocks = heads * DH, tokens // BLOCK
    shapes = [
        ((tokens, width), BF16),
        ((width, columns), BF16),
        ((tokens, 2 * columns), BF16),
        ((blocks, heads, DH, DH), F32),
        ((heads, DH + EXTRA, DH), BF16),
        ((blocks, BLOCK, 8), F32),
        ((blocks, 8, BLOCK), F32),
        ((blocks, 8, DH), F32),
    ]
    return pl.pallas_call(
        kv_kernel,
        in_specs=[in_hbm()] * 5,
        out_specs=[in_vmem()] * len(shapes),
        out_shape=[pltpu.VMEM(*shape) for shape in shapes],
        scratch_shapes=[
            pltpu.VMEM((width, 2 * columns), BF16),
            pltpu.VMEM((heads, tokens), F32),
            pltpu.VMEM((heads, DH, DH), F32),
            pltpu.SemaphoreType.DMA((tokens // STEP + 7,)),
        ],
        compiler_params=pltpu.CompilerParams(vmem_limit_bytes=16 * MIB),
        cost_estimate=cost(4 * tokens * width * columns, 4 * tokens * width),
        name="keys_values",
    )(*stay_in_hbm(activations, w_key, w_value, w_query, log_decay))


def queries(activations, w_query):
    tokens, width = activations.shape
    columns = w_query.shape[1]
    return pl.pallas_call(
        project_kernel,
        in_specs=[in_vmem()] * 2,
        out_specs=in_vmem(),
        out_shape=pltpu.VMEM((tokens, columns), BF16),
        compiler_params=pltpu.CompilerParams(vmem_limit_bytes=16 * MIB),
        cost_estimate=cost(2 * tokens * width * columns, 2 * tokens * width),
        name="queries",
    )(activations, w_query)


def attend(sources, query, *rest):
    received = len(rest) - 5
    tokens, columns = query.shape
    shares = (sources, tokens // sources, columns)
    return pl.pallas_call(
        functools.partial(attend_kernel, received),
        in_specs=[in_vmem()] * (len(rest) + 1),
        out_specs=in_hbm(),
        out_shape=pltpu.HBM(shares, BF16),
        scratch_shapes=[pltpu.VMEM(shares, BF16), pltpu.SemaphoreType.DMA((sources,))],
        compiler_params=pltpu.CompilerParams(vmem_limit_bytes=16 * MIB),
        cost_estimate=cost(20 * tokens * BLOCK * columns, 8 * tokens * columns),
        name="attend",
    )(query, *rest)


def swap(value, axis, bit):
    count = lax.axis_size(axis)
    return lax.ppermute(value, axis, [(i, i ^ bit) for i in range(count)])


def bits_of(count):
    return [1 << b for b in reversed(range(count.bit_length() - 1))]


def gather_rows(w_out):
    half = w_out.shape[0] // 2
    piece = lax.dynamic_slice_in_dim(w_out, lax.axis_index("grp") * half, half, axis=0)
    return piece, swap(piece, "head", bits_of(lax.axis_size("head"))[0])


def gather_rest(piece, received):
    top, *others = bits_of(lax.axis_size("head"))
    order = [0, top]
    piece = jnp.concatenate([piece, received], axis=0)
    for bit in others[:-1]:
        piece = jnp.concatenate([piece, swap(piece, "head", bit)], axis=0)
        order = order + [r ^ bit for r in order]
    return piece, swap(piece, "head", others[-1]), order + [r ^ others[-1] for r in order]


def gather_columns(piece):
    middle = piece.shape[0] // 2
    across, beside = swap(piece, "seq", 2), swap(piece, "grp", 1)
    corner = [swap(beside[:middle], "seq", 2), swap(across[middle:], "grp", 1)]
    found = {(0, 0): [piece], (0, 2): [across], (1, 0): [beside], (1, 2): corner}
    for bit in bits_of(lax.axis_size("seq"))[:-2]:
        found.update(
            {
                (g, s ^ bit): [swap(part, "seq", bit) for part in parts]
                for (g, s), parts in list(found.items())
            }
        )
    found.update(
        {(g, s ^ 1): [swap(part, "seq", 1) for part in parts] for (g, s), parts in found.items()}
    )
    return found


def project_out(features, found, order):
    sources, rows, columns = features.shape
    half = columns // 2
    operands, plan = [], []
    for offset in sorted({s for _, s in found}):
        pieces, products, begin = [], [], 0
        for g in range(2):
            for r in order:
                products.append((r, g * half, begin + order.index(r) * half))
            for part in found[(g, offset)]:
                pieces.append((len(operands), begin))
                operands.append(part)
                begin += part.shape[0]
        plan.append((offset, tuple(pieces), tuple(products)))
    width = operands[0].shape[1]
    return pl.pallas_call(
        functools.partial(out_kernel, tuple(plan)),
        out_shape=jax.ShapeDtypeStruct((rows, len(plan) * width), BF16),
        in_specs=[in_vmem()] + [in_hbm()] * len(operands),
        out_specs=in_vmem(),
        scratch_shapes=[
            pltpu.VMEM((len(plan), sources * columns, width), BF16),
            pltpu.SemaphoreType.DMA((len(operands),)),
        ],
        compiler_params=pltpu.CompilerParams(vmem_limit_bytes=24 * MIB),
        cost_estimate=cost(2 * rows * sources * columns * width * len(plan), 8 * MIB),
        name="project_out",
    )(features, *stay_in_hbm(*operands))


def after(value, *earlier):
    return lax.optimization_barrier((value, *earlier))[0]


def on_device(activations, w_query, w_key, w_value, w_out, log_decay):
    heads, tokens = log_decay.shape
    places, sources = lax.axis_size("seq"), lax.axis_size("head")
    own, farthest = gather_rows(w_out)
    rows, w_query, kv, before, payload, wcol, wrow, reach = keys_values(
        activations, w_key, w_value, w_query, log_decay
    )
    payload, farthest = lax.optimization_barrier((payload, farthest))
    arrivals = [swap(payload, "seq", r) for r in range(1, places)]
    low, high, order = gather_rest(own, farthest)
    query = queries(after(rows, low), w_query)
    normed = attend(sources, query, kv, before, wcol, wrow, reach, *arrivals)
    normed, high = lax.optimization_barrier((normed, high))
    features = lax.all_to_all(normed, "head", 0, 0)
    found = gather_columns(jnp.concatenate([low, high], axis=0))
    return project_out(features, found, order)


def solution(mesh):
    return jax.shard_map(
        on_device,
        mesh=mesh,
        in_specs=(
            P(("grp", "seq"), None),
            P(None, "head"),
            P(None, "head"),
            P(None, "head"),
            P("head", "seq"),
            P("head", ("grp", "seq")),
        ),
        out_specs=P(("grp", "seq", "head"), None),
        check_vma=False,
    )
```

time: 214 us -> 102 us (0.48)
  matrix products: 71.1 us -> 0 us
  blocking collectives: 60.5 us -> 0 us
  Pallas kernels: 0 us -> 38.7 us
  waiting for transfers between devices: 1.4 us -> 40 us
  local copies, waits for them, and re-layouts: 41.4 us -> 2.94 us
  other arithmetic: 24.2 us -> 1.15 us
  starting transfers between devices: 0.08 us -> 18.4 us
  between operations: 14 us -> 0.33 us
    dot_general x9 -> x0, matrix products: 71.1 us -> none  [the longest x1 10.7 us: on_device(): jnp.dot(activations, w_value, preferred_element_type=jnp.float32)]
    all_to_all x1 -> x0, blocking collectives: 52.1 us -> none  [on_device(): lax.all_to_all(normed, 'head', split_axis=0, concat_axis=1, tiled=True)]
    pallas_call x0 -> x4, Pallas kernels: none -> 38.7 us  [the longest x1 15.5 us: keys_values(): pl.pallas_call(kv_kernel, in_specs=[in_hbm()] * 5, out_specs=[in_vmem()]...]
    ppermute x0 -> x14, waiting for transfers between devices: none -> 36.7 us  [swap(): return lax.ppermute(value, axis, [(i, i ^ bit) for i in range(count)])]
    reshape x7 -> x0, local copies, waits for them, and re-layouts: 19.6 us -> none  [the longest x2 6.8 us: on_device(): key_blocks = key_proj.reshape(blocks, BLOCK, heads_here, DH)]
    ppermute x0 -> x14, starting transfers between devices: none -> 14.6 us  [swap(): return lax.ppermute(value, axis, [(i, i ^ bit) for i in range(count)])]
    mul x2 -> x0, local copies, waits for them, and re-layouts: 9.33 us -> none  [on_device(): attended * lax.rsqrt(jnp.mean(attended * attended, axis=-1, keepdims=True...]
    unnamed x1 -> x0, blocking collectives: 8.48 us -> none
  transfers between devices with their start and end apart: 3 -> 15, of which waited for: 0 -> 7; matrix products, arithmetic and copies ran while one was open for 59% -> 1% of each run, Pallas kernels for 0% -> 30%
where the time goes in v3:
time: 102 us
  waiting for transfers between devices  40 us (39%)
  Pallas kernels  38.7 us (38%)
  starting transfers between devices  18.4 us (18%)
  local copies, waits for them, and re-layouts  2.94 us (3%)
  other arithmetic  1.15 us (1%)
    ppermute x14, waiting for transfers between devices, swap(): return lax.ppermute(value, axis, [(i, i ^ bit) for i in range(count)])  36.7 us
    pallas_call x1, Pallas kernels, keys_values(): pl.pallas_call(kv_kernel, in_specs=[in_hbm()] * 5, out_specs=[in_vmem()]...  15.5 us
    ppermute x14, starting transfers between devices, swap(): return lax.ppermute(value, axis, [(i, i ^ bit) for i in range(count)])  14.6 us
    pallas_call x1, Pallas kernels, attend(): pl.pallas_call(functools.partial(attend_kernel, received), in_specs=[in_v...  10.7 us
    pallas_call x1, Pallas kernels, project_out(): pl.pallas_call(functools.partial(out_kernel, tuple(plan)), out_shape=jax....  7.95 us
    pallas_call x1, Pallas kernels, queries(): pl.pallas_call(project_kernel, in_specs=[in_vmem()] * 2, out_specs=in_vme...  4.48 us
    all_to_all x1, starting transfers between devices, on_device(): features = lax.all_to_all(normed, 'head', 0, 0)  3.8 us
    all_to_all x1, waiting for transfers between devices, on_device(): features = lax.all_to_all(normed, 'head', 0, 0)  3.32 us
  transfers between devices with their start and end apart: 15, of which 7 were waited for; matrix products, arithmetic and copies ran while one was open for 1% of the time, Pallas kernels for 30%

profile of v3, /device:TPU:0, one launch (start us, length us, event | category | flops | bytes accessed | tf_op | source)
XLA Modules:
  0.0 101.5 jit_solution(16402550142949727482)
XLA Ops:
  0.0 1.0 %copy-done = bf16[512,512]{1,0:T(8,128)(2,1)S(1)} copy-done((bf16[512,512]{1,0:T(8,128)(2,1)S(1)}, bf16[512,512]{1,0:T(8,128)(2,1)}, u32[]{:S(2)}) %copy-start) | copy-done | bytes 524312
  1.1 4.1 %collective-permute-start = (bf16[256,512]{1,0:T(8,128)(2,1)S(1)}, bf16[256,512]{1,0:T(8,128)(2,1)S(1)}, u32[]{:S(2)}, u32[]{:S(2)}) collective-permute-start(bf16[256,512]{1,0:T(8,128)(2,1)S(1)} %constant_dynamic-slice_fusion), channel_id=1, source_target_pairs={{0,2},{1,3},{2,0},{3,1},{4,6},{5,7},{6,4},{7,5},{8,10},{9,11},{10,... | collective-permute-start | bytes 786440 | tf_op jit(solution)/shard_map/ppermute | solution.py:306
  5.2 15.5 %keys_values.1 = (bf16[2048,2048]{1,0:T(8,128)(2,1)S(1)}, bf16[2048,512]{1,0:T(8,128)(2,1)S(1)}, bf16[2048,1024]{1,0:T(8,128)(2,1)S(1)}, f32[8,4,128,128]{3,2,1,...) custom-call(bf16[2048,2048]{1,0:T(8,128)(2,1)} %act.1, ...), custom_call_target="tpu_custom_call" | custom-call | flops 8589934592 | bytes 16777216 | tf_op jit(solution)/shard_map/keys_values/pallas_call | solution.py:257
  20.8 1.6 %collective-permute-start.2 = (bf16[4,144,128]{2,1,0:T(8,128)(2,1)S(1)}, bf16[4,144,128]{2,1,0:T(8,128)(2,1)S(1)}, u32[]{:S(2)}, u32[]{:S(2)}) collective-permute-start(bf16[4,144,128]{2,1,0:T(8,128)(2,1)S(1)} %get-tuple-element.28), channel_id=1, source_target_pairs={{0,8},{4,12},{8,0},{12,4},{1,9},{5,13},{9,1},{13,5},{2,10},{6,14},... | collective-permute-start | bytes 442376 | tf_op jit(solution)/shard_map/ppermute | solution.py:306
  22.7 1.6 %collective-permute-start.4 = (bf16[512,512]{1,0:T(8,128)(2,1)S(1)}, bf16[512,512]{1,0:T(8,128)(2,1)}, u32[]{:S(2)}, u32[]{:S(2)}) collective-permute-start(bf16[512,512]{1,0:T(8,128)(2,1)S(1)} %pad_maximum_fusion.1), channel_id=1, source_target_pairs={{0,1},{1,0},{2,3},{3,2},{4,5},{5,4},{6,7},{7,6},{8,9},{9,8},{10,11... | collective-permute-start | bytes 1572872 | tf_op jit(solution)/shard_map/ppermute | solution.py:306
  24.3 4.5 %queries.1.q = bf16[2048,512]{1,0:T(8,128)(2,1)S(1)} custom-call(bf16[2048,2048]{1,0:T(8,128)(2,1)S(1)} %get-tuple-element.21.act, bf16[2048,512]{1,0:T(8,128)(2,1)S(1)} %get-tuple-element.22.w), custom_call_target="tpu_custom_call" | custom-call | flops 4294967296 | bytes 8388608 | tf_op jit(solution)/shard_map/queries/pallas_call | solution.py:277
  28.8 0.9 collective-permute-done.3.rest_2_
  29.8 10.7 %attend.1 = bf16[4,512,512]{2,1,0:T(8,128)(2,1)} custom-call(bf16[2048,512]{1,0:T(8,128)(2,1)S(1)} %queries.1.q, bf16[2048,1024]{1,0:T(8,128)(2,1)S(1)} %get-tuple-element.23.kv, f32[8,4,128,128]{3,2,1,0:T(8,128)S(1)} %get-tuple-element.24.before, f32[8,256,8]{2,1,0:T(8,128)S(1)} %get-tuple-element.25.wcol, f32[8,8,256]{2,1,0:T(8,128)S(1)} %get-tuple-element.26.wrow, ...), custom_call_target="tpu_custom_call" | custom-call | flops 5368709120 | bytes 8388608 | tf_op jit(solution)/shard_map/attend/pallas_call | solution.py:292
  40.5 3.8 %all-to-all-start = ((bf16[4,512,512]{2,1,0:T(8,128)(2,1)}), bf16[4,512,512]{2,1,0:T(8,128)(2,1)S(1)}, u32[]{:S(2)}, u32[]{:S(2)}) async-start(bf16[4,512,512]{2,1,0:T(8,128)(2,1)} %attend.1), calls=%async_computation | async-start | bytes 4194304 | tf_op jit(solution)/shard_map/all_to_all | solution.py:394
  44.3 1.1 %pad_maximum_fusion.rest_0_ = bf16[1024,512]{1,0:T(8,128)(2,1)S(1)} fusion(bf16[512,512]{1,0:T(8,128)(2,1)} %collective-permute-done.4, bf16[256,512]{1,0:T(8,128)(2,1)S(1)} %collective-permute-done, bf16[256,512]{1,0:T(8,128)(2,1)S(1)} %constant_dynamic-slice_fusion), kind=kLoop, calls=%fused_computation | loop fusion | flops 3145728 | bytes 2097152 | tf_op jit(solution)/shard_map/concatenate | solution.py:395
  45.4 1.6 %collective-permute-start.5 = (bf16[1024,512]{1,0:T(8,128)(2,1)S(1)}, bf16[1024,512]{1,0:T(8,128)(2,1)S(1)}, u32[]{:S(2)}, u32[]{:S(2)}) collective-permute-start(bf16[1024,512]{1,0:T(8,128)(2,1)S(1)} %pad_maximum_fusion.rest_0_), channel_id=1, source_target_pairs={{0,16},{16,0},{1,17},{17,1},{2,18},{18,2},{3,19},{19,3},{4,20},{20... | collective-permute-start | bytes 3145736 | tf_op jit(solution)/shard_map/ppermute | solution.py:306
  47.0 1.5 %collective-permute-start.8 = (bf16[1024,512]{1,0:T(8,128)(2,1)S(1)}, bf16[1024,512]{1,0:T(8,128)(2,1)S(1)}, u32[]{:S(2)}, u32[]{:S(2)}) collective-permute-start(bf16[1024,512]{1,0:T(8,128)(2,1)S(1)} %pad_maximum_fusion.rest_0_), channel_id=1, source_target_pairs={{0,8},{4,12},{8,0},{12,4},{1,9},{5,13},{9,1},{13,5},{2,10},{6,14},... | collective-permute-start | bytes 3145736 | tf_op jit(solution)/shard_map/ppermute | solution.py:306
  48.6 22.6 %collective-permute-done.5.rest_1_ = bf16[1024,512]{1,0:T(8,128)(2,1)S(1)} collective-permute-done((bf16[1024,512]{1,0:T(8,128)(2,1)S(1)}, bf16[1024,512]{1,0:T(8,128)(2,1)S(1)}, u32[]{:S(2)}, u32[]{:S(2)}) %collective-permute-start.5) | collective-permute-done | bytes 1048608 | tf_op jit(solution)/shard_map/ppermute | solution.py:306
  71.3 1.6 %collective-permute-start.9 = (bf16[512,512]{1,0:T(8,128)(2,1)S(1)}, bf16[512,512]{1,0:T(8,128)(2,1)S(1)}, u32[]{:S(2)}, u32[]{:S(2)}) collective-permute-start(bf16[512,512]{1,0:T(8,128)(2,1)S(1)} %slice.8), channel_id=1, source_target_pairs={{0,8},{4,12},{8,0},{12,4},{1,9},{5,13},{9,1},{13,5},{2,10},{6,14},... | collective-permute-start | bytes 1572872 | tf_op jit(solution)/shard_map/ppermute | solution.py:306
  72.9 1.6 %collective-permute-start.10 = (bf16[512,512]{1,0:T(8,128)(2,1)S(1)}, bf16[512,512]{1,0:T(8,128)(2,1)S(1)}, u32[]{:S(2)}, u32[]{:S(2)}) collective-permute-start(bf16[512,512]{1,0:T(8,128)(2,1)S(1)} %slice.9), channel_id=1, source_target_pairs={{0,16},{16,0},{1,17},{17,1},{2,18},{18,2},{3,19},{19,3},{4,20},{20... | collective-permute-start | bytes 1572872 | tf_op jit(solution)/shard_map/ppermute | solution.py:306
  74.5 0.5 collective-permute-start.7
  75.0 10.0 %collective-permute-done.9.rest_5_ = bf16[512,512]{1,0:T(8,128)(2,1)S(1)} collective-permute-done((bf16[512,512]{1,0:T(8,128)(2,1)S(1)}, bf16[512,512]{1,0:T(8,128)(2,1)S(1)}, u32[]{:S(2)}, u32[]{:S(2)}) %collective-permute-start.9) | collective-permute-done | bytes 524320 | tf_op jit(solution)/shard_map/ppermute | solution.py:306
  85.0 1.3 %collective-permute-done.10.rest_6_ = bf16[512,512]{1,0:T(8,128)(2,1)S(1)} collective-permute-done((bf16[512,512]{1,0:T(8,128)(2,1)S(1)}, bf16[512,512]{1,0:T(8,128)(2,1)S(1)}, u32[]{:S(2)}, u32[]{:S(2)}) %collective-permute-start.10) | collective-permute-done | bytes 524320 | tf_op jit(solution)/shard_map/ppermute | solution.py:306
  86.3 0.6 collective-permute-done.12.rest_8_
  86.9 1.3 %collective-permute-done.13.rest_9_ = bf16[512,512]{1,0:T(8,128)(2,1)S(1)} collective-permute-done((bf16[512,512]{1,0:T(8,128)(2,1)S(1)}, bf16[512,512]{1,0:T(8,128)(2,1)S(1)}, u32[]{:S(2)}, u32[]{:S(2)}) %collective-permute-start.13) | collective-permute-done | bytes 524320 | tf_op jit(solution)/shard_map/ppermute | solution.py:306
  88.3 0.8 copy-done.9
  89.1 1.0 copy-done.5
  90.1 3.3 %all-to-all-done.features = bf16[4,512,512]{2,1,0:T(8,128)(2,1)S(1)} async-done(((bf16[4,512,512]{2,1,0:T(8,128)(2,1)}), bf16[4,512,512]{2,1,0:T(8,128)(2,1)S(1)}, u32[]{:S(2)}, u32[]{:S(2)}) %all-to-all-start) | async-done | bytes 2097184 | tf_op jit(solution)/shard_map/all_to_all | solution.py:394
  93.4 8.0 %project_out.1 = bf16[512,2048]{1,0:T(8,128)(2,1)} custom-call(bf16[4,512,512]{2,1,0:T(8,128)(2,1)S(1)} %all-to-all-done.features, bf16[1024,512]{1,0:T(8,128)(2,1)} %copy-done.1, bf16[1024,512]{1,0:T(8,128)(2,1)} %copy-done.2, bf16[1024,512]{1,0:T(8,128)(2,1)} %copy-done.4, bf16[1024,512]{1,0:T(8,128)(2,1)} %collective-permute-done.7.rest_3_, ...), custom_call_target="tpu_custom_call" | custom-call | flops 4294967296 | bytes 8388608 | tf_op jit(solution)/shard_map/project_out/pallas_call | solution.py:362
  (35 shorter events, 0.7 us)
Async XLA Ops:
  0.0 1.0 %copy-start = (bf16[512,512]{1,0:T(8,128)(2,1)S(1)}, bf16[512,512]{1,0:T(8,128)(2,1)}, u32[]{:S(2)}) copy-start(bf16[512,512]{1,0:T(8,128)(2,1)} %param.10) | copy-start | bytes 1572868
  1.1 19.6 %collective-permute-start = (bf16[256,512]{1,0:T(8,128)(2,1)S(1)}, bf16[256,512]{1,0:T(8,128)(2,1)S(1)}, u32[]{:S(2)}, u32[]{:S(2)}) collective-permute-start(bf16[256,512]{1,0:T(8,128)(2,1)S(1)} %constant_dynamic-slice_fusion), channel_id=1, source_target_pairs={{0,2},{1,3},{2,0},{3,1},{4,6},{5,7},{6,4},{7,5},{8,10},{9,11},{10,... | collective-permute-start | bytes 786440 | tf_op jit(solution)/shard_map/ppermute | solution.py:306
  20.7 8.1 %collective-permute-start.1 = (bf16[4,144,128]{2,1,0:T(8,128)(2,1)S(1)}, bf16[4,144,128]{2,1,0:T(8,128)(2,1)S(1)}, u32[]{:S(2)}, u32[]{:S(2)}) collective-permute-start(bf16[4,144,128]{2,1,0:T(8,128)(2,1)S(1)} %get-tuple-element.28), channel_id=1, source_target_pairs={{0,4},{4,0},{8,12},{12,8},{1,5},{5,1},{9,13},{13,9},{2,6},{6,2},{1... | collective-permute-start | bytes 442376 | tf_op jit(solution)/shard_map/ppermute | solution.py:306
  20.8 8.0 %collective-permute-start.2 = (bf16[4,144,128]{2,1,0:T(8,128)(2,1)S(1)}, bf16[4,144,128]{2,1,0:T(8,128)(2,1)S(1)}, u32[]{:S(2)}, u32[]{:S(2)}) collective-permute-start(bf16[4,144,128]{2,1,0:T(8,128)(2,1)S(1)} %get-tuple-element.28), channel_id=1, source_target_pairs={{0,8},{4,12},{8,0},{12,4},{1,9},{5,13},{9,1},{13,5},{2,10},{6,14},... | collective-permute-start | bytes 442376 | tf_op jit(solution)/shard_map/ppermute | solution.py:306
  22.4 7.4 %collective-permute-start.3 = (bf16[4,144,128]{2,1,0:T(8,128)(2,1)S(1)}, bf16[4,144,128]{2,1,0:T(8,128)(2,1)S(1)}, u32[]{:S(2)}, u32[]{:S(2)}) collective-permute-start(bf16[4,144,128]{2,1,0:T(8,128)(2,1)S(1)} %get-tuple-element.28), channel_id=1, source_target_pairs={{0,12},{4,8},{8,4},{12,0},{1,13},{5,9},{9,5},{13,1},{2,14},{6,10},... | collective-permute-start | bytes 442376 | tf_op jit(solution)/shard_map/ppermute | solution.py:306
  22.7 17.8 %collective-permute-start.4 = (bf16[512,512]{1,0:T(8,128)(2,1)S(1)}, bf16[512,512]{1,0:T(8,128)(2,1)}, u32[]{:S(2)}, u32[]{:S(2)}) collective-permute-start(bf16[512,512]{1,0:T(8,128)(2,1)S(1)} %pad_maximum_fusion.1), channel_id=1, source_target_pairs={{0,1},{1,0},{2,3},{3,2},{4,5},{5,4},{6,7},{7,6},{8,9},{9,8},{10,11... | collective-permute-start | bytes 1572872 | tf_op jit(solution)/shard_map/ppermute | solution.py:306
  40.5 52.9 %all-to-all-start = ((bf16[4,512,512]{2,1,0:T(8,128)(2,1)}), bf16[4,512,512]{2,1,0:T(8,128)(2,1)S(1)}, u32[]{:S(2)}, u32[]{:S(2)}) async-start(bf16[4,512,512]{2,1,0:T(8,128)(2,1)} %attend.1), calls=%async_computation | async-start | bytes 4194304 | tf_op jit(solution)/shard_map/all_to_all | solution.py:394
  45.4 42.8 %copy-start.1 = (bf16[1024,512]{1,0:T(8,128)(2,1)}, bf16[1024,512]{1,0:T(8,128)(2,1)S(1)}, u32[]{:S(2)}) copy-start(bf16[1024,512]{1,0:T(8,128)(2,1)S(1)} %pad_maximum_fusion.rest_0_) | copy-start | bytes 3145732
  45.4 25.8 %collective-permute-start.5 = (bf16[1024,512]{1,0:T(8,128)(2,1)S(1)}, bf16[1024,512]{1,0:T(8,128)(2,1)S(1)}, u32[]{:S(2)}, u32[]{:S(2)}) collective-permute-start(bf16[1024,512]{1,0:T(8,128)(2,1)S(1)} %pad_maximum_fusion.rest_0_), channel_id=1, source_target_pairs={{0,16},{16,0},{1,17},{17,1},{2,18},{18,2},{3,19},{19,3},{4,20},{20... | collective-permute-start | bytes 3145736 | tf_op jit(solution)/shard_map/ppermute | solution.py:306
  47.0 25.8 %collective-permute-start.8 = (bf16[1024,512]{1,0:T(8,128)(2,1)S(1)}, bf16[1024,512]{1,0:T(8,128)(2,1)S(1)}, u32[]{:S(2)}, u32[]{:S(2)}) collective-permute-start(bf16[1024,512]{1,0:T(8,128)(2,1)S(1)} %pad_maximum_fusion.rest_0_), channel_id=1, source_target_pairs={{0,8},{4,12},{8,0},{12,4},{1,9},{5,13},{9,1},{13,5},{2,10},{6,14},... | collective-permute-start | bytes 3145736 | tf_op jit(solution)/shard_map/ppermute | solution.py:306
  48.5 37.8 %collective-permute-start.6 = (bf16[1024,512]{1,0:T(8,128)(2,1)S(1)}, bf16[1024,512]{1,0:T(8,128)(2,1)S(1)}, u32[]{:S(2)}, u32[]{:S(2)}) collective-permute-start(bf16[1024,512]{1,0:T(8,128)(2,1)S(1)} %pad_maximum_fusion.rest_0_), channel_id=1, source_target_pairs={{0,4},{4,0},{8,12},{12,8},{1,5},{5,1},{9,13},{13,9},{2,6},{6,2},{1... | collective-permute-start | bytes 3145736 | tf_op jit(solution)/shard_map/ppermute | solution.py:306
  71.2 17.0 %copy-start.2 = (bf16[1024,512]{1,0:T(8,128)(2,1)}, bf16[1024,512]{1,0:T(8,128)(2,1)S(1)}, u32[]{:S(2)}) copy-start(bf16[1024,512]{1,0:T(8,128)(2,1)S(1)} %collective-permute-done.5.rest_1_) | copy-start | bytes 3145732
  71.3 13.7 %collective-permute-start.9 = (bf16[512,512]{1,0:T(8,128)(2,1)S(1)}, bf16[512,512]{1,0:T(8,128)(2,1)S(1)}, u32[]{:S(2)}, u32[]{:S(2)}) collective-permute-start(bf16[512,512]{1,0:T(8,128)(2,1)S(1)} %slice.8), channel_id=1, source_target_pairs={{0,8},{4,12},{8,0},{12,4},{1,9},{5,13},{9,1},{13,5},{2,10},{6,14},... | collective-permute-start | bytes 1572872 | tf_op jit(solution)/shard_map/ppermute | solution.py:306
  72.8 15.4 %copy-start.3 = (bf16[1024,512]{1,0:T(8,128)(2,1)}, bf16[1024,512]{1,0:T(8,128)(2,1)S(1)}, u32[]{:S(2)}) copy-start(bf16[1024,512]{1,0:T(8,128)(2,1)S(1)} %collective-permute-done.8.rest_4_) | copy-start | bytes 3145732
  72.9 13.4 %collective-permute-start.10 = (bf16[512,512]{1,0:T(8,128)(2,1)S(1)}, bf16[512,512]{1,0:T(8,128)(2,1)S(1)}, u32[]{:S(2)}, u32[]{:S(2)}) collective-permute-start(bf16[512,512]{1,0:T(8,128)(2,1)S(1)} %slice.9), channel_id=1, source_target_pairs={{0,16},{16,0},{1,17},{17,1},{2,18},{18,2},{3,19},{19,3},{4,20},{20... | collective-permute-start | bytes 1572872 | tf_op jit(solution)/shard_map/ppermute | solution.py:306
  74.5 13.8 %collective-permute-start.11 = (bf16[1024,512]{1,0:T(8,128)(2,1)S(1)}, bf16[1024,512]{1,0:T(8,128)(2,1)S(1)}, u32[]{:S(2)}, u32[]{:S(2)}) collective-permute-start(bf16[1024,512]{1,0:T(8,128)(2,1)S(1)} %collective-permute-done.8.rest_4_), channel_id=1, source_target_pairs={{0,4},{4,0},{8,12},{12,8},{1,5},{5,1},{9,13},{13,9},{2,6},{6,2},{1... | collective-permute-start | bytes 3145736 | tf_op jit(solution)/shard_map/ppermute | solution.py:306
  74.5 15.6 %collective-permute-start.7 = (bf16[1024,512]{1,0:T(8,128)(2,1)S(1)}, bf16[1024,512]{1,0:T(8,128)(2,1)}, u32[]{:S(2)}, u32[]{:S(2)}) collective-permute-start(bf16[1024,512]{1,0:T(8,128)(2,1)S(1)} %collective-permute-done.5.rest_1_), channel_id=1, source_target_pairs={{0,4},{4,0},{8,12},{12,8},{1,5},{5,1},{9,13},{13,9},{2,6},{6,2},{1... | collective-permute-start | bytes 3145736 | tf_op jit(solution)/shard_map/ppermute | solution.py:306
  85.0 8.4 %copy-start.6 = (bf16[512,512]{1,0:T(8,128)(2,1)}, bf16[512,512]{1,0:T(8,128)(2,1)S(1)}, u32[]{:S(2)}) copy-start(bf16[512,512]{1,0:T(8,128)(2,1)S(1)} %collective-permute-done.9.rest_5_) | copy-start | bytes 1572868
  85.0 1.9 %collective-permute-start.12 = (bf16[512,512]{1,0:T(8,128)(2,1)S(1)}, bf16[512,512]{1,0:T(8,128)(2,1)S(1)}, u32[]{:S(2)}, u32[]{:S(2)}) collective-permute-start(bf16[512,512]{1,0:T(8,128)(2,1)S(1)} %collective-permute-done.9.rest_5_), channel_id=1, source_target_pairs={{0,4},{4,0},{8,12},{12,8},{1,5},{5,1},{9,13},{13,9},{2,6},{6,2},{1... | collective-permute-start | bytes 1572872 | tf_op jit(solution)/shard_map/ppermute | solution.py:306
  86.3 1.9 %copy-start.7 = (bf16[512,512]{1,0:T(8,128)(2,1)}, bf16[512,512]{1,0:T(8,128)(2,1)S(1)}, u32[]{:S(2)}) copy-start(bf16[512,512]{1,0:T(8,128)(2,1)S(1)} %collective-permute-done.10.rest_6_) | copy-start | bytes 1572868
  86.3 1.9 %collective-permute-start.13 = (bf16[512,512]{1,0:T(8,128)(2,1)S(1)}, bf16[512,512]{1,0:T(8,128)(2,1)S(1)}, u32[]{:S(2)}, u32[]{:S(2)}) collective-permute-start(bf16[512,512]{1,0:T(8,128)(2,1)S(1)} %collective-permute-done.10.rest_6_), channel_id=1, source_target_pairs={{0,4},{4,0},{8,12},{12,8},{1,5},{5,1},{9,13},{13,9},{2,6},{6,2},{1... | collective-permute-start | bytes 1572872 | tf_op jit(solution)/shard_map/ppermute | solution.py:306
  86.3 1.9 %copy-start.4 = (bf16[1024,512]{1,0:T(8,128)(2,1)}, bf16[1024,512]{1,0:T(8,128)(2,1)S(1)}, u32[]{:S(2)}) copy-start(bf16[1024,512]{1,0:T(8,128)(2,1)S(1)} %collective-permute-done.6.rest_2_) | copy-start | bytes 3145732
  86.9 1.4 %copy-start.8 = (bf16[512,512]{1,0:T(8,128)(2,1)}, bf16[512,512]{1,0:T(8,128)(2,1)S(1)}, u32[]{:S(2)}) copy-start(bf16[512,512]{1,0:T(8,128)(2,1)S(1)} %collective-permute-done.12.rest_8_) | copy-start | bytes 1572868
  89.1 1.0 copy-start.5
  (1 other events, 0.9 us)

commit v4 on v3

v4 whole, which is shorter than its diff:
```python
import functools

import jax
import jax.numpy as jnp
from jax import lax
from jax.experimental import pallas as pl
from jax.experimental.pallas import tpu as pltpu
from jax.sharding import PartitionSpec as P

DH = 128
BLOCK = 256
STEP = 512
AHEAD = 3
OUT_AHEAD = 8
EXTRA = 16
F32 = jnp.float32
BF16 = jnp.bfloat16
HIGHEST = lax.Precision.HIGHEST
LOG2E = 1.4426950408889634
MIB = 1 << 20


def dot(a, b, dims=((1,), (0,)), precision=None):
    return lax.dot_general(a, b, (dims, ((), ())), precision=precision, preferred_element_type=F32)


def relative_half(part, width):
    start = lax.rem(part + lax.axis_index("grp"), 2) * width
    return pl.ds(pl.multiple_of(start, width), width)


def kv_kernel(part, act, wk, wv, wq, decay, act_out, wq_out, kv_out, before, payload, spread, wrow, reach,
              held, logs, state, wcol, sems):
    half, tokens = decay.shape[0] // 2, decay.shape[1]
    blocks = tokens // BLOCK
    wide = half * DH
    chunks = [(0, BLOCK), (BLOCK, STEP - BLOCK)]
    chunks += [(start, STEP) for start in range(STEP, tokens, STEP)]

    def load_rows(start, size):
        rows = pl.ds(start, size)
        return functools.partial(pltpu.make_async_copy, act.at[rows], act_out.at[rows])

    def load_half(source, target, lane):
        return functools.partial(
            pltpu.make_async_copy,
            source.at[:, relative_half(part, wide)],
            target.at[:, pl.ds(lane, wide)],
        )

    matrices = [wk, wv]
    loads = [load_rows(*chunks[0])]
    loads += [load_half(w, held, at * wide) for at, w in enumerate(matrices)]
    loads += [load_rows(*chunk) for chunk in chunks[1:]]
    loads += [load_half(wq, wq_out, 0)]
    queue = [load(sems.at[at]) for at, load in enumerate(loads)]
    load_logs = pltpu.make_async_copy(decay, logs, sems.at[len(queue)])
    load_logs.start()
    for copy in queue[:AHEAD]:
        copy.start()

    def take(at):
        queue[at].wait()
        if at + AHEAD < len(queue):
            queue[at + AHEAD].start()

    load_logs.wait()
    rates = jnp.where(lax.axis_index("grp") == part, logs[:half], logs[half:])
    rates = jnp.concatenate([rates, jnp.zeros((8 - half, tokens), F32)], axis=0)
    stacked = jnp.concatenate([rates[:, n * BLOCK : (n + 1) * BLOCK] for n in range(blocks)], axis=0)
    upper = (
        lax.broadcasted_iota(jnp.int32, (BLOCK, BLOCK), 0)
        <= lax.broadcasted_iota(jnp.int32, (BLOCK, BLOCK), 1)
    ).astype(F32)
    within = LOG2E * dot(stacked, upper, precision=HIGHEST)
    total = jnp.zeros((8, 1), F32)
    for n in range(blocks):
        rows = within[n * 8 : (n + 1) * 8]
        wrow[n] = rows
        wcol[n] = rows.T
        reach[n] = jnp.broadcast_to(jnp.exp2(total), (8, DH))
        total = total + rows[:, BLOCK - 1 :]
    factor = jnp.broadcast_to(jnp.exp2(total), (8, DH))
    state[...] = jnp.zeros_like(state)

    for chunk, (start, size) in enumerate(chunks):
        rows = slice(start, start + size)
        take(chunk + len(matrices) if chunk else 0)
        halves = []
        for at in range(len(matrices)):
            if chunk == 0:
                take(1 + at)
            lanes = slice(at * wide, (at + 1) * wide)
            halves.append(dot(act_out[rows], held[:, lanes]).astype(BF16))
            kv_out[rows, lanes] = halves[at]
        for b in range(size // BLOCK):
            n = start // BLOCK + b
            block = slice(b * BLOCK, (b + 1) * BLOCK)
            for h in range(half):
                lanes = slice(h * DH, (h + 1) * DH)
                cols = jnp.broadcast_to(wcol[n][:, h : h + 1], (BLOCK, DH))
                spread[n, h] = cols
                last = cols[BLOCK - 1 :]
                k_b = halves[0][block, lanes].astype(F32) * jnp.exp2(last - cols)
                update = dot(k_b.astype(BF16), halves[1][block, lanes], ((0,), (0,)))
                old = state[h]
                before[n, h] = old
                state[h] = jnp.exp2(last) * old + update

    for h in range(half):
        payload[h, :DH] = state[h].astype(BF16)
        whole = jnp.broadcast_to(factor[h : h + 1], (EXTRA, DH))
        high = whole.astype(BF16).astype(F32)
        first = lax.broadcasted_iota(jnp.int32, (EXTRA, DH), 0) < EXTRA // 2
        payload[h, DH:] = jnp.where(first, high, whole - high).astype(BF16)
    take(len(queue) - 1)


def project_kernel(act, w, out):
    for step in range(act.shape[0] // STEP):
        rows = slice(step * STEP, (step + 1) * STEP)
        out[rows] = dot(act[rows], w[...]).astype(BF16)


def incoming_state(arrivals, h):
    place = lax.axis_index("seq")
    sources = [lax.bitwise_xor(place, r + 1) for r in range(len(arrivals))]
    reaches = []
    for piece in arrivals:
        extra = piece[h, DH:].astype(F32)
        reaches.append(extra[:1] + extra[EXTRA // 2 : EXTRA // 2 + 1])
    total = jnp.zeros((DH, DH), F32)
    for source, piece in zip(sources, arrivals):
        weight = jnp.where(source < place, jnp.ones((1, DH), F32), 0.0)
        for other, reach in zip(sources, reaches):
            between = jnp.logical_and(other > source, other < place)
            weight = weight * jnp.where(between, reach, 1.0)
        total = total + weight * piece[h, :DH].astype(F32)
    return total


def attend_kernel(received, q, kv, before, spread, wrow, reach, *rest):
    arrivals, (out, held, bound, sems) = rest[:received], rest[received:]
    sources, share, columns = out.shape
    heads = columns // DH

    def send(target):
        return pltpu.make_async_copy(held.at[target], out.at[target], sems.at[target])

    causal = lax.broadcasted_iota(jnp.int32, (BLOCK, BLOCK), 0) >= lax.broadcasted_iota(
        jnp.int32, (BLOCK, BLOCK), 1
    )
    bound[...] = jnp.where(causal, 0.0, -1e30)
    prefix = [incoming_state(arrivals, h) for h in range(heads)]

    @pl.loop(0, sources)
    def _(target):
        for b in range(share // BLOCK):
            n = target * (share // BLOCK) + b
            rows = pl.ds(pl.multiple_of(n * BLOCK, BLOCK), BLOCK)
            reached = reach[n]
            lanes = [slice(h * DH, (h + 1) * DH) for h in range(heads)]
            scores = [dot(q[rows, lane], kv[rows, lane], ((1,), (1,))) for lane in lanes]
            carried = []
            for h, lane in enumerate(lanes):
                incoming = (before[n, h] + reached[h : h + 1] * prefix[h]).astype(BF16)
                carried.append(dot(q[rows, lane], incoming))
            weights = []
            for h in range(heads):
                cols = spread[n, h]
                gap = jnp.concatenate([cols] * (BLOCK // DH), axis=1) - wrow[n, h : h + 1]
                weights.append((scores[h] * jnp.exp2(jnp.minimum(gap, bound[...]))).astype(BF16))
            for h, lane in enumerate(lanes):
                v_b = kv[rows, columns + h * DH : columns + (h + 1) * DH]
                attended = dot(weights[h], v_b) + jnp.exp2(spread[n, h]) * carried[h]
                mean = jnp.mean(attended * attended, axis=1, keepdims=True)
                normed = (attended * lax.rsqrt(mean + 1e-5)).astype(BF16)
                held[target, b * BLOCK : (b + 1) * BLOCK, lane] = normed
        send(target).start()

    for target in range(sources):
        send(target).wait()


def out_kernel(offsets, order, begun, features, *rest):
    if begun:
        earlier, rest = rest[0], rest[1:]
    weights, (out, left, held, ready, done, sems, out_sems) = rest[:-7], rest[-7:]
    mine, place = lax.axis_index("head"), lax.axis_index("seq")
    half = features.shape[2]
    width = done.shape[2]
    each = len(weights) // len(offsets)

    def store(slot):
        if not begun:
            return pltpu.make_async_copy(done.at[slot], out.at[slot], out_sems.at[slot])
        columns = pl.ds(pl.multiple_of(lax.bitwise_xor(place, offsets[slot]) * width, width), width)
        return pltpu.make_async_copy(done.at[slot], out.at[:, columns], out_sems.at[slot])

    loads, parts = [], []
    for slot in range(len(offsets)):
        begin = 0
        for piece in weights[slot * each : (slot + 1) * each]:
            rows = pl.ds(begin, piece.shape[0])
            parts.append((slot, rows, len(loads)))
            loads.append((piece, held.at[slot, rows]))
            begin += piece.shape[0]
        if begun:
            loads.append((earlier.at[slot], ready.at[slot]))
    queue = [pltpu.make_async_copy(*pair, sems.at[i]) for i, pair in enumerate(loads)]
    for copy in queue[:OUT_AHEAD]:
        copy.start()

    def take(i):
        queue[i].wait()
        if i + OUT_AHEAD < len(queue):
            queue[i + OUT_AHEAD].start()

    for i, r in enumerate(order):
        left[:, i * half : (i + 1) * half] = features[lax.bitwise_xor(mine, r)]
    for slot in range(len(offsets)):
        total = None
        for at, rows, i in parts:
            if at == slot:
                take(i)
                term = dot(left[:, rows], held[slot, rows])
                total = term if total is None else total + term
        if begun:
            take((slot + 1) * (each + 1) - 1)
            total = total + ready[slot]
        done[slot] = total.astype(done.dtype)
        store(slot).start()
    for slot in range(len(offsets)):
        store(slot).wait()


def cost(flops, moved):
    return pl.CostEstimate(flops=flops, bytes_accessed=moved, transcendentals=0)


def in_hbm():
    return pl.BlockSpec(memory_space=pltpu.HBM)


def stay_in_hbm(*values):
    return [pltpu.with_memory_space_constraint(value, pltpu.HBM) for value in values]


def in_vmem():
    return pl.BlockSpec(memory_space=pltpu.VMEM)


def keys_values(part, activations, w_key, w_value, w_query, log_decay):
    tokens, width = activations.shape
    heads = log_decay.shape[0] // 2
    columns, blocks = heads * DH, tokens // BLOCK
    shapes = [
        ((tokens, width), BF16),
        ((width, columns), BF16),
        ((tokens, 2 * columns), BF16),
        ((blocks, heads, DH, DH), F32),
        ((heads, DH + EXTRA, DH), BF16),
        ((blocks, heads, BLOCK, DH), F32),
        ((blocks, 8, BLOCK), F32),
        ((blocks, 8, DH), F32),
    ]
    return pl.pallas_call(
        functools.partial(kv_kernel, part),
        in_specs=[in_hbm()] * 5,
        out_specs=[in_vmem()] * len(shapes),
        out_shape=[pltpu.VMEM(*shape) for shape in shapes],
        scratch_shapes=[
            pltpu.VMEM((width, 2 * columns), BF16),
            pltpu.VMEM((2 * heads, tokens), F32),
            pltpu.VMEM((heads, DH, DH), F32),
            pltpu.VMEM((blocks, BLOCK, 8), F32),
            pltpu.SemaphoreType.DMA((tokens // STEP + 8,)),
        ],
        compiler_params=pltpu.CompilerParams(vmem_limit_bytes=16 * MIB),
        cost_estimate=cost(4 * tokens * width * columns, 4 * tokens * width),
        name="keys_values",
    )(*stay_in_hbm(activations, w_key, w_value, w_query, log_decay))


def queries(activations, w_query):
    tokens, width = activations.shape
    columns = w_query.shape[1]
    return pl.pallas_call(
        project_kernel,
        in_specs=[in_vmem()] * 2,
        out_specs=in_vmem(),
        out_shape=pltpu.VMEM((tokens, columns), BF16),
        compiler_params=pltpu.CompilerParams(vmem_limit_bytes=16 * MIB),
        cost_estimate=cost(2 * tokens * width * columns, 2 * tokens * width),
        name="queries",
    )(activations, w_query)


def attend(sources, query, *rest):
    received = len(rest) - 5
    tokens, columns = query.shape
    shares = (sources, tokens // sources, columns)
    return pl.pallas_call(
        functools.partial(attend_kernel, received),
        in_specs=[in_vmem()] * (len(rest) + 1),
        out_specs=in_hbm(),
        out_shape=pltpu.HBM(shares, BF16),
        scratch_shapes=[
            pltpu.VMEM(shares, BF16),
            pltpu.VMEM((BLOCK, BLOCK), F32),
            pltpu.SemaphoreType.DMA((sources,)),
        ],
        compiler_params=pltpu.CompilerParams(vmem_limit_bytes=16 * MIB),
        cost_estimate=cost(20 * tokens * BLOCK * columns, 8 * tokens * columns),
        name="attend",
    )(query, *rest)


def swap(value, axis, bit):
    count = lax.axis_size(axis)
    return lax.ppermute(value, axis, [(i, i ^ bit) for i in range(count)])


def bits_of(count):
    return [1 << b for b in reversed(range(count.bit_length() - 1))]


def gather_rows(w_out):
    half = w_out.shape[0] // 2
    own = lax.dynamic_slice_in_dim(w_out, lax.axis_index("grp") * half, half, axis=0)
    return {0: own} | {bit: swap(own, "head", bit) for bit in bits_of(lax.axis_size("head"))}


def gather_rest(pieces):
    pieces = dict(pieces)
    for r in range(lax.axis_size("head")):
        if r not in pieces:
            pieces[r] = swap(pieces[r & (r - 1)], "head", r & -r)
    return pieces


def gather_columns(even, odd, even_across, even_beside, settled):
    across, beside = [even_across], [even_beside]
    even_beside, odd = after((even_beside, odd), *settled)
    odd_across, odd_beside = lax.optimization_barrier((swap(odd, "seq", 2), swap(odd, "grp", 1)))
    across.append(odd_across)
    beside.append(odd_beside)
    corner = [swap(even_beside, "seq", 2), swap(across[1], "grp", 1)]
    found = {(0, 0): [even, odd], (0, 2): across, (1, 0): beside, (1, 2): corner}
    for bit in bits_of(lax.axis_size("seq"))[:-2]:
        found.update(
            {
                (g, s ^ bit): [swap(part, "seq", bit) for part in parts]
                for (g, s), parts in list(found.items())
            }
        )
    return found


def gather_partner(found):
    return found | {
        (g, s ^ 1): [swap(part, "seq", 1) for part in parts] for (g, s), parts in found.items()
    }


def project_out(features, part, found, order, earlier=None):
    sources, rows, columns = features.shape
    offsets = sorted({s for _, s in found})
    operands = [piece for offset in offsets for piece in found[(part, offset)]]
    width, blocks = operands[0].shape[1], len(offsets)
    lead = [] if earlier is None else [earlier]
    shape = (rows, blocks * width) if lead else (blocks, rows, width)
    dtype = BF16 if lead else F32
    return pl.pallas_call(
        functools.partial(out_kernel, offsets, order, bool(lead)),
        out_shape=pltpu.HBM(shape, dtype),
        in_specs=[in_vmem()] + [in_hbm()] * (len(lead) + len(operands)),
        out_specs=in_hbm(),
        scratch_shapes=[
            pltpu.VMEM((rows, sources * columns), BF16),
            pltpu.VMEM((blocks, sources * columns, width), BF16),
            pltpu.VMEM((blocks, rows, width) if lead else (8, 128), F32),
            pltpu.VMEM((blocks, rows, width), dtype),
            pltpu.SemaphoreType.DMA((len(operands) + blocks * len(lead),)),
            pltpu.SemaphoreType.DMA((blocks,)),
        ],
        compiler_params=pltpu.CompilerParams(vmem_limit_bytes=24 * MIB),
        cost_estimate=cost(2 * rows * sources * columns * width * blocks, 8 * MIB),
        name="project_out",
    )(features, *stay_in_hbm(*lead, *operands))


def after(value, *earlier):
    return lax.optimization_barrier((value, *earlier))[0]


def on_device(activations, w_query, w_key, w_value, w_out, log_decay):
    places, sources = lax.axis_size("seq"), lax.axis_size("head")
    pieces = gather_rows(w_out)
    features = []
    for part in range(2):
        rows, w_part, kv, before, payload, spread, wrow, reach = keys_values(
            part, activations, w_key, w_value, w_query, log_decay
        )
        arrivals = [swap(payload, "seq", r) for r in range(1, places)]
        if part == 0:
            rows, pieces = lax.optimization_barrier((rows, pieces))
            pieces = gather_rest(pieces)
        else:
            rows, across, beside = lax.optimization_barrier((rows, across, beside))
        query = queries(rows, w_part)
        normed = attend(sources, query, kv, before, spread, wrow, reach, *arrivals)
        if part == 0:
            normed, pieces, activations = lax.optimization_barrier((normed, pieces, activations))
            even, odd = [r for r in pieces if r % 2 == 0], [r for r in pieces if r % 2]
            order = even + odd
            even, odd = [
                jnp.concatenate([pieces[r] for r in group], axis=0) for group in (even, odd)
            ]
            across, beside = swap(even, "seq", 2), swap(even, "grp", 1)
        features.append(lax.all_to_all(normed, "head", 0, 0))
    found = gather_columns(even, odd, across, beside, arrivals)
    first = {(g, s): parts for (g, s), parts in found.items() if g == 0}
    begun = project_out(features[0], 0, gather_partner(first), order)
    second = {(g, s): parts for (g, s), parts in found.items() if g == 1}
    second, begun = lax.optimization_barrier((second, begun))
    return project_out(features[1], 1, gather_partner(second), order, begun)


def solution(mesh):
    return jax.shard_map(
        on_device,
        mesh=mesh,
        in_specs=(
            P(("grp", "seq"), None),
            P(None, "head"),
            P(None, "head"),
            P(None, "head"),
            P("head", "seq"),
            P("head", ("grp", "seq")),
        ),
        out_specs=P(("grp", "seq", "head"), None),
        check_vma=False,
    )
```

time: 102 us -> 92.1 us (0.903)
  waiting for transfers between devices: 40 us -> 21 us
  starting transfers between devices: 18.4 us -> 26.6 us
  Pallas kernels: 38.7 us -> 39.9 us
  other arithmetic: 1.15 us -> 0.03 us
    ppermute x14 -> x23, waiting for transfers between devices: 36.7 us -> 14.5 us  [swap(): return lax.ppermute(value, axis, [(i, i ^ bit) for i in range(count)])]
    pallas_call x2 -> x4, Pallas kernels: 23.5 us -> 28.1 us  [the longest x2 17.4 us: keys_values(): pl.pallas_call(functools.partial(kv_kernel, part), in_specs=[in_hbm()] *...]
    all_to_all x1 -> x2, starting transfers between devices: 3.8 us -> 8.31 us  [on_device(): features.append(lax.all_to_all(normed, 'head', 0, 0))]
    ppermute x14 -> x23, starting transfers between devices: 14.6 us -> 18.3 us  [swap(): return lax.ppermute(value, axis, [(i, i ^ bit) for i in range(count)])]
    pallas_call x1 -> x2, Pallas kernels: 10.7 us -> 7.13 us  [attend(): pl.pallas_call(functools.partial(attend_kernel, received), in_specs=[in_v...]
    all_to_all x1 -> x2, waiting for transfers between devices: 3.32 us -> 6.53 us  [on_device(): features.append(lax.all_to_all(normed, 'head', 0, 0))]
    concatenate x2 -> x1, other arithmetic: 1.15 us -> 0.03 us  [on_device(): jnp.concatenate([pieces[r] for r in group], axis=0)]
    unnamed x20 -> x25, local copies, waits for them, and re-layouts: 2.86 us -> 3.83 us
  transfers between devices with their start and end apart: 15 -> 25, of which waited for: 7 -> 13; matrix products, arithmetic and copies ran while one was open for 1% -> 0% of each run, Pallas kernels for 30% -> 38%
where the time goes in v4:
time: 92.1 us; the launch traced here: 91.8 us
  Pallas kernels  39.9 us (43%)
  starting transfers between devices  26.6 us (29%)
  waiting for transfers between devices  21 us (23%)
  local copies, waits for them, and re-layouts  3.87 us (4%)
    ppermute x23, starting transfers between devices, swap(): return lax.ppermute(value, axis, [(i, i ^ bit) for i in range(count)])  18.3 us
    pallas_call x2, Pallas kernels, keys_values(): pl.pallas_call(functools.partial(kv_kernel, part), in_specs=[in_hbm()] *...  17.4 us
    ppermute x23, waiting for transfers between devices, swap(): return lax.ppermute(value, axis, [(i, i ^ bit) for i in range(count)])  14.5 us
    pallas_call x2, Pallas kernels, project_out(): pl.pallas_call(functools.partial(out_kernel, offsets, order, bool(lead)),...  10.7 us
    all_to_all x2, starting transfers between devices, on_device(): features.append(lax.all_to_all(normed, 'head', 0, 0))  8.31 us
    pallas_call x2, Pallas kernels, attend(): pl.pallas_call(functools.partial(attend_kernel, received), in_specs=[in_v...  7.13 us
    all_to_all x2, waiting for transfers between devices, on_device(): features.append(lax.all_to_all(normed, 'head', 0, 0))  6.53 us
    pallas_call x2, Pallas kernels, queries(): pl.pallas_call(project_kernel, in_specs=[in_vmem()] * 2, out_specs=in_vme...  4.65 us
  transfers between devices with their start and end apart: 25, of which 13 were waited for; matrix products, arithmetic and copies ran while one was open for 0% of the time, Pallas kernels for 38%

profile of v4, /device:TPU:0, one launch (start us, length us, event | category | flops | bytes accessed | tf_op | source)
XLA Modules:
  0.0 91.8 jit_solution(238618498110777220)
XLA Ops:
  0.0 1.0 %copy-done = bf16[512,512]{1,0:T(8,128)(2,1)S(1)} copy-done((bf16[512,512]{1,0:T(8,128)(2,1)S(1)}, bf16[512,512]{1,0:T(8,128)(2,1)}, u32[]{:S(2)}) %copy-start) | copy-done | bytes 524312
  1.1 3.1 %collective-permute-start = (bf16[256,512]{1,0:T(8,128)(2,1)S(1)}, bf16[256,512]{1,0:T(8,128)(2,1)S(1)}, u32[]{:S(2)}, u32[]{:S(2)}) collective-permute-start(bf16[256,512]{1,0:T(8,128)(2,1)S(1)} %constant_dynamic-slice_fusion), channel_id=1, source_target_pairs={{0,1},{1,0},{2,3},{3,2},{4,5},{5,4},{6,7},{7,6},{8,9},{9,8},{10,11... | collective-permute-start | bytes 786440 | tf_op jit(solution)/shard_map/ppermute | solution.py:321
  4.2 2.6 %collective-permute-start.1 = (bf16[256,512]{1,0:T(8,128)(2,1)S(1)}, bf16[256,512]{1,0:T(8,128)(2,1)S(1)}, u32[]{:S(2)}, u32[]{:S(2)}) collective-permute-start(bf16[256,512]{1,0:T(8,128)(2,1)S(1)} %constant_dynamic-slice_fusion), channel_id=1, source_target_pairs={{0,2},{1,3},{2,0},{3,1},{4,6},{5,7},{6,4},{7,5},{8,10},{9,11},{10,... | collective-permute-start | bytes 786440 | tf_op jit(solution)/shard_map/ppermute | solution.py:321
  6.7 8.7 %keys_values.2 = (bf16[2048,2048]{1,0:T(8,128)(2,1)S(1)}, bf16[2048,256]{1,0:T(8,128)(2,1)S(1)}, bf16[2048,512]{1,0:T(8,128)(2,1)S(1)}, f32[8,2,128,128]{3,2,1,0...) custom-call(bf16[2048,2048]{1,0:T(8,128)(2,1)} %act.2, ...), custom_call_target="tpu_custom_call" | custom-call | flops 4294967296 | bytes 16777216 | tf_op jit(solution)/shard_map/keys_values/pallas_call | solution.py:267
  15.5 1.6 %collective-permute-start.3 = (bf16[2,144,128]{2,1,0:T(8,128)(2,1)S(1)}, bf16[2,144,128]{2,1,0:T(8,128)(2,1)S(1)}, u32[]{:S(2)}, u32[]{:S(2)}) collective-permute-start(bf16[2,144,128]{2,1,0:T(8,128)(2,1)S(1)} %get-tuple-element.51), channel_id=1, source_target_pairs={{0,8},{4,12},{8,0},{12,4},{1,9},{5,13},{9,1},{13,5},{2,10},{6,14},... | collective-permute-start | bytes 221192 | tf_op jit(solution)/shard_map/ppermute | solution.py:321
  17.4 1.1 %collective-permute-done.1 = bf16[256,512]{1,0:T(8,128)(2,1)S(1)} collective-permute-done((bf16[256,512]{1,0:T(8,128)(2,1)S(1)}, bf16[256,512]{1,0:T(8,128)(2,1)S(1)}, u32[]{:S(2)}, u32[]{:S(2)}) %collective-permute-start.1) | collective-permute-done | bytes 262176 | tf_op jit(solution)/shard_map/ppermute | solution.py:321
  18.9 2.3 %queries.2.q = bf16[2048,256]{1,0:T(8,128)(2,1)S(1)} custom-call(bf16[2048,2048]{1,0:T(8,128)(2,1)S(1)} %get-tuple-element.44.act, bf16[2048,256]{1,0:T(8,128)(2,1)S(1)} %get-tuple-element.45.w), custom_call_target="tpu_custom_call" | custom-call | flops 2147483648 | bytes 8388608 | tf_op jit(solution)/shard_map/queries/pallas_call | solution.py:288
  21.6 3.5 %attend.2 = bf16[4,512,256]{2,1,0:T(8,128)(2,1)} custom-call(bf16[2048,256]{1,0:T(8,128)(2,1)S(1)} %queries.2.q, bf16[2048,512]{1,0:T(8,128)(2,1)S(1)} %get-tuple-element.46.kv, f32[8,2,128,128]{3,2,1,0:T(8,128)S(1)} %get-tuple-element.47.before, f32[8,2,256,128]{3,2,1,0:T(8,128)S(1)} %get-tuple-element.48.spread, f32[8,8,256]{2,1,0:T(8,128)S(1)} %get-tuple-element.49.wrow, ...), custom_call_target="tpu_custom_call" | custom-call | flops 2684354560 | bytes 4194304 | tf_op jit(solution)/shard_map/attend/pallas_call | solution.py:303
  26.0 3.7 %all-to-all-start.1 = ((bf16[4,512,256]{2,1,0:T(8,128)(2,1)}), bf16[4,512,256]{2,1,0:T(8,128)(2,1)S(1)}, u32[]{:S(2)}, u32[]{:S(2)}) async-start(bf16[4,512,256]{2,1,0:T(8,128)(2,1)} %attend.2), calls=%async_computation.1 | async-start | bytes 2097152 | tf_op jit(solution)/shard_map/all_to_all | solution.py:421
  29.7 1.6 %collective-permute-start.6 = (bf16[512,512]{1,0:T(8,128)(2,1)S(1)}, bf16[512,512]{1,0:T(8,128)(2,1)S(1)}, u32[]{:S(2)}, u32[]{:S(2)}) collective-permute-start(bf16[512,512]{1,0:T(8,128)(2,1)S(1)} %constant_dynamic-update-slice_fusion.rest_0_), channel_id=1, source_target_pairs={{0,8},{4,12},{8,0},{12,4},{1,9},{5,13},{9,1},{13,5},{2,10},{6,14},... | collective-permute-start | bytes 1572872 | tf_op jit(solution)/shard_map/ppermute | solution.py:321
  31.3 1.5 %collective-permute-start.7 = (bf16[512,512]{1,0:T(8,128)(2,1)S(1)}, bf16[512,512]{1,0:T(8,128)(2,1)}, u32[]{:S(2)}, u32[]{:S(2)}) collective-permute-start(bf16[512,512]{1,0:T(8,128)(2,1)S(1)} %constant_dynamic-update-slice_fusion.rest_0_), channel_id=1, source_target_pairs={{0,16},{16,0},{1,17},{17,1},{2,18},{18,2},{3,19},{19,3},{4,20},{20... | collective-permute-start | bytes 1572872 | tf_op jit(solution)/shard_map/ppermute | solution.py:321
  32.8 8.7 %keys_values.3 = (bf16[2048,2048]{1,0:T(8,128)(2,1)S(1)}, bf16[2048,256]{1,0:T(8,128)(2,1)S(1)}, bf16[2048,512]{1,0:T(8,128)(2,1)S(1)}, f32[8,2,128,128]{3,2,1,0...) custom-call(bf16[2048,2048]{1,0:T(8,128)(2,1)} %act.2, ...), custom_call_target="tpu_custom_call" | custom-call | flops 4294967296 | bytes 16777216 | tf_op jit(solution)/shard_map/keys_values/pallas_call | solution.py:267
  42.2 1.3 %collective-permute-start.10 = (bf16[2,144,128]{2,1,0:T(8,128)(2,1)S(1)}, bf16[2,144,128]{2,1,0:T(8,128)(2,1)S(1)}, u32[]{:S(2)}, u32[]{:S(2)}) collective-permute-start(bf16[2,144,128]{2,1,0:T(8,128)(2,1)S(1)} %get-tuple-element.66), channel_id=1, source_target_pairs={{0,12},{4,8},{8,4},{12,0},{1,13},{5,9},{9,5},{13,1},{2,14},{6,10},... | collective-permute-start | bytes 221192 | tf_op jit(solution)/shard_map/ppermute | solution.py:321
  44.1 2.6 %collective-permute-done.9.rest_1_ = bf16[2,144,128]{2,1,0:T(8,128)(2,1)S(1)} collective-permute-done((bf16[2,144,128]{2,1,0:T(8,128)(2,1)S(1)}, bf16[2,144,128]{2,1,0:T(8,128)(2,1)S(1)}, u32[]{:S(2)}, u32[]{:S(2)}) %collective-permute-start.9) | collective-permute-done | bytes 73760 | tf_op jit(solution)/shard_map/ppermute | solution.py:321
  48.7 2.3 %queries.3.q = bf16[2048,256]{1,0:T(8,128)(2,1)S(1)} custom-call(bf16[2048,2048]{1,0:T(8,128)(2,1)S(1)} %get-tuple-element.59.act, bf16[2048,256]{1,0:T(8,128)(2,1)S(1)} %get-tuple-element.60.w), custom_call_target="tpu_custom_call" | custom-call | flops 2147483648 | bytes 8388608 | tf_op jit(solution)/shard_map/queries/pallas_call | solution.py:288
  51.1 3.6 %attend.3 = bf16[4,512,256]{2,1,0:T(8,128)(2,1)} custom-call(bf16[2048,256]{1,0:T(8,128)(2,1)S(1)} %queries.3.q, bf16[2048,512]{1,0:T(8,128)(2,1)S(1)} %get-tuple-element.61.kv, f32[8,2,128,128]{3,2,1,0:T(8,128)S(1)} %get-tuple-element.62.before, f32[8,2,256,128]{3,2,1,0:T(8,128)S(1)} %get-tuple-element.63.spread, f32[8,8,256]{2,1,0:T(8,128)S(1)} %get-tuple-element.64.wrow, ...), custom_call_target="tpu_custom_call" | custom-call | flops 2684354560 | bytes 4194304 | tf_op jit(solution)/shard_map/attend/pallas_call | solution.py:303
  54.9 4.6 %all-to-all-start = ((bf16[4,512,256]{2,1,0:T(8,128)(2,1)}), bf16[4,512,256]{2,1,0:T(8,128)(2,1)S(1)}, u32[]{:S(2)}, u32[]{:S(2)}) async-start(bf16[4,512,256]{2,1,0:T(8,128)(2,1)} %attend.3), calls=%async_computation | async-start | bytes 2097152 | tf_op jit(solution)/shard_map/all_to_all | solution.py:421
  60.0 1.6 %collective-permute-done.11.rest_5_ = bf16[512,512]{1,0:T(8,128)(2,1)} collective-permute-done((bf16[512,512]{1,0:T(8,128)(2,1)S(1)}, bf16[512,512]{1,0:T(8,128)(2,1)}, u32[]{:S(2)}, u32[]{:S(2)}) %collective-permute-start.11) | collective-permute-done | bytes 524320 | tf_op jit(solution)/shard_map/ppermute | solution.py:321
  62.0 1.4 %collective-permute-start.13 = (bf16[512,512]{1,0:T(8,128)(2,1)}, bf16[512,512]{1,0:T(8,128)(2,1)}, u32[]{:S(2)}, u32[]{:S(2)}) collective-permute-start(bf16[512,512]{1,0:T(8,128)(2,1)} %collective-permute-done.7.rest_1_), channel_id=1, source_target_pairs={{0,8},{4,12},{8,0},{12,4},{1,9},{5,13},{9,1},{13,5},{2,10},{6,14},... | collective-permute-start | bytes 1572872 | tf_op jit(solution)/shard_map/ppermute | solution.py:321
  65.7 5.2 %project_out.2.rest_0_ = f32[4,512,512]{2,1,0:T(8,128)} custom-call(bf16[4,512,256]{2,1,0:T(8,128)(2,1)S(1)} %all-to-all-done.1.features, bf16[512,512]{1,0:T(8,128)(2,1)} %copy-done.3, bf16[512,512]{1,0:T(8,128)(2,1)} %copy-done.2, bf16[512,512]{1,0:T(8,128)(2,1)} %collective-permute-done.15.rest_2_, bf16[512,512]{1,0:T(8,128)(2,1)} %copy-done.6, ...), custom_call_target="tpu_custom_call" | custom-call | flops 2147483648 | bytes 8388608 | tf_op jit(solution)/shard_map/project_out/pallas_call | solution.py:374
  70.9 5.7 %collective-permute-done.13.rest_5_ = bf16[512,512]{1,0:T(8,128)(2,1)} collective-permute-done((bf16[512,512]{1,0:T(8,128)(2,1)}, bf16[512,512]{1,0:T(8,128)(2,1)}, u32[]{:S(2)}, u32[]{:S(2)}) %collective-permute-start.13) | collective-permute-done | bytes 524320 | tf_op jit(solution)/shard_map/ppermute | solution.py:321
  76.6 1.0 %collective-permute-done.14.rest_6_ = bf16[512,512]{1,0:T(8,128)(2,1)S(1)} collective-permute-done((bf16[512,512]{1,0:T(8,128)(2,1)}, bf16[512,512]{1,0:T(8,128)(2,1)S(1)}, u32[]{:S(2)}, u32[]{:S(2)}) %collective-permute-start.14) | collective-permute-done | bytes 524320 | tf_op jit(solution)/shard_map/ppermute | solution.py:321
  78.7 6.3 %all-to-all-done.features = bf16[4,512,256]{2,1,0:T(8,128)(2,1)S(1)} async-done(((bf16[4,512,256]{2,1,0:T(8,128)(2,1)}), bf16[4,512,256]{2,1,0:T(8,128)(2,1)S(1)}, u32[]{:S(2)}, u32[]{:S(2)}) %all-to-all-start) | async-done | bytes 1048608 | tf_op jit(solution)/shard_map/all_to_all | solution.py:421
  86.2 5.5 %project_out.3 = bf16[512,2048]{1,0:T(8,128)(2,1)} custom-call(bf16[4,512,256]{2,1,0:T(8,128)(2,1)S(1)} %all-to-all-done.features, f32[4,512,512]{2,1,0:T(8,128)} %project_out.2.rest_0_, bf16[512,512]{1,0:T(8,128)(2,1)} %collective-permute-done.7.rest_1_, bf16[512,512]{1,0:T(8,128)(2,1)} %collective-permute-done.12.rest_2_, bf16[512,512]{1,0:T(8,128)(2,1)} %copy-done.8, ...), custom_call_target="tpu_custom_call" | custom-call | flops 2147483648 | bytes 8388608 | tf_op jit(solution)/shard_map/project_out/pallas_call | solution.py:374
  (62 shorter events, 11.0 us)
Async XLA Ops:
  1.1 16.3 %collective-permute-start = (bf16[256,512]{1,0:T(8,128)(2,1)S(1)}, bf16[256,512]{1,0:T(8,128)(2,1)S(1)}, u32[]{:S(2)}, u32[]{:S(2)}) collective-permute-start(bf16[256,512]{1,0:T(8,128)(2,1)S(1)} %constant_dynamic-slice_fusion), channel_id=1, source_target_pairs={{0,1},{1,0},{2,3},{3,2},{4,5},{5,4},{6,7},{7,6},{8,9},{9,8},{10,11... | collective-permute-start | bytes 786440 | tf_op jit(solution)/shard_map/ppermute | solution.py:321
  4.2 14.3 %collective-permute-start.1 = (bf16[256,512]{1,0:T(8,128)(2,1)S(1)}, bf16[256,512]{1,0:T(8,128)(2,1)S(1)}, u32[]{:S(2)}, u32[]{:S(2)}) collective-permute-start(bf16[256,512]{1,0:T(8,128)(2,1)S(1)} %constant_dynamic-slice_fusion), channel_id=1, source_target_pairs={{0,2},{1,3},{2,0},{3,1},{4,6},{5,7},{6,4},{7,5},{8,10},{9,11},{10,... | collective-permute-start | bytes 786440 | tf_op jit(solution)/shard_map/ppermute | solution.py:321
  15.4 5.8 %collective-permute-start.2 = (bf16[2,144,128]{2,1,0:T(8,128)(2,1)S(1)}, bf16[2,144,128]{2,1,0:T(8,128)(2,1)S(1)}, u32[]{:S(2)}, u32[]{:S(2)}) collective-permute-start(bf16[2,144,128]{2,1,0:T(8,128)(2,1)S(1)} %get-tuple-element.51), channel_id=1, source_target_pairs={{0,4},{4,0},{8,12},{12,8},{1,5},{5,1},{9,13},{13,9},{2,6},{6,2},{1... | collective-permute-start | bytes 221192 | tf_op jit(solution)/shard_map/ppermute | solution.py:321
  15.5 5.8 %collective-permute-start.3 = (bf16[2,144,128]{2,1,0:T(8,128)(2,1)S(1)}, bf16[2,144,128]{2,1,0:T(8,128)(2,1)S(1)}, u32[]{:S(2)}, u32[]{:S(2)}) collective-permute-start(bf16[2,144,128]{2,1,0:T(8,128)(2,1)S(1)} %get-tuple-element.51), channel_id=1, source_target_pairs={{0,8},{4,12},{8,0},{12,4},{1,9},{5,13},{9,1},{13,5},{2,10},{6,14},... | collective-permute-start | bytes 221192 | tf_op jit(solution)/shard_map/ppermute | solution.py:321
  17.1 4.5 %collective-permute-start.4 = (bf16[2,144,128]{2,1,0:T(8,128)(2,1)S(1)}, bf16[2,144,128]{2,1,0:T(8,128)(2,1)S(1)}, u32[]{:S(2)}, u32[]{:S(2)}) collective-permute-start(bf16[2,144,128]{2,1,0:T(8,128)(2,1)S(1)} %get-tuple-element.51), channel_id=1, source_target_pairs={{0,12},{4,8},{8,4},{12,0},{1,13},{5,9},{9,5},{13,1},{2,14},{6,10},... | collective-permute-start | bytes 221192 | tf_op jit(solution)/shard_map/ppermute | solution.py:321
  18.5 7.5 %collective-permute-start.5 = (bf16[256,512]{1,0:T(8,128)(2,1)S(1)}, bf16[256,512]{1,0:T(8,128)(2,1)S(1)}, u32[]{:S(2)}, u32[]{:S(2)}) collective-permute-start(bf16[256,512]{1,0:T(8,128)(2,1)S(1)} %collective-permute-done.1), channel_id=1, source_target_pairs={{0,1},{1,0},{2,3},{3,2},{4,5},{5,4},{6,7},{7,6},{8,9},{9,8},{10,11... | collective-permute-start | bytes 786440 | tf_op jit(solution)/shard_map/ppermute | solution.py:321
  26.0 29.0 %all-to-all-start.1 = ((bf16[4,512,256]{2,1,0:T(8,128)(2,1)}), bf16[4,512,256]{2,1,0:T(8,128)(2,1)S(1)}, u32[]{:S(2)}, u32[]{:S(2)}) async-start(bf16[4,512,256]{2,1,0:T(8,128)(2,1)} %attend.2), calls=%async_computation.1 | async-start | bytes 2097152 | tf_op jit(solution)/shard_map/all_to_all | solution.py:421
  29.7 13.8 %collective-permute-start.6 = (bf16[512,512]{1,0:T(8,128)(2,1)S(1)}, bf16[512,512]{1,0:T(8,128)(2,1)S(1)}, u32[]{:S(2)}, u32[]{:S(2)}) collective-permute-start(bf16[512,512]{1,0:T(8,128)(2,1)S(1)} %constant_dynamic-update-slice_fusion.rest_0_), channel_id=1, source_target_pairs={{0,8},{4,12},{8,0},{12,4},{1,9},{5,13},{9,1},{13,5},{2,10},{6,14},... | collective-permute-start | bytes 1572872 | tf_op jit(solution)/shard_map/ppermute | solution.py:321
  31.3 12.9 %collective-permute-start.7 = (bf16[512,512]{1,0:T(8,128)(2,1)S(1)}, bf16[512,512]{1,0:T(8,128)(2,1)}, u32[]{:S(2)}, u32[]{:S(2)}) collective-permute-start(bf16[512,512]{1,0:T(8,128)(2,1)S(1)} %constant_dynamic-update-slice_fusion.rest_0_), channel_id=1, source_target_pairs={{0,16},{16,0},{1,17},{17,1},{2,18},{18,2},{3,19},{19,3},{4,20},{20... | collective-permute-start | bytes 1572872 | tf_op jit(solution)/shard_map/ppermute | solution.py:321
  41.5 2.6 %collective-permute-start.8 = (bf16[2,144,128]{2,1,0:T(8,128)(2,1)S(1)}, bf16[2,144,128]{2,1,0:T(8,128)(2,1)S(1)}, u32[]{:S(2)}, u32[]{:S(2)}) collective-permute-start(bf16[2,144,128]{2,1,0:T(8,128)(2,1)S(1)} %get-tuple-element.66), channel_id=1, source_target_pairs={{0,4},{4,0},{8,12},{12,8},{1,5},{5,1},{9,13},{13,9},{2,6},{6,2},{1... | collective-permute-start | bytes 221192 | tf_op jit(solution)/shard_map/ppermute | solution.py:321
  41.6 5.1 %collective-permute-start.9 = (bf16[2,144,128]{2,1,0:T(8,128)(2,1)S(1)}, bf16[2,144,128]{2,1,0:T(8,128)(2,1)S(1)}, u32[]{:S(2)}, u32[]{:S(2)}) collective-permute-start(bf16[2,144,128]{2,1,0:T(8,128)(2,1)S(1)} %get-tuple-element.66), channel_id=1, source_target_pairs={{0,8},{4,12},{8,0},{12,4},{1,9},{5,13},{9,1},{13,5},{2,10},{6,14},... | collective-permute-start | bytes 221192 | tf_op jit(solution)/shard_map/ppermute | solution.py:321
  42.2 5.2 %collective-permute-start.10 = (bf16[2,144,128]{2,1,0:T(8,128)(2,1)S(1)}, bf16[2,144,128]{2,1,0:T(8,128)(2,1)S(1)}, u32[]{:S(2)}, u32[]{:S(2)}) collective-permute-start(bf16[2,144,128]{2,1,0:T(8,128)(2,1)S(1)} %get-tuple-element.66), channel_id=1, source_target_pairs={{0,12},{4,8},{8,4},{12,0},{1,13},{5,9},{9,5},{13,1},{2,14},{6,10},... | collective-permute-start | bytes 221192 | tf_op jit(solution)/shard_map/ppermute | solution.py:321
  43.5 19.8 %collective-permute-start.15 = (bf16[512,512]{1,0:T(8,128)(2,1)S(1)}, bf16[512,512]{1,0:T(8,128)(2,1)}, u32[]{:S(2)}, u32[]{:S(2)}) collective-permute-start(bf16[512,512]{1,0:T(8,128)(2,1)S(1)} %constant_dynamic-update-slice_fusion.rest_0_), channel_id=1, source_target_pairs={{0,4},{4,0},{8,12},{12,8},{1,5},{5,1},{9,13},{13,9},{2,6},{6,2},{1... | collective-permute-start | bytes 1572872 | tf_op jit(solution)/shard_map/ppermute | solution.py:321
  47.4 14.2 %collective-permute-start.11 = (bf16[512,512]{1,0:T(8,128)(2,1)S(1)}, bf16[512,512]{1,0:T(8,128)(2,1)}, u32[]{:S(2)}, u32[]{:S(2)}) collective-permute-start(bf16[512,512]{1,0:T(8,128)(2,1)S(1)} %pad_maximum_fusion.rest_1_), channel_id=1, source_target_pairs={{0,8},{4,12},{8,0},{12,4},{1,9},{5,13},{9,1},{13,5},{2,10},{6,14},... | collective-permute-start | bytes 1572872 | tf_op jit(solution)/shard_map/ppermute | solution.py:321
  48.2 13.8 %collective-permute-start.12 = (bf16[512,512]{1,0:T(8,128)(2,1)S(1)}, bf16[512,512]{1,0:T(8,128)(2,1)}, u32[]{:S(2)}, u32[]{:S(2)}) collective-permute-start(bf16[512,512]{1,0:T(8,128)(2,1)S(1)} %pad_maximum_fusion.rest_1_), channel_id=1, source_target_pairs={{0,16},{16,0},{1,17},{17,1},{2,18},{18,2},{3,19},{19,3},{4,20},{20... | collective-permute-start | bytes 1572872 | tf_op jit(solution)/shard_map/ppermute | solution.py:321
  54.9 30.0 %all-to-all-start = ((bf16[4,512,256]{2,1,0:T(8,128)(2,1)}), bf16[4,512,256]{2,1,0:T(8,128)(2,1)S(1)}, u32[]{:S(2)}, u32[]{:S(2)}) async-start(bf16[4,512,256]{2,1,0:T(8,128)(2,1)} %attend.3), calls=%async_computation | async-start | bytes 2097152 | tf_op jit(solution)/shard_map/all_to_all | solution.py:421
  59.5 4.3 %collective-permute-start.16 = (bf16[512,512]{1,0:T(8,128)(2,1)S(1)}, bf16[512,512]{1,0:T(8,128)(2,1)S(1)}, u32[]{:S(2)}, u32[]{:S(2)}) collective-permute-start(bf16[512,512]{1,0:T(8,128)(2,1)S(1)} %pad_maximum_fusion.rest_1_), channel_id=1, source_target_pairs={{0,4},{4,0},{8,12},{12,8},{1,5},{5,1},{9,13},{13,9},{2,6},{6,2},{1... | collective-permute-start | bytes 1572872 | tf_op jit(solution)/shard_map/ppermute | solution.py:321
  59.5 4.3 %collective-permute-start.17 = (bf16[512,512]{1,0:T(8,128)(2,1)}, bf16[512,512]{1,0:T(8,128)(2,1)S(1)}, u32[]{:S(2)}, u32[]{:S(2)}) collective-permute-start(bf16[512,512]{1,0:T(8,128)(2,1)} %copy-done.4), channel_id=1, source_target_pairs={{0,4},{4,0},{8,12},{12,8},{1,5},{5,1},{9,13},{13,9},{2,6},{6,2},{1... | collective-permute-start | bytes 1572872 | tf_op jit(solution)/shard_map/ppermute | solution.py:321
  62.0 14.7 %collective-permute-start.13 = (bf16[512,512]{1,0:T(8,128)(2,1)}, bf16[512,512]{1,0:T(8,128)(2,1)}, u32[]{:S(2)}, u32[]{:S(2)}) collective-permute-start(bf16[512,512]{1,0:T(8,128)(2,1)} %collective-permute-done.7.rest_1_), channel_id=1, source_target_pairs={{0,8},{4,12},{8,0},{12,4},{1,9},{5,13},{9,1},{13,5},{2,10},{6,14},... | collective-permute-start | bytes 1572872 | tf_op jit(solution)/shard_map/ppermute | solution.py:321
  63.4 14.3 %collective-permute-start.14 = (bf16[512,512]{1,0:T(8,128)(2,1)}, bf16[512,512]{1,0:T(8,128)(2,1)S(1)}, u32[]{:S(2)}, u32[]{:S(2)}) collective-permute-start(bf16[512,512]{1,0:T(8,128)(2,1)} %collective-permute-done.11.rest_5_), channel_id=1, source_target_pairs={{0,16},{16,0},{1,17},{17,1},{2,18},{18,2},{3,19},{19,3},{4,20},{20... | collective-permute-start | bytes 1572872 | tf_op jit(solution)/shard_map/ppermute | solution.py:321
  77.6 7.3 %collective-permute-start.19 = (bf16[512,512]{1,0:T(8,128)(2,1)}, bf16[512,512]{1,0:T(8,128)(2,1)S(1)}, u32[]{:S(2)}, u32[]{:S(2)}) collective-permute-start(bf16[512,512]{1,0:T(8,128)(2,1)} %collective-permute-done.7.rest_1_), channel_id=1, source_target_pairs={{0,4},{4,0},{8,12},{12,8},{1,5},{5,1},{9,13},{13,9},{2,6},{6,2},{1... | collective-permute-start | bytes 1572872 | tf_op jit(solution)/shard_map/ppermute | solution.py:321
  77.6 7.3 %collective-permute-start.20 = (bf16[512,512]{1,0:T(8,128)(2,1)}, bf16[512,512]{1,0:T(8,128)(2,1)S(1)}, u32[]{:S(2)}, u32[]{:S(2)}) collective-permute-start(bf16[512,512]{1,0:T(8,128)(2,1)} %collective-permute-done.12.rest_2_), channel_id=1, source_target_pairs={{0,4},{4,0},{8,12},{12,8},{1,5},{5,1},{9,13},{13,9},{2,6},{6,2},{1... | collective-permute-start | bytes 1572872 | tf_op jit(solution)/shard_map/ppermute | solution.py:321
  78.1 6.9 %collective-permute-start.21 = (bf16[512,512]{1,0:T(8,128)(2,1)}, bf16[512,512]{1,0:T(8,128)(2,1)S(1)}, u32[]{:S(2)}, u32[]{:S(2)}) collective-permute-start(bf16[512,512]{1,0:T(8,128)(2,1)} %collective-permute-done.13.rest_5_), channel_id=1, source_target_pairs={{0,4},{4,0},{8,12},{12,8},{1,5},{5,1},{9,13},{13,9},{2,6},{6,2},{1... | collective-permute-start | bytes 1572872 | tf_op jit(solution)/shard_map/ppermute | solution.py:321
  78.1 6.9 %collective-permute-start.22 = (bf16[512,512]{1,0:T(8,128)(2,1)S(1)}, bf16[512,512]{1,0:T(8,128)(2,1)}, u32[]{:S(2)}, u32[]{:S(2)}) collective-permute-start(bf16[512,512]{1,0:T(8,128)(2,1)S(1)} %collective-permute-done.14.rest_6_), channel_id=1, source_target_pairs={{0,4},{4,0},{8,12},{12,8},{1,5},{5,1},{9,13},{13,9},{2,6},{6,2},{1... | collective-permute-start | bytes 1572872 | tf_op jit(solution)/shard_map/ppermute | solution.py:321
  (13 other events, 56.6 us)

commit v5 on v4

--- a/solution.py
+++ b/solution.py
@@ -34,8 +34,10 @@
     half, tokens = decay.shape[0] // 2, decay.shape[1]
     blocks = tokens // BLOCK
     wide = half * DH
-    chunks = [(0, BLOCK), (BLOCK, STEP - BLOCK)]
-    chunks += [(start, STEP) for start in range(STEP, tokens, STEP)]
+    chunks = [(0, BLOCK)]
+    while sum(chunks[-1]) < tokens:
+        start = sum(chunks[-1])
+        chunks.append((start, min(start, tokens - start)))
 
     def load_rows(start, size):
         rows = pl.ds(start, size)
@@ -274,7 +276,7 @@
             pltpu.VMEM((2 * heads, tokens), F32),
             pltpu.VMEM((heads, DH, DH), F32),
             pltpu.VMEM((blocks, BLOCK, 8), F32),
-            pltpu.SemaphoreType.DMA((tokens // STEP + 8,)),
+            pltpu.SemaphoreType.DMA((tokens // BLOCK + 4,)),
         ],
         compiler_params=pltpu.CompilerParams(vmem_limit_bytes=16 * MIB),
         cost_estimate=cost(4 * tokens * width * columns, 4 * tokens * width),
@@ -419,7 +421,7 @@
             ]
             across, beside = swap(even, "seq", 2), swap(even, "grp", 1)
         features.append(lax.all_to_all(normed, "head", 0, 0))
-    found = gather_columns(even, odd, across, beside, arrivals)
+    found = gather_columns(even, odd, across, beside, [query, *arrivals])
     first = {(g, s): parts for (g, s), parts in found.items() if g == 0}
     begun = project_out(features[0], 0, gather_partner(first), order)
     second = {(g, s): parts for (g, s), parts in found.items() if g == 1}

time: 92.1 us -> 89.2 us (0.969)
  waiting for transfers between devices: 21 us -> 18.4 us
  Pallas kernels: 39.9 us -> 38.9 us
    all_to_all x2, waiting for transfers between devices: 6.53 us -> 3.59 us  [on_device(): features.append(lax.all_to_all(normed, 'head', 0, 0))]
    ppermute x23, starting transfers between devices: 18.3 us -> 19.8 us  [swap(): return lax.ppermute(value, axis, [(i, i ^ bit) for i in range(count)])]
    unnamed x25 -> x31, local copies, waits for them, and re-layouts: 3.83 us -> 3.74 us
  transfers between devices with their start and end apart: 25 -> 25, of which waited for: 13 -> 11; matrix products, arithmetic and copies ran while one was open for 0% -> 0% of each run, Pallas kernels for 38% -> 38%
where the time goes in v5:
time: 89.2 us; the launch traced here: 88.9 us
  Pallas kernels  38.9 us (44%)
  starting transfers between devices  27.3 us (31%)
  waiting for transfers between devices  18.4 us (21%)
  local copies, waits for them, and re-layouts  3.78 us (4%)
    ppermute x23, starting transfers between devices, swap(): return lax.ppermute(value, axis, [(i, i ^ bit) for i in range(count)])  19.8 us
    pallas_call x2, Pallas kernels, keys_values(): pl.pallas_call(functools.partial(kv_kernel, part), in_specs=[in_hbm()] *...  16.6 us
    ppermute x23, waiting for transfers between devices, swap(): return lax.ppermute(value, axis, [(i, i ^ bit) for i in range(count)])  14.8 us
    pallas_call x2, Pallas kernels, project_out(): pl.pallas_call(functools.partial(out_kernel, offsets, order, bool(lead)),...  10.7 us
    all_to_all x2, starting transfers between devices, on_device(): features.append(lax.all_to_all(normed, 'head', 0, 0))  7.43 us
    pallas_call x2, Pallas kernels, attend(): pl.pallas_call(functools.partial(attend_kernel, received), in_specs=[in_v...  7.03 us
    pallas_call x2, Pallas kernels, queries(): pl.pallas_call(project_kernel, in_specs=[in_vmem()] * 2, out_specs=in_vme...  4.65 us
    unnamed x31, local copies, waits for them, and re-layouts  3.74 us
  transfers between devices with their start and end apart: 25, of which 11 were waited for; matrix products, arithmetic and copies ran while one was open for 0% of the time, Pallas kernels for 38%

profile of v5, /device:TPU:0, one launch (start us, length us, event | category | flops | bytes accessed | tf_op | source)
XLA Modules:
  0.0 88.9 jit_solution(10407593226176724397)
XLA Ops:
  1.1 3.1 %collective-permute-start = (bf16[256,512]{1,0:T(8,128)(2,1)S(1)}, bf16[256,512]{1,0:T(8,128)(2,1)S(1)}, u32[]{:S(2)}, u32[]{:S(2)}) collective-permute-start(bf16[256,512]{1,0:T(8,128)(2,1)S(1)} %constant_dynamic-slice_fusion), channel_id=1, source_target_pairs={{0,1},{1,0},{2,3},{3,2},{4,5},{5,4},{6,7},{7,6},{8,9},{9,8},{10,11... | collective-permute-start | bytes 786440 | tf_op jit(solution)/shard_map/ppermute | solution.py:323
  4.2 2.6 %collective-permute-start.1 = (bf16[256,512]{1,0:T(8,128)(2,1)S(1)}, bf16[256,512]{1,0:T(8,128)(2,1)S(1)}, u32[]{:S(2)}, u32[]{:S(2)}) collective-permute-start(bf16[256,512]{1,0:T(8,128)(2,1)S(1)} %constant_dynamic-slice_fusion), channel_id=1, source_target_pairs={{0,2},{1,3},{2,0},{3,1},{4,6},{5,7},{6,4},{7,5},{8,10},{9,11},{10,... | collective-permute-start | bytes 786440 | tf_op jit(solution)/shard_map/ppermute | solution.py:323
  6.7 8.3 %keys_values.2 = (bf16[2048,2048]{1,0:T(8,128)(2,1)S(1)}, bf16[2048,256]{1,0:T(8,128)(2,1)S(1)}, bf16[2048,512]{1,0:T(8,128)(2,1)S(1)}, f32[8,2,128,128]{3,2,1,0...) custom-call(bf16[2048,2048]{1,0:T(8,128)(2,1)} %act.2, ...), custom_call_target="tpu_custom_call" | custom-call | flops 4294967296 | bytes 16777216 | tf_op jit(solution)/shard_map/keys_values/pallas_call | solution.py:269
  15.1 1.6 %collective-permute-start.3 = (bf16[2,144,128]{2,1,0:T(8,128)(2,1)S(1)}, bf16[2,144,128]{2,1,0:T(8,128)(2,1)S(1)}, u32[]{:S(2)}, u32[]{:S(2)}) collective-permute-start(bf16[2,144,128]{2,1,0:T(8,128)(2,1)S(1)} %get-tuple-element.51), channel_id=1, source_target_pairs={{0,8},{4,12},{8,0},{12,4},{1,9},{5,13},{9,1},{13,5},{2,10},{6,14},... | collective-permute-start | bytes 221192 | tf_op jit(solution)/shard_map/ppermute | solution.py:323
  17.0 1.5 %collective-permute-done.1 = bf16[256,512]{1,0:T(8,128)(2,1)S(1)} collective-permute-done((bf16[256,512]{1,0:T(8,128)(2,1)S(1)}, bf16[256,512]{1,0:T(8,128)(2,1)S(1)}, u32[]{:S(2)}, u32[]{:S(2)}) %collective-permute-start.1) | collective-permute-done | bytes 262176 | tf_op jit(solution)/shard_map/ppermute | solution.py:323
  18.9 2.3 %queries.2.q = bf16[2048,256]{1,0:T(8,128)(2,1)S(1)} custom-call(bf16[2048,2048]{1,0:T(8,128)(2,1)S(1)} %get-tuple-element.44.act, bf16[2048,256]{1,0:T(8,128)(2,1)S(1)} %get-tuple-element.45.w), custom_call_target="tpu_custom_call" | custom-call | flops 2147483648 | bytes 8388608 | tf_op jit(solution)/shard_map/queries/pallas_call | solution.py:290
  21.3 3.5 %attend.2 = bf16[4,512,256]{2,1,0:T(8,128)(2,1)} custom-call(bf16[2048,256]{1,0:T(8,128)(2,1)S(1)} %queries.2.q, bf16[2048,512]{1,0:T(8,128)(2,1)S(1)} %get-tuple-element.46.kv, f32[8,2,128,128]{3,2,1,0:T(8,128)S(1)} %get-tuple-element.47.before, f32[8,2,256,128]{3,2,1,0:T(8,128)S(1)} %get-tuple-element.48.spread, f32[8,8,256]{2,1,0:T(8,128)S(1)} %get-tuple-element.49.wrow, ...), custom_call_target="tpu_custom_call" | custom-call | flops 2684354560 | bytes 4194304 | tf_op jit(solution)/shard_map/attend/pallas_call | solution.py:305
  25.5 3.7 %all-to-all-start.1 = ((bf16[4,512,256]{2,1,0:T(8,128)(2,1)}), bf16[4,512,256]{2,1,0:T(8,128)(2,1)S(1)}, u32[]{:S(2)}, u32[]{:S(2)}) async-start(bf16[4,512,256]{2,1,0:T(8,128)(2,1)} %attend.2), calls=%async_computation.1 | async-start | bytes 2097152 | tf_op jit(solution)/shard_map/all_to_all | solution.py:423
  29.3 1.6 %collective-permute-start.6 = (bf16[512,512]{1,0:T(8,128)(2,1)S(1)}, bf16[512,512]{1,0:T(8,128)(2,1)S(1)}, u32[]{:S(2)}, u32[]{:S(2)}) collective-permute-start(bf16[512,512]{1,0:T(8,128)(2,1)S(1)} %constant_dynamic-update-slice_fusion.rest_0_), channel_id=1, source_target_pairs={{0,8},{4,12},{8,0},{12,4},{1,9},{5,13},{9,1},{13,5},{2,10},{6,14},... | collective-permute-start | bytes 1572872 | tf_op jit(solution)/shard_map/ppermute | solution.py:323
  30.9 1.5 %collective-permute-start.7 = (bf16[512,512]{1,0:T(8,128)(2,1)S(1)}, bf16[512,512]{1,0:T(8,128)(2,1)S(1)}, u32[]{:S(2)}, u32[]{:S(2)}) collective-permute-start(bf16[512,512]{1,0:T(8,128)(2,1)S(1)} %constant_dynamic-update-slice_fusion.rest_0_), channel_id=1, source_target_pairs={{0,16},{16,0},{1,17},{17,1},{2,18},{18,2},{3,19},{19,3},{4,20},{20... | collective-permute-start | bytes 1572872 | tf_op jit(solution)/shard_map/ppermute | solution.py:323
  32.4 8.3 %keys_values.3 = (bf16[2048,2048]{1,0:T(8,128)(2,1)S(1)}, bf16[2048,256]{1,0:T(8,128)(2,1)S(1)}, bf16[2048,512]{1,0:T(8,128)(2,1)S(1)}, f32[8,2,128,128]{3,2,1,0...) custom-call(bf16[2048,2048]{1,0:T(8,128)(2,1)} %act.2, ...), custom_call_target="tpu_custom_call" | custom-call | flops 4294967296 | bytes 16777216 | tf_op jit(solution)/shard_map/keys_values/pallas_call | solution.py:269
  41.4 1.5 %collective-permute-start.9 = (bf16[2,144,128]{2,1,0:T(8,128)(2,1)S(1)}, bf16[2,144,128]{2,1,0:T(8,128)(2,1)S(1)}, u32[]{:S(2)}, u32[]{:S(2)}) collective-permute-start(bf16[2,144,128]{2,1,0:T(8,128)(2,1)S(1)} %get-tuple-element.66), channel_id=1, source_target_pairs={{0,8},{4,12},{8,0},{12,4},{1,9},{5,13},{9,1},{13,5},{2,10},{6,14},... | collective-permute-start | bytes 221192 | tf_op jit(solution)/shard_map/ppermute | solution.py:323
  44.4 2.3 %queries.3.q = bf16[2048,256]{1,0:T(8,128)(2,1)S(1)} custom-call(bf16[2048,2048]{1,0:T(8,128)(2,1)S(1)} %get-tuple-element.59.act, bf16[2048,256]{1,0:T(8,128)(2,1)S(1)} %get-tuple-element.60.w), custom_call_target="tpu_custom_call" | custom-call | flops 2147483648 | bytes 8388608 | tf_op jit(solution)/shard_map/queries/pallas_call | solution.py:290
  47.5 2.0 %collective-permute-start.12 = (bf16[512,512]{1,0:T(8,128)(2,1)S(1)}, bf16[512,512]{1,0:T(8,128)(2,1)}, u32[]{:S(2)}, u32[]{:S(2)}) collective-permute-start(bf16[512,512]{1,0:T(8,128)(2,1)S(1)} %pad_maximum_fusion.rest_1_), channel_id=1, source_target_pairs={{0,16},{16,0},{1,17},{17,1},{2,18},{18,2},{3,19},{19,3},{4,20},{20... | collective-permute-start | bytes 1572872 | tf_op jit(solution)/shard_map/ppermute | solution.py:323
  49.5 3.5 %attend.3 = bf16[4,512,256]{2,1,0:T(8,128)(2,1)} custom-call(bf16[2048,256]{1,0:T(8,128)(2,1)S(1)} %queries.3.q, bf16[2048,512]{1,0:T(8,128)(2,1)S(1)} %get-tuple-element.61.kv, f32[8,2,128,128]{3,2,1,0:T(8,128)S(1)} %get-tuple-element.62.before, f32[8,2,256,128]{3,2,1,0:T(8,128)S(1)} %get-tuple-element.63.spread, f32[8,8,256]{2,1,0:T(8,128)S(1)} %get-tuple-element.64.wrow, ...), custom_call_target="tpu_custom_call" | custom-call | flops 2684354560 | bytes 4194304 | tf_op jit(solution)/shard_map/attend/pallas_call | solution.py:305
  53.0 1.4 %all-to-all-done.1.features = bf16[4,512,256]{2,1,0:T(8,128)(2,1)S(1)} async-done(((bf16[4,512,256]{2,1,0:T(8,128)(2,1)}), bf16[4,512,256]{2,1,0:T(8,128)(2,1)S(1)}, u32[]{:S(2)}, u32[]{:S(2)}) %all-to-all-start.1) | async-done | bytes 1048608 | tf_op jit(solution)/shard_map/all_to_all | solution.py:423
  54.5 3.7 %all-to-all-start = ((bf16[4,512,256]{2,1,0:T(8,128)(2,1)}), bf16[4,512,256]{2,1,0:T(8,128)(2,1)S(1)}, u32[]{:S(2)}, u32[]{:S(2)}) async-start(bf16[4,512,256]{2,1,0:T(8,128)(2,1)} %attend.3), calls=%async_computation | async-start | bytes 2097152 | tf_op jit(solution)/shard_map/all_to_all | solution.py:423
  58.8 1.9 %collective-permute-done.11.rest_5_ = bf16[512,512]{1,0:T(8,128)(2,1)} collective-permute-done((bf16[512,512]{1,0:T(8,128)(2,1)S(1)}, bf16[512,512]{1,0:T(8,128)(2,1)}, u32[]{:S(2)}, u32[]{:S(2)}) %collective-permute-start.11) | collective-permute-done | bytes 524320 | tf_op jit(solution)/shard_map/ppermute | solution.py:323
  62.5 1.3 %collective-permute-start.14 = (bf16[512,512]{1,0:T(8,128)(2,1)}, bf16[512,512]{1,0:T(8,128)(2,1)S(1)}, u32[]{:S(2)}, u32[]{:S(2)}) collective-permute-start(bf16[512,512]{1,0:T(8,128)(2,1)} %collective-permute-done.11.rest_5_), channel_id=1, source_target_pairs={{0,16},{16,0},{1,17},{17,1},{2,18},{18,2},{3,19},{19,3},{4,20},{20... | collective-permute-start | bytes 1572872 | tf_op jit(solution)/shard_map/ppermute | solution.py:323
  65.7 5.2 %project_out.2.rest_0_ = f32[4,512,512]{2,1,0:T(8,128)} custom-call(bf16[4,512,256]{2,1,0:T(8,128)(2,1)S(1)} %all-to-all-done.1.features, bf16[512,512]{1,0:T(8,128)(2,1)} %copy-done.3, bf16[512,512]{1,0:T(8,128)(2,1)} %copy-done.2, bf16[512,512]{1,0:T(8,128)(2,1)} %collective-permute-done.15.rest_2_, bf16[512,512]{1,0:T(8,128)(2,1)} %copy-done.9, ...), custom_call_target="tpu_custom_call" | custom-call | flops 2147483648 | bytes 8388608 | tf_op jit(solution)/shard_map/project_out/pallas_call | solution.py:376
  70.9 5.3 %collective-permute-done.13.rest_5_ = bf16[512,512]{1,0:T(8,128)(2,1)S(1)} collective-permute-done((bf16[512,512]{1,0:T(8,128)(2,1)}, bf16[512,512]{1,0:T(8,128)(2,1)S(1)}, u32[]{:S(2)}, u32[]{:S(2)}) %collective-permute-start.13) | collective-permute-done | bytes 524320 | tf_op jit(solution)/shard_map/ppermute | solution.py:323
  78.7 2.3 %collective-permute-done.20.rest_4_ = bf16[512,512]{1,0:T(8,128)(2,1)S(1)} collective-permute-done((bf16[512,512]{1,0:T(8,128)(2,1)}, bf16[512,512]{1,0:T(8,128)(2,1)S(1)}, u32[]{:S(2)}, u32[]{:S(2)}) %collective-permute-start.20) | collective-permute-done | bytes 524320 | tf_op jit(solution)/shard_map/ppermute | solution.py:323
  81.0 2.1 %all-to-all-done.features = bf16[4,512,256]{2,1,0:T(8,128)(2,1)S(1)} async-done(((bf16[4,512,256]{2,1,0:T(8,128)(2,1)}), bf16[4,512,256]{2,1,0:T(8,128)(2,1)S(1)}, u32[]{:S(2)}, u32[]{:S(2)}) %all-to-all-start) | async-done | bytes 1048608 | tf_op jit(solution)/shard_map/all_to_all | solution.py:423
  83.2 5.5 %project_out.3 = bf16[512,2048]{1,0:T(8,128)(2,1)} custom-call(bf16[4,512,256]{2,1,0:T(8,128)(2,1)S(1)} %all-to-all-done.features, f32[4,512,512]{2,1,0:T(8,128)} %project_out.2.rest_0_, bf16[512,512]{1,0:T(8,128)(2,1)} %copy-done.4, bf16[512,512]{1,0:T(8,128)(2,1)} %collective-permute-done.12.rest_2_, bf16[512,512]{1,0:T(8,128)(2,1)} %copy-done.11, ...), custom_call_target="tpu_custom_call" | custom-call | flops 2147483648 | bytes 8388608 | tf_op jit(solution)/shard_map/project_out/pallas_call | solution.py:376
  (68 shorter events, 12.2 us)
Async XLA Ops:
  1.1 15.9 %collective-permute-start = (bf16[256,512]{1,0:T(8,128)(2,1)S(1)}, bf16[256,512]{1,0:T(8,128)(2,1)S(1)}, u32[]{:S(2)}, u32[]{:S(2)}) collective-permute-start(bf16[256,512]{1,0:T(8,128)(2,1)S(1)} %constant_dynamic-slice_fusion), channel_id=1, source_target_pairs={{0,1},{1,0},{2,3},{3,2},{4,5},{5,4},{6,7},{7,6},{8,9},{9,8},{10,11... | collective-permute-start | bytes 786440 | tf_op jit(solution)/shard_map/ppermute | solution.py:323
  4.2 14.3 %collective-permute-start.1 = (bf16[256,512]{1,0:T(8,128)(2,1)S(1)}, bf16[256,512]{1,0:T(8,128)(2,1)S(1)}, u32[]{:S(2)}, u32[]{:S(2)}) collective-permute-start(bf16[256,512]{1,0:T(8,128)(2,1)S(1)} %constant_dynamic-slice_fusion), channel_id=1, source_target_pairs={{0,2},{1,3},{2,0},{3,1},{4,6},{5,7},{6,4},{7,5},{8,10},{9,11},{10,... | collective-permute-start | bytes 786440 | tf_op jit(solution)/shard_map/ppermute | solution.py:323
  15.0 6.2 %collective-permute-start.2 = (bf16[2,144,128]{2,1,0:T(8,128)(2,1)S(1)}, bf16[2,144,128]{2,1,0:T(8,128)(2,1)S(1)}, u32[]{:S(2)}, u32[]{:S(2)}) collective-permute-start(bf16[2,144,128]{2,1,0:T(8,128)(2,1)S(1)} %get-tuple-element.51), channel_id=1, source_target_pairs={{0,4},{4,0},{8,12},{12,8},{1,5},{5,1},{9,13},{13,9},{2,6},{6,2},{1... | collective-permute-start | bytes 221192 | tf_op jit(solution)/shard_map/ppermute | solution.py:323
  15.1 6.2 %collective-permute-start.3 = (bf16[2,144,128]{2,1,0:T(8,128)(2,1)S(1)}, bf16[2,144,128]{2,1,0:T(8,128)(2,1)S(1)}, u32[]{:S(2)}, u32[]{:S(2)}) collective-permute-start(bf16[2,144,128]{2,1,0:T(8,128)(2,1)S(1)} %get-tuple-element.51), channel_id=1, source_target_pairs={{0,8},{4,12},{8,0},{12,4},{1,9},{5,13},{9,1},{13,5},{2,10},{6,14},... | collective-permute-start | bytes 221192 | tf_op jit(solution)/shard_map/ppermute | solution.py:323
  16.7 4.6 %collective-permute-start.4 = (bf16[2,144,128]{2,1,0:T(8,128)(2,1)S(1)}, bf16[2,144,128]{2,1,0:T(8,128)(2,1)S(1)}, u32[]{:S(2)}, u32[]{:S(2)}) collective-permute-start(bf16[2,144,128]{2,1,0:T(8,128)(2,1)S(1)} %get-tuple-element.51), channel_id=1, source_target_pairs={{0,12},{4,8},{8,4},{12,0},{1,13},{5,9},{9,5},{13,1},{2,14},{6,10},... | collective-permute-start | bytes 221192 | tf_op jit(solution)/shard_map/ppermute | solution.py:323
  18.5 7.1 %collective-permute-start.5 = (bf16[256,512]{1,0:T(8,128)(2,1)S(1)}, bf16[256,512]{1,0:T(8,128)(2,1)S(1)}, u32[]{:S(2)}, u32[]{:S(2)}) collective-permute-start(bf16[256,512]{1,0:T(8,128)(2,1)S(1)} %collective-permute-done.1), channel_id=1, source_target_pairs={{0,1},{1,0},{2,3},{3,2},{4,5},{5,4},{6,7},{7,6},{8,9},{9,8},{10,11... | collective-permute-start | bytes 786440 | tf_op jit(solution)/shard_map/ppermute | solution.py:323
  25.5 28.9 %all-to-all-start.1 = ((bf16[4,512,256]{2,1,0:T(8,128)(2,1)}), bf16[4,512,256]{2,1,0:T(8,128)(2,1)S(1)}, u32[]{:S(2)}, u32[]{:S(2)}) async-start(bf16[4,512,256]{2,1,0:T(8,128)(2,1)} %attend.2), calls=%async_computation.1 | async-start | bytes 2097152 | tf_op jit(solution)/shard_map/all_to_all | solution.py:423
  29.3 13.6 %collective-permute-start.6 = (bf16[512,512]{1,0:T(8,128)(2,1)S(1)}, bf16[512,512]{1,0:T(8,128)(2,1)S(1)}, u32[]{:S(2)}, u32[]{:S(2)}) collective-permute-start(bf16[512,512]{1,0:T(8,128)(2,1)S(1)} %constant_dynamic-update-slice_fusion.rest_0_), channel_id=1, source_target_pairs={{0,8},{4,12},{8,0},{12,4},{1,9},{5,13},{9,1},{13,5},{2,10},{6,14},... | collective-permute-start | bytes 1572872 | tf_op jit(solution)/shard_map/ppermute | solution.py:323
  30.9 12.8 %collective-permute-start.7 = (bf16[512,512]{1,0:T(8,128)(2,1)S(1)}, bf16[512,512]{1,0:T(8,128)(2,1)S(1)}, u32[]{:S(2)}, u32[]{:S(2)}) collective-permute-start(bf16[512,512]{1,0:T(8,128)(2,1)S(1)} %constant_dynamic-update-slice_fusion.rest_0_), channel_id=1, source_target_pairs={{0,16},{16,0},{1,17},{17,1},{2,18},{18,2},{3,19},{19,3},{4,20},{20... | collective-permute-start | bytes 1572872 | tf_op jit(solution)/shard_map/ppermute | solution.py:323
  40.7 6.1 %collective-permute-start.10 = (bf16[2,144,128]{2,1,0:T(8,128)(2,1)S(1)}, bf16[2,144,128]{2,1,0:T(8,128)(2,1)S(1)}, u32[]{:S(2)}, u32[]{:S(2)}) collective-permute-start(bf16[2,144,128]{2,1,0:T(8,128)(2,1)S(1)} %get-tuple-element.66), channel_id=1, source_target_pairs={{0,12},{4,8},{8,4},{12,0},{1,13},{5,9},{9,5},{13,1},{2,14},{6,10},... | collective-permute-start | bytes 221192 | tf_op jit(solution)/shard_map/ppermute | solution.py:323
  40.8 6.0 %collective-permute-start.8 = (bf16[2,144,128]{2,1,0:T(8,128)(2,1)S(1)}, bf16[2,144,128]{2,1,0:T(8,128)(2,1)S(1)}, u32[]{:S(2)}, u32[]{:S(2)}) collective-permute-start(bf16[2,144,128]{2,1,0:T(8,128)(2,1)S(1)} %get-tuple-element.66), channel_id=1, source_target_pairs={{0,4},{4,0},{8,12},{12,8},{1,5},{5,1},{9,13},{13,9},{2,6},{6,2},{1... | collective-permute-start | bytes 221192 | tf_op jit(solution)/shard_map/ppermute | solution.py:323
  41.4 5.4 %collective-permute-start.9 = (bf16[2,144,128]{2,1,0:T(8,128)(2,1)S(1)}, bf16[2,144,128]{2,1,0:T(8,128)(2,1)S(1)}, u32[]{:S(2)}, u32[]{:S(2)}) collective-permute-start(bf16[2,144,128]{2,1,0:T(8,128)(2,1)S(1)} %get-tuple-element.66), channel_id=1, source_target_pairs={{0,8},{4,12},{8,0},{12,4},{1,9},{5,13},{9,1},{13,5},{2,10},{6,14},... | collective-permute-start | bytes 221192 | tf_op jit(solution)/shard_map/ppermute | solution.py:323
  43.0 19.5 %collective-permute-start.15 = (bf16[512,512]{1,0:T(8,128)(2,1)S(1)}, bf16[512,512]{1,0:T(8,128)(2,1)}, u32[]{:S(2)}, u32[]{:S(2)}) collective-permute-start(bf16[512,512]{1,0:T(8,128)(2,1)S(1)} %constant_dynamic-update-slice_fusion.rest_0_), channel_id=1, source_target_pairs={{0,4},{4,0},{8,12},{12,8},{1,5},{5,1},{9,13},{13,9},{2,6},{6,2},{1... | collective-permute-start | bytes 1572872 | tf_op jit(solution)/shard_map/ppermute | solution.py:323
  46.8 13.9 %collective-permute-start.11 = (bf16[512,512]{1,0:T(8,128)(2,1)S(1)}, bf16[512,512]{1,0:T(8,128)(2,1)}, u32[]{:S(2)}, u32[]{:S(2)}) collective-permute-start(bf16[512,512]{1,0:T(8,128)(2,1)S(1)} %pad_maximum_fusion.rest_1_), channel_id=1, source_target_pairs={{0,8},{4,12},{8,0},{12,4},{1,9},{5,13},{9,1},{13,5},{2,10},{6,14},... | collective-permute-start | bytes 1572872 | tf_op jit(solution)/shard_map/ppermute | solution.py:323
  47.5 14.2 %collective-permute-start.12 = (bf16[512,512]{1,0:T(8,128)(2,1)S(1)}, bf16[512,512]{1,0:T(8,128)(2,1)}, u32[]{:S(2)}, u32[]{:S(2)}) collective-permute-start(bf16[512,512]{1,0:T(8,128)(2,1)S(1)} %pad_maximum_fusion.rest_1_), channel_id=1, source_target_pairs={{0,16},{16,0},{1,17},{17,1},{2,18},{18,2},{3,19},{19,3},{4,20},{20... | collective-permute-start | bytes 1572872 | tf_op jit(solution)/shard_map/ppermute | solution.py:323
  54.5 28.7 %all-to-all-start = ((bf16[4,512,256]{2,1,0:T(8,128)(2,1)}), bf16[4,512,256]{2,1,0:T(8,128)(2,1)S(1)}, u32[]{:S(2)}, u32[]{:S(2)}) async-start(bf16[4,512,256]{2,1,0:T(8,128)(2,1)} %attend.3), calls=%async_computation | async-start | bytes 2097152 | tf_op jit(solution)/shard_map/all_to_all | solution.py:423
  58.3 5.5 %collective-permute-start.16 = (bf16[512,512]{1,0:T(8,128)(2,1)S(1)}, bf16[512,512]{1,0:T(8,128)(2,1)S(1)}, u32[]{:S(2)}, u32[]{:S(2)}) collective-permute-start(bf16[512,512]{1,0:T(8,128)(2,1)S(1)} %pad_maximum_fusion.rest_1_), channel_id=1, source_target_pairs={{0,4},{4,0},{8,12},{12,8},{1,5},{5,1},{9,13},{13,9},{2,6},{6,2},{1... | collective-permute-start | bytes 1572872 | tf_op jit(solution)/shard_map/ppermute | solution.py:323
  58.3 5.5 %collective-permute-start.17 = (bf16[512,512]{1,0:T(8,128)(2,1)}, bf16[512,512]{1,0:T(8,128)(2,1)S(1)}, u32[]{:S(2)}, u32[]{:S(2)}) collective-permute-start(bf16[512,512]{1,0:T(8,128)(2,1)} %copy-done.6), channel_id=1, source_target_pairs={{0,4},{4,0},{8,12},{12,8},{1,5},{5,1},{9,13},{13,9},{2,6},{6,2},{1... | collective-permute-start | bytes 1572872 | tf_op jit(solution)/shard_map/ppermute | solution.py:323
  61.7 2.1 %collective-permute-start.18 = (bf16[512,512]{1,0:T(8,128)(2,1)}, bf16[512,512]{1,0:T(8,128)(2,1)S(1)}, u32[]{:S(2)}, u32[]{:S(2)}) collective-permute-start(bf16[512,512]{1,0:T(8,128)(2,1)} %collective-permute-done.11.rest_5_), channel_id=1, source_target_pairs={{0,4},{4,0},{8,12},{12,8},{1,5},{5,1},{9,13},{13,9},{2,6},{6,2},{1... | collective-permute-start | bytes 1572872 | tf_op jit(solution)/shard_map/ppermute | solution.py:323
  61.7 14.5 %collective-permute-start.13 = (bf16[512,512]{1,0:T(8,128)(2,1)}, bf16[512,512]{1,0:T(8,128)(2,1)S(1)}, u32[]{:S(2)}, u32[]{:S(2)}) collective-permute-start(bf16[512,512]{1,0:T(8,128)(2,1)} %copy-done.4), channel_id=1, source_target_pairs={{0,8},{4,12},{8,0},{12,4},{1,9},{5,13},{9,1},{13,5},{2,10},{6,14},... | collective-permute-start | bytes 1572872 | tf_op jit(solution)/shard_map/ppermute | solution.py:323
  62.5 14.3 %collective-permute-start.14 = (bf16[512,512]{1,0:T(8,128)(2,1)}, bf16[512,512]{1,0:T(8,128)(2,1)S(1)}, u32[]{:S(2)}, u32[]{:S(2)}) collective-permute-start(bf16[512,512]{1,0:T(8,128)(2,1)} %collective-permute-done.11.rest_5_), channel_id=1, source_target_pairs={{0,16},{16,0},{1,17},{17,1},{2,18},{18,2},{3,19},{19,3},{4,20},{20... | collective-permute-start | bytes 1572872 | tf_op jit(solution)/shard_map/ppermute | solution.py:323
  76.7 4.3 %collective-permute-start.20 = (bf16[512,512]{1,0:T(8,128)(2,1)}, bf16[512,512]{1,0:T(8,128)(2,1)S(1)}, u32[]{:S(2)}, u32[]{:S(2)}) collective-permute-start(bf16[512,512]{1,0:T(8,128)(2,1)} %collective-permute-done.12.rest_2_), channel_id=1, source_target_pairs={{0,4},{4,0},{8,12},{12,8},{1,5},{5,1},{9,13},{13,9},{2,6},{6,2},{1... | collective-permute-start | bytes 1572872 | tf_op jit(solution)/shard_map/ppermute | solution.py:323
  77.2 3.8 %collective-permute-start.21 = (bf16[512,512]{1,0:T(8,128)(2,1)S(1)}, bf16[512,512]{1,0:T(8,128)(2,1)S(1)}, u32[]{:S(2)}, u32[]{:S(2)}) collective-permute-start(bf16[512,512]{1,0:T(8,128)(2,1)S(1)} %collective-permute-done.13.rest_5_), channel_id=1, source_target_pairs={{0,4},{4,0},{8,12},{12,8},{1,5},{5,1},{9,13},{13,9},{2,6},{6,2},{1... | collective-permute-start | bytes 1572872 | tf_op jit(solution)/shard_map/ppermute | solution.py:323
  77.3 3.7 %collective-permute-start.22 = (bf16[512,512]{1,0:T(8,128)(2,1)S(1)}, bf16[512,512]{1,0:T(8,128)(2,1)}, u32[]{:S(2)}, u32[]{:S(2)}) collective-permute-start(bf16[512,512]{1,0:T(8,128)(2,1)S(1)} %collective-permute-done.14.rest_6_), channel_id=1, source_target_pairs={{0,4},{4,0},{8,12},{12,8},{1,5},{5,1},{9,13},{13,9},{2,6},{6,2},{1... | collective-permute-start | bytes 1572872 | tf_op jit(solution)/shard_map/ppermute | solution.py:323
  (16 other events, 78.3 us)

commit v6 on v5

--- a/solution.py
+++ b/solution.py
@@ -157,27 +157,26 @@
 
     @pl.loop(0, sources)
     def _(target):
+        chains = []
         for b in range(share // BLOCK):
             n = target * (share // BLOCK) + b
             rows = pl.ds(pl.multiple_of(n * BLOCK, BLOCK), BLOCK)
-            reached = reach[n]
-            lanes = [slice(h * DH, (h + 1) * DH) for h in range(heads)]
-            scores = [dot(q[rows, lane], kv[rows, lane], ((1,), (1,))) for lane in lanes]
-            carried = []
-            for h, lane in enumerate(lanes):
-                incoming = (before[n, h] + reached[h : h + 1] * prefix[h]).astype(BF16)
-                carried.append(dot(q[rows, lane], incoming))
-            weights = []
-            for h in range(heads):
-                cols = spread[n, h]
-                gap = jnp.concatenate([cols] * (BLOCK // DH), axis=1) - wrow[n, h : h + 1]
-                weights.append((scores[h] * jnp.exp2(jnp.minimum(gap, bound[...]))).astype(BF16))
-            for h, lane in enumerate(lanes):
-                v_b = kv[rows, columns + h * DH : columns + (h + 1) * DH]
-                attended = dot(weights[h], v_b) + jnp.exp2(spread[n, h]) * carried[h]
-                mean = jnp.mean(attended * attended, axis=1, keepdims=True)
-                normed = (attended * lax.rsqrt(mean + 1e-5)).astype(BF16)
-                held[target, b * BLOCK : (b + 1) * BLOCK, lane] = normed
+            chains += [(b, n, rows, h, slice(h * DH, (h + 1) * DH)) for h in range(heads)]
+        scores = [dot(q[rows, lane], kv[rows, lane], ((1,), (1,))) for _, _, rows, _, lane in chains]
+        carried = []
+        for _, n, rows, h, lane in chains:
+            incoming = (before[n, h] + reach[n, h : h + 1] * prefix[h]).astype(BF16)
+            carried.append(dot(q[rows, lane], incoming))
+        weights = []
+        for score, (_, n, _, h, _) in zip(scores, chains):
+            gap = jnp.concatenate([spread[n, h]] * (BLOCK // DH), axis=1) - wrow[n, h : h + 1]
+            weights.append((score * jnp.exp2(jnp.minimum(gap, bound[...]))).astype(BF16))
+        for weight, late, (b, n, rows, h, lane) in zip(weights, carried, chains):
+            v_b = kv[rows, columns + h * DH : columns + (h + 1) * DH]
+            attended = dot(weight, v_b) + jnp.exp2(spread[n, h]) * late
+            mean = jnp.mean(attended * attended, axis=1, keepdims=True)
+            normed = (attended * lax.rsqrt(mean + 1e-5)).astype(BF16)
+            held[target, b * BLOCK : (b + 1) * BLOCK, lane] = normed
         send(target).start()
 
     for target in range(sources):

time: 89.2 us -> 89 us (level)
  transfers between devices with their start and end apart: 25 -> 25, of which waited for: 11 -> 11; matrix products, arithmetic and copies ran while one was open for 0% -> 0% of each run, Pallas kernels for 38% -> 37%
where the time goes in v6:
time: 89 us; the launch traced here: 88.7 us
  Pallas kernels  38.5 us (43%)
  starting transfers between devices  27.1 us (30%)
  waiting for transfers between devices  18.8 us (21%)
  local copies, waits for them, and re-layouts  3.78 us (4%)
    ppermute x23, starting transfers between devices, swap(): return lax.ppermute(value, axis, [(i, i ^ bit) for i in range(count)])  19.6 us
    pallas_call x2, Pallas kernels, keys_values(): pl.pallas_call(functools.partial(kv_kernel, part), in_specs=[in_hbm()] *...  16.6 us
    ppermute x23, waiting for transfers between devices, swap(): return lax.ppermute(value, axis, [(i, i ^ bit) for i in range(count)])  15 us
    pallas_call x2, Pallas kernels, project_out(): pl.pallas_call(functools.partial(out_kernel, offsets, order, bool(lead)),...  10.7 us
    all_to_all x2, starting transfers between devices, on_device(): features.append(lax.all_to_all(normed, 'head', 0, 0))  7.43 us
    pallas_call x2, Pallas kernels, attend(): pl.pallas_call(functools.partial(attend_kernel, received), in_specs=[in_v...  6.63 us
    pallas_call x2, Pallas kernels, queries(): pl.pallas_call(project_kernel, in_specs=[in_vmem()] * 2, out_specs=in_vme...  4.65 us
    all_to_all x2, waiting for transfers between devices, on_device(): features.append(lax.all_to_all(normed, 'head', 0, 0))  3.81 us
  transfers between devices with their start and end apart: 25, of which 11 were waited for; matrix products, arithmetic and copies ran while one was open for 0% of the time, Pallas kernels for 37%

profile of v6, /device:TPU:0, one launch (start us, length us, event | category | flops | bytes accessed | tf_op | source)
XLA Modules:
  0.0 88.7 jit_solution(13528645037643984334)
XLA Ops:
  1.1 3.1 %collective-permute-start = (bf16[256,512]{1,0:T(8,128)(2,1)S(1)}, bf16[256,512]{1,0:T(8,128)(2,1)S(1)}, u32[]{:S(2)}, u32[]{:S(2)}) collective-permute-start(bf16[256,512]{1,0:T(8,128)(2,1)S(1)} %constant_dynamic-slice_fusion), channel_id=1, source_target_pairs={{0,1},{1,0},{2,3},{3,2},{4,5},{5,4},{6,7},{7,6},{8,9},{9,8},{10,11... | collective-permute-start | bytes 786440 | tf_op jit(solution)/shard_map/ppermute | solution.py:322
  4.2 2.6 %collective-permute-start.1 = (bf16[256,512]{1,0:T(8,128)(2,1)S(1)}, bf16[256,512]{1,0:T(8,128)(2,1)S(1)}, u32[]{:S(2)}, u32[]{:S(2)}) collective-permute-start(bf16[256,512]{1,0:T(8,128)(2,1)S(1)} %constant_dynamic-slice_fusion), channel_id=1, source_target_pairs={{0,2},{1,3},{2,0},{3,1},{4,6},{5,7},{6,4},{7,5},{8,10},{9,11},{10,... | collective-permute-start | bytes 786440 | tf_op jit(solution)/shard_map/ppermute | solution.py:322
  6.7 8.3 %keys_values.2 = (bf16[2048,2048]{1,0:T(8,128)(2,1)S(1)}, bf16[2048,256]{1,0:T(8,128)(2,1)S(1)}, bf16[2048,512]{1,0:T(8,128)(2,1)S(1)}, f32[8,2,128,128]{3,2,1,0...) custom-call(bf16[2048,2048]{1,0:T(8,128)(2,1)} %act.2, ...), custom_call_target="tpu_custom_call" | custom-call | flops 4294967296 | bytes 16777216 | tf_op jit(solution)/shard_map/keys_values/pallas_call | solution.py:268
  15.1 1.6 %collective-permute-start.3 = (bf16[2,144,128]{2,1,0:T(8,128)(2,1)S(1)}, bf16[2,144,128]{2,1,0:T(8,128)(2,1)S(1)}, u32[]{:S(2)}, u32[]{:S(2)}) collective-permute-start(bf16[2,144,128]{2,1,0:T(8,128)(2,1)S(1)} %get-tuple-element.51), channel_id=1, source_target_pairs={{0,8},{4,12},{8,0},{12,4},{1,9},{5,13},{9,1},{13,5},{2,10},{6,14},... | collective-permute-start | bytes 221192 | tf_op jit(solution)/shard_map/ppermute | solution.py:322
  17.0 1.5 %collective-permute-done.1 = bf16[256,512]{1,0:T(8,128)(2,1)S(1)} collective-permute-done((bf16[256,512]{1,0:T(8,128)(2,1)S(1)}, bf16[256,512]{1,0:T(8,128)(2,1)S(1)}, u32[]{:S(2)}, u32[]{:S(2)}) %collective-permute-start.1) | collective-permute-done | bytes 262176 | tf_op jit(solution)/shard_map/ppermute | solution.py:322
  18.9 2.3 %queries.2.q = bf16[2048,256]{1,0:T(8,128)(2,1)S(1)} custom-call(bf16[2048,2048]{1,0:T(8,128)(2,1)S(1)} %get-tuple-element.44.act, bf16[2048,256]{1,0:T(8,128)(2,1)S(1)} %get-tuple-element.45.w), custom_call_target="tpu_custom_call" | custom-call | flops 2147483648 | bytes 8388608 | tf_op jit(solution)/shard_map/queries/pallas_call | solution.py:289
  21.3 3.3 %attend.2 = bf16[4,512,256]{2,1,0:T(8,128)(2,1)} custom-call(bf16[2048,256]{1,0:T(8,128)(2,1)S(1)} %queries.2.q, bf16[2048,512]{1,0:T(8,128)(2,1)S(1)} %get-tuple-element.46.kv, f32[8,2,128,128]{3,2,1,0:T(8,128)S(1)} %get-tuple-element.47.before, f32[8,2,256,128]{3,2,1,0:T(8,128)S(1)} %get-tuple-element.48.spread, f32[8,8,256]{2,1,0:T(8,128)S(1)} %get-tuple-element.49.wrow, ...), custom_call_target="tpu_custom_call" | custom-call | flops 2684354560 | bytes 4194304 | tf_op jit(solution)/shard_map/attend/pallas_call | solution.py:304
  25.5 3.7 %all-to-all-start.1 = ((bf16[4,512,256]{2,1,0:T(8,128)(2,1)}), bf16[4,512,256]{2,1,0:T(8,128)(2,1)S(1)}, u32[]{:S(2)}, u32[]{:S(2)}) async-start(bf16[4,512,256]{2,1,0:T(8,128)(2,1)} %attend.2), calls=%async_computation.1 | async-start | bytes 2097152 | tf_op jit(solution)/shard_map/all_to_all | solution.py:422
  29.3 1.6 %collective-permute-start.6 = (bf16[512,512]{1,0:T(8,128)(2,1)S(1)}, bf16[512,512]{1,0:T(8,128)(2,1)S(1)}, u32[]{:S(2)}, u32[]{:S(2)}) collective-permute-start(bf16[512,512]{1,0:T(8,128)(2,1)S(1)} %constant_dynamic-update-slice_fusion.rest_0_), channel_id=1, source_target_pairs={{0,8},{4,12},{8,0},{12,4},{1,9},{5,13},{9,1},{13,5},{2,10},{6,14},... | collective-permute-start | bytes 1572872 | tf_op jit(solution)/shard_map/ppermute | solution.py:322
  30.9 1.5 %collective-permute-start.7 = (bf16[512,512]{1,0:T(8,128)(2,1)S(1)}, bf16[512,512]{1,0:T(8,128)(2,1)S(1)}, u32[]{:S(2)}, u32[]{:S(2)}) collective-permute-start(bf16[512,512]{1,0:T(8,128)(2,1)S(1)} %constant_dynamic-update-slice_fusion.rest_0_), channel_id=1, source_target_pairs={{0,16},{16,0},{1,17},{17,1},{2,18},{18,2},{3,19},{19,3},{4,20},{20... | collective-permute-start | bytes 1572872 | tf_op jit(solution)/shard_map/ppermute | solution.py:322
  32.4 8.3 %keys_values.3 = (bf16[2048,2048]{1,0:T(8,128)(2,1)S(1)}, bf16[2048,256]{1,0:T(8,128)(2,1)S(1)}, bf16[2048,512]{1,0:T(8,128)(2,1)S(1)}, f32[8,2,128,128]{3,2,1,0...) custom-call(bf16[2048,2048]{1,0:T(8,128)(2,1)} %act.2, ...), custom_call_target="tpu_custom_call" | custom-call | flops 4294967296 | bytes 16777216 | tf_op jit(solution)/shard_map/keys_values/pallas_call | solution.py:268
  41.4 1.5 %collective-permute-start.9 = (bf16[2,144,128]{2,1,0:T(8,128)(2,1)S(1)}, bf16[2,144,128]{2,1,0:T(8,128)(2,1)S(1)}, u32[]{:S(2)}, u32[]{:S(2)}) collective-permute-start(bf16[2,144,128]{2,1,0:T(8,128)(2,1)S(1)} %get-tuple-element.66), channel_id=1, source_target_pairs={{0,8},{4,12},{8,0},{12,4},{1,9},{5,13},{9,1},{13,5},{2,10},{6,14},... | collective-permute-start | bytes 221192 | tf_op jit(solution)/shard_map/ppermute | solution.py:322
  44.2 2.3 %queries.3.q = bf16[2048,256]{1,0:T(8,128)(2,1)S(1)} custom-call(bf16[2048,2048]{1,0:T(8,128)(2,1)S(1)} %get-tuple-element.59.act, bf16[2048,256]{1,0:T(8,128)(2,1)S(1)} %get-tuple-element.60.w), custom_call_target="tpu_custom_call" | custom-call | flops 2147483648 | bytes 8388608 | tf_op jit(solution)/shard_map/queries/pallas_call | solution.py:289
  47.4 1.7 %collective-permute-start.12 = (bf16[512,512]{1,0:T(8,128)(2,1)S(1)}, bf16[512,512]{1,0:T(8,128)(2,1)}, u32[]{:S(2)}, u32[]{:S(2)}) collective-permute-start(bf16[512,512]{1,0:T(8,128)(2,1)S(1)} %pad_maximum_fusion.rest_1_), channel_id=1, source_target_pairs={{0,16},{16,0},{1,17},{17,1},{2,18},{18,2},{3,19},{19,3},{4,20},{20... | collective-permute-start | bytes 1572872 | tf_op jit(solution)/shard_map/ppermute | solution.py:322
  49.1 3.3 %attend.3 = bf16[4,512,256]{2,1,0:T(8,128)(2,1)} custom-call(bf16[2048,256]{1,0:T(8,128)(2,1)S(1)} %queries.3.q, bf16[2048,512]{1,0:T(8,128)(2,1)S(1)} %get-tuple-element.61.kv, f32[8,2,128,128]{3,2,1,0:T(8,128)S(1)} %get-tuple-element.62.before, f32[8,2,256,128]{3,2,1,0:T(8,128)S(1)} %get-tuple-element.63.spread, f32[8,8,256]{2,1,0:T(8,128)S(1)} %get-tuple-element.64.wrow, ...), custom_call_target="tpu_custom_call" | custom-call | flops 2684354560 | bytes 4194304 | tf_op jit(solution)/shard_map/attend/pallas_call | solution.py:304
  52.4 1.9 %all-to-all-done.1.features = bf16[4,512,256]{2,1,0:T(8,128)(2,1)S(1)} async-done(((bf16[4,512,256]{2,1,0:T(8,128)(2,1)}), bf16[4,512,256]{2,1,0:T(8,128)(2,1)S(1)}, u32[]{:S(2)}, u32[]{:S(2)}) %all-to-all-start.1) | async-done | bytes 1048608 | tf_op jit(solution)/shard_map/all_to_all | solution.py:422
  54.3 3.7 %all-to-all-start = ((bf16[4,512,256]{2,1,0:T(8,128)(2,1)}), bf16[4,512,256]{2,1,0:T(8,128)(2,1)S(1)}, u32[]{:S(2)}, u32[]{:S(2)}) async-start(bf16[4,512,256]{2,1,0:T(8,128)(2,1)} %attend.3), calls=%async_computation | async-start | bytes 2097152 | tf_op jit(solution)/shard_map/all_to_all | solution.py:422
  58.6 2.1 %collective-permute-done.11.rest_5_ = bf16[512,512]{1,0:T(8,128)(2,1)} collective-permute-done((bf16[512,512]{1,0:T(8,128)(2,1)S(1)}, bf16[512,512]{1,0:T(8,128)(2,1)}, u32[]{:S(2)}, u32[]{:S(2)}) %collective-permute-start.11) | collective-permute-done | bytes 524320 | tf_op jit(solution)/shard_map/ppermute | solution.py:322
  61.3 1.2 %collective-permute-start.13 = (bf16[512,512]{1,0:T(8,128)(2,1)}, bf16[512,512]{1,0:T(8,128)(2,1)S(1)}, u32[]{:S(2)}, u32[]{:S(2)}) collective-permute-start(bf16[512,512]{1,0:T(8,128)(2,1)} %copy-done.4), channel_id=1, source_target_pairs={{0,8},{4,12},{8,0},{12,4},{1,9},{5,13},{9,1},{13,5},{2,10},{6,14},... | collective-permute-start | bytes 1572872 | tf_op jit(solution)/shard_map/ppermute | solution.py:322
  65.3 5.2 %project_out.2.rest_0_ = f32[4,512,512]{2,1,0:T(8,128)} custom-call(bf16[4,512,256]{2,1,0:T(8,128)(2,1)S(1)} %all-to-all-done.1.features, bf16[512,512]{1,0:T(8,128)(2,1)} %copy-done.3, bf16[512,512]{1,0:T(8,128)(2,1)} %copy-done.2, bf16[512,512]{1,0:T(8,128)(2,1)} %collective-permute-done.15.rest_2_, bf16[512,512]{1,0:T(8,128)(2,1)} %copy-done.9, ...), custom_call_target="tpu_custom_call" | custom-call | flops 2147483648 | bytes 8388608 | tf_op jit(solution)/shard_map/project_out/pallas_call | solution.py:375
  70.5 5.3 %collective-permute-done.13.rest_5_ = bf16[512,512]{1,0:T(8,128)(2,1)S(1)} collective-permute-done((bf16[512,512]{1,0:T(8,128)(2,1)}, bf16[512,512]{1,0:T(8,128)(2,1)S(1)}, u32[]{:S(2)}, u32[]{:S(2)}) %collective-permute-start.13) | collective-permute-done | bytes 524320 | tf_op jit(solution)/shard_map/ppermute | solution.py:322
  78.7 2.3 %collective-permute-done.20.rest_4_ = bf16[512,512]{1,0:T(8,128)(2,1)S(1)} collective-permute-done((bf16[512,512]{1,0:T(8,128)(2,1)}, bf16[512,512]{1,0:T(8,128)(2,1)S(1)}, u32[]{:S(2)}, u32[]{:S(2)}) %collective-permute-start.20) | collective-permute-done | bytes 524320 | tf_op jit(solution)/shard_map/ppermute | solution.py:322
  81.0 2.0 %all-to-all-done.features = bf16[4,512,256]{2,1,0:T(8,128)(2,1)S(1)} async-done(((bf16[4,512,256]{2,1,0:T(8,128)(2,1)}), bf16[4,512,256]{2,1,0:T(8,128)(2,1)S(1)}, u32[]{:S(2)}, u32[]{:S(2)}) %all-to-all-start) | async-done | bytes 1048608 | tf_op jit(solution)/shard_map/all_to_all | solution.py:422
  83.0 5.5 %project_out.3 = bf16[512,2048]{1,0:T(8,128)(2,1)} custom-call(bf16[4,512,256]{2,1,0:T(8,128)(2,1)S(1)} %all-to-all-done.features, f32[4,512,512]{2,1,0:T(8,128)} %project_out.2.rest_0_, bf16[512,512]{1,0:T(8,128)(2,1)} %copy-done.4, bf16[512,512]{1,0:T(8,128)(2,1)} %collective-permute-done.12.rest_2_, bf16[512,512]{1,0:T(8,128)(2,1)} %copy-done.11, ...), custom_call_target="tpu_custom_call" | custom-call | flops 2147483648 | bytes 8388608 | tf_op jit(solution)/shard_map/project_out/pallas_call | solution.py:375
  (68 shorter events, 12.5 us)
Async XLA Ops:
  1.1 15.9 %collective-permute-start = (bf16[256,512]{1,0:T(8,128)(2,1)S(1)}, bf16[256,512]{1,0:T(8,128)(2,1)S(1)}, u32[]{:S(2)}, u32[]{:S(2)}) collective-permute-start(bf16[256,512]{1,0:T(8,128)(2,1)S(1)} %constant_dynamic-slice_fusion), channel_id=1, source_target_pairs={{0,1},{1,0},{2,3},{3,2},{4,5},{5,4},{6,7},{7,6},{8,9},{9,8},{10,11... | collective-permute-start | bytes 786440 | tf_op jit(solution)/shard_map/ppermute | solution.py:322
  4.2 14.3 %collective-permute-start.1 = (bf16[256,512]{1,0:T(8,128)(2,1)S(1)}, bf16[256,512]{1,0:T(8,128)(2,1)S(1)}, u32[]{:S(2)}, u32[]{:S(2)}) collective-permute-start(bf16[256,512]{1,0:T(8,128)(2,1)S(1)} %constant_dynamic-slice_fusion), channel_id=1, source_target_pairs={{0,2},{1,3},{2,0},{3,1},{4,6},{5,7},{6,4},{7,5},{8,10},{9,11},{10,... | collective-permute-start | bytes 786440 | tf_op jit(solution)/shard_map/ppermute | solution.py:322
  15.0 6.2 %collective-permute-start.2 = (bf16[2,144,128]{2,1,0:T(8,128)(2,1)S(1)}, bf16[2,144,128]{2,1,0:T(8,128)(2,1)S(1)}, u32[]{:S(2)}, u32[]{:S(2)}) collective-permute-start(bf16[2,144,128]{2,1,0:T(8,128)(2,1)S(1)} %get-tuple-element.51), channel_id=1, source_target_pairs={{0,4},{4,0},{8,12},{12,8},{1,5},{5,1},{9,13},{13,9},{2,6},{6,2},{1... | collective-permute-start | bytes 221192 | tf_op jit(solution)/shard_map/ppermute | solution.py:322
  15.1 6.2 %collective-permute-start.3 = (bf16[2,144,128]{2,1,0:T(8,128)(2,1)S(1)}, bf16[2,144,128]{2,1,0:T(8,128)(2,1)S(1)}, u32[]{:S(2)}, u32[]{:S(2)}) collective-permute-start(bf16[2,144,128]{2,1,0:T(8,128)(2,1)S(1)} %get-tuple-element.51), channel_id=1, source_target_pairs={{0,8},{4,12},{8,0},{12,4},{1,9},{5,13},{9,1},{13,5},{2,10},{6,14},... | collective-permute-start | bytes 221192 | tf_op jit(solution)/shard_map/ppermute | solution.py:322
  16.7 4.6 %collective-permute-start.4 = (bf16[2,144,128]{2,1,0:T(8,128)(2,1)S(1)}, bf16[2,144,128]{2,1,0:T(8,128)(2,1)S(1)}, u32[]{:S(2)}, u32[]{:S(2)}) collective-permute-start(bf16[2,144,128]{2,1,0:T(8,128)(2,1)S(1)} %get-tuple-element.51), channel_id=1, source_target_pairs={{0,12},{4,8},{8,4},{12,0},{1,13},{5,9},{9,5},{13,1},{2,14},{6,10},... | collective-permute-start | bytes 221192 | tf_op jit(solution)/shard_map/ppermute | solution.py:322
  18.5 7.1 %collective-permute-start.5 = (bf16[256,512]{1,0:T(8,128)(2,1)S(1)}, bf16[256,512]{1,0:T(8,128)(2,1)S(1)}, u32[]{:S(2)}, u32[]{:S(2)}) collective-permute-start(bf16[256,512]{1,0:T(8,128)(2,1)S(1)} %collective-permute-done.1), channel_id=1, source_target_pairs={{0,1},{1,0},{2,3},{3,2},{4,5},{5,4},{6,7},{7,6},{8,9},{9,8},{10,11... | collective-permute-start | bytes 786440 | tf_op jit(solution)/shard_map/ppermute | solution.py:322
  25.5 28.8 %all-to-all-start.1 = ((bf16[4,512,256]{2,1,0:T(8,128)(2,1)}), bf16[4,512,256]{2,1,0:T(8,128)(2,1)S(1)}, u32[]{:S(2)}, u32[]{:S(2)}) async-start(bf16[4,512,256]{2,1,0:T(8,128)(2,1)} %attend.2), calls=%async_computation.1 | async-start | bytes 2097152 | tf_op jit(solution)/shard_map/all_to_all | solution.py:422
  29.3 13.6 %collective-permute-start.6 = (bf16[512,512]{1,0:T(8,128)(2,1)S(1)}, bf16[512,512]{1,0:T(8,128)(2,1)S(1)}, u32[]{:S(2)}, u32[]{:S(2)}) collective-permute-start(bf16[512,512]{1,0:T(8,128)(2,1)S(1)} %constant_dynamic-update-slice_fusion.rest_0_), channel_id=1, source_target_pairs={{0,8},{4,12},{8,0},{12,4},{1,9},{5,13},{9,1},{13,5},{2,10},{6,14},... | collective-permute-start | bytes 1572872 | tf_op jit(solution)/shard_map/ppermute | solution.py:322
  30.9 12.6 %collective-permute-start.7 = (bf16[512,512]{1,0:T(8,128)(2,1)S(1)}, bf16[512,512]{1,0:T(8,128)(2,1)S(1)}, u32[]{:S(2)}, u32[]{:S(2)}) collective-permute-start(bf16[512,512]{1,0:T(8,128)(2,1)S(1)} %constant_dynamic-update-slice_fusion.rest_0_), channel_id=1, source_target_pairs={{0,16},{16,0},{1,17},{17,1},{2,18},{18,2},{3,19},{19,3},{4,20},{20... | collective-permute-start | bytes 1572872 | tf_op jit(solution)/shard_map/ppermute | solution.py:322
  40.7 5.9 %collective-permute-start.10 = (bf16[2,144,128]{2,1,0:T(8,128)(2,1)S(1)}, bf16[2,144,128]{2,1,0:T(8,128)(2,1)S(1)}, u32[]{:S(2)}, u32[]{:S(2)}) collective-permute-start(bf16[2,144,128]{2,1,0:T(8,128)(2,1)S(1)} %get-tuple-element.66), channel_id=1, source_target_pairs={{0,12},{4,8},{8,4},{12,0},{1,13},{5,9},{9,5},{13,1},{2,14},{6,10},... | collective-permute-start | bytes 221192 | tf_op jit(solution)/shard_map/ppermute | solution.py:322
  40.8 5.8 %collective-permute-start.8 = (bf16[2,144,128]{2,1,0:T(8,128)(2,1)S(1)}, bf16[2,144,128]{2,1,0:T(8,128)(2,1)S(1)}, u32[]{:S(2)}, u32[]{:S(2)}) collective-permute-start(bf16[2,144,128]{2,1,0:T(8,128)(2,1)S(1)} %get-tuple-element.66), channel_id=1, source_target_pairs={{0,4},{4,0},{8,12},{12,8},{1,5},{5,1},{9,13},{13,9},{2,6},{6,2},{1... | collective-permute-start | bytes 221192 | tf_op jit(solution)/shard_map/ppermute | solution.py:322
  41.4 5.2 %collective-permute-start.9 = (bf16[2,144,128]{2,1,0:T(8,128)(2,1)S(1)}, bf16[2,144,128]{2,1,0:T(8,128)(2,1)S(1)}, u32[]{:S(2)}, u32[]{:S(2)}) collective-permute-start(bf16[2,144,128]{2,1,0:T(8,128)(2,1)S(1)} %get-tuple-element.66), channel_id=1, source_target_pairs={{0,8},{4,12},{8,0},{12,4},{1,9},{5,13},{9,1},{13,5},{2,10},{6,14},... | collective-permute-start | bytes 221192 | tf_op jit(solution)/shard_map/ppermute | solution.py:322
  43.0 19.5 %collective-permute-start.15 = (bf16[512,512]{1,0:T(8,128)(2,1)S(1)}, bf16[512,512]{1,0:T(8,128)(2,1)}, u32[]{:S(2)}, u32[]{:S(2)}) collective-permute-start(bf16[512,512]{1,0:T(8,128)(2,1)S(1)} %constant_dynamic-update-slice_fusion.rest_0_), channel_id=1, source_target_pairs={{0,4},{4,0},{8,12},{12,8},{1,5},{5,1},{9,13},{13,9},{2,6},{6,2},{1... | collective-permute-start | bytes 1572872 | tf_op jit(solution)/shard_map/ppermute | solution.py:322
  46.6 14.1 %collective-permute-start.11 = (bf16[512,512]{1,0:T(8,128)(2,1)S(1)}, bf16[512,512]{1,0:T(8,128)(2,1)}, u32[]{:S(2)}, u32[]{:S(2)}) collective-permute-start(bf16[512,512]{1,0:T(8,128)(2,1)S(1)} %pad_maximum_fusion.rest_1_), channel_id=1, source_target_pairs={{0,8},{4,12},{8,0},{12,4},{1,9},{5,13},{9,1},{13,5},{2,10},{6,14},... | collective-permute-start | bytes 1572872 | tf_op jit(solution)/shard_map/ppermute | solution.py:322
  47.4 13.9 %collective-permute-start.12 = (bf16[512,512]{1,0:T(8,128)(2,1)S(1)}, bf16[512,512]{1,0:T(8,128)(2,1)}, u32[]{:S(2)}, u32[]{:S(2)}) collective-permute-start(bf16[512,512]{1,0:T(8,128)(2,1)S(1)} %pad_maximum_fusion.rest_1_), channel_id=1, source_target_pairs={{0,16},{16,0},{1,17},{17,1},{2,18},{18,2},{3,19},{19,3},{4,20},{20... | collective-permute-start | bytes 1572872 | tf_op jit(solution)/shard_map/ppermute | solution.py:322
  54.3 28.7 %all-to-all-start = ((bf16[4,512,256]{2,1,0:T(8,128)(2,1)}), bf16[4,512,256]{2,1,0:T(8,128)(2,1)S(1)}, u32[]{:S(2)}, u32[]{:S(2)}) async-start(bf16[4,512,256]{2,1,0:T(8,128)(2,1)} %attend.3), calls=%async_computation | async-start | bytes 2097152 | tf_op jit(solution)/shard_map/all_to_all | solution.py:422
  58.1 5.3 %collective-permute-start.16 = (bf16[512,512]{1,0:T(8,128)(2,1)S(1)}, bf16[512,512]{1,0:T(8,128)(2,1)S(1)}, u32[]{:S(2)}, u32[]{:S(2)}) collective-permute-start(bf16[512,512]{1,0:T(8,128)(2,1)S(1)} %pad_maximum_fusion.rest_1_), channel_id=1, source_target_pairs={{0,4},{4,0},{8,12},{12,8},{1,5},{5,1},{9,13},{13,9},{2,6},{6,2},{1... | collective-permute-start | bytes 1572872 | tf_op jit(solution)/shard_map/ppermute | solution.py:322
  58.1 5.2 %collective-permute-start.17 = (bf16[512,512]{1,0:T(8,128)(2,1)}, bf16[512,512]{1,0:T(8,128)(2,1)S(1)}, u32[]{:S(2)}, u32[]{:S(2)}) collective-permute-start(bf16[512,512]{1,0:T(8,128)(2,1)} %copy-done.6), channel_id=1, source_target_pairs={{0,4},{4,0},{8,12},{12,8},{1,5},{5,1},{9,13},{13,9},{2,6},{6,2},{1... | collective-permute-start | bytes 1572872 | tf_op jit(solution)/shard_map/ppermute | solution.py:322
  61.3 2.1 %collective-permute-start.18 = (bf16[512,512]{1,0:T(8,128)(2,1)}, bf16[512,512]{1,0:T(8,128)(2,1)S(1)}, u32[]{:S(2)}, u32[]{:S(2)}) collective-permute-start(bf16[512,512]{1,0:T(8,128)(2,1)} %collective-permute-done.11.rest_5_), channel_id=1, source_target_pairs={{0,4},{4,0},{8,12},{12,8},{1,5},{5,1},{9,13},{13,9},{2,6},{6,2},{1... | collective-permute-start | bytes 1572872 | tf_op jit(solution)/shard_map/ppermute | solution.py:322
  61.3 14.5 %collective-permute-start.13 = (bf16[512,512]{1,0:T(8,128)(2,1)}, bf16[512,512]{1,0:T(8,128)(2,1)S(1)}, u32[]{:S(2)}, u32[]{:S(2)}) collective-permute-start(bf16[512,512]{1,0:T(8,128)(2,1)} %copy-done.4), channel_id=1, source_target_pairs={{0,8},{4,12},{8,0},{12,4},{1,9},{5,13},{9,1},{13,5},{2,10},{6,14},... | collective-permute-start | bytes 1572872 | tf_op jit(solution)/shard_map/ppermute | solution.py:322
  62.5 14.3 %collective-permute-start.14 = (bf16[512,512]{1,0:T(8,128)(2,1)}, bf16[512,512]{1,0:T(8,128)(2,1)S(1)}, u32[]{:S(2)}, u32[]{:S(2)}) collective-permute-start(bf16[512,512]{1,0:T(8,128)(2,1)} %collective-permute-done.11.rest_5_), channel_id=1, source_target_pairs={{0,16},{16,0},{1,17},{17,1},{2,18},{18,2},{3,19},{19,3},{4,20},{20... | collective-permute-start | bytes 1572872 | tf_op jit(solution)/shard_map/ppermute | solution.py:322
  76.7 4.3 %collective-permute-start.20 = (bf16[512,512]{1,0:T(8,128)(2,1)}, bf16[512,512]{1,0:T(8,128)(2,1)S(1)}, u32[]{:S(2)}, u32[]{:S(2)}) collective-permute-start(bf16[512,512]{1,0:T(8,128)(2,1)} %collective-permute-done.12.rest_2_), channel_id=1, source_target_pairs={{0,4},{4,0},{8,12},{12,8},{1,5},{5,1},{9,13},{13,9},{2,6},{6,2},{1... | collective-permute-start | bytes 1572872 | tf_op jit(solution)/shard_map/ppermute | solution.py:322
  77.2 3.8 %collective-permute-start.21 = (bf16[512,512]{1,0:T(8,128)(2,1)S(1)}, bf16[512,512]{1,0:T(8,128)(2,1)S(1)}, u32[]{:S(2)}, u32[]{:S(2)}) collective-permute-start(bf16[512,512]{1,0:T(8,128)(2,1)S(1)} %collective-permute-done.13.rest_5_), channel_id=1, source_target_pairs={{0,4},{4,0},{8,12},{12,8},{1,5},{5,1},{9,13},{13,9},{2,6},{6,2},{1... | collective-permute-start | bytes 1572872 | tf_op jit(solution)/shard_map/ppermute | solution.py:322
  77.3 3.7 %collective-permute-start.22 = (bf16[512,512]{1,0:T(8,128)(2,1)S(1)}, bf16[512,512]{1,0:T(8,128)(2,1)}, u32[]{:S(2)}, u32[]{:S(2)}) collective-permute-start(bf16[512,512]{1,0:T(8,128)(2,1)S(1)} %collective-permute-done.14.rest_6_), channel_id=1, source_target_pairs={{0,4},{4,0},{8,12},{12,8},{1,5},{5,1},{9,13},{13,9},{2,6},{6,2},{1... | collective-permute-start | bytes 1572872 | tf_op jit(solution)/shard_map/ppermute | solution.py:322
  (16 other events, 78.1 us)
